TPU v7x, 32 devices: a whole 2x2x4 slice. The times are simulated.
32 devices in a mesh: groups: 2 (over y), seq: 4 (over z), batch: 2 (over x), head: 2 (over core).
Axes of the slice: x: 2, y: 2, z: 4, core: 2. Of those that a mesh axis runs over, the one named last changes fastest.
Arguments:
- x_inner: bfloat16 [4, 2048, 3072], P(('groups', 'batch'), 'seq', 'head'), parts along dimension 0, may hold values from -6 to 6
- gating_branch_values: bfloat16 [4, 2048, 3072], P(('groups', 'batch'), 'seq', 'head'), parts along dimension 0, may hold values from -6 to 6
- b_proj: bfloat16 [4, 2048, 128], P(('groups', 'batch'), 'seq'), parts along dimension 0, may hold values from -2 to 2
- c_proj: bfloat16 [4, 2048, 128], P(('groups', 'batch'), 'seq'), parts along dimension 0, may hold values from -2 to 2
- unbiased_step_size: float32 [4, 2048, 48], P(('groups', 'batch'), 'seq', 'head'), parts along dimension 0, may hold values from -3 to 10
- record_lengths: int32 [4, 2], P(('groups', 'batch')), parts along dimension 0, may hold values from 1 to 1536, 2048 in all within a row
- dt_bias: float32 [48], P('head'), may hold values from -9 to -3
- a_log: float32 [48], P('head'), may hold values from -0.5 to 0.5
- d_skip: float32 [48], P('head'), may hold values from 0.5 to 1.5
- norm_gain: float32 [3072], P('head'), may hold values from 0.5 to 1.5
- out_grad: bfloat16 [4, 2048, 3072], P(('groups', 'batch'), 'seq', 'head'), parts along dimension 0, may hold values from -6 to 6
Outputs:
- normed: bfloat16 [4, 2048, 3072], P(('groups', 'batch'), 'seq', 'head'), parts along dimension 0
- x_grad: bfloat16 [4, 2048, 3072], P(('groups', 'batch'), 'seq', 'head'), parts along dimension 0
- z_grad: bfloat16 [4, 2048, 3072], P(('groups', 'batch'), 'seq', 'head'), parts along dimension 0
- input_matrix_gradient: float32 [4, 2048, 128], P(('groups', 'batch'), 'seq'), parts along dimension 0
- c_grad: float32 [4, 2048, 128], P(('groups', 'batch'), 'seq'), parts along dimension 0
- dt_grad: float32 [4, 2048, 48], P(('groups', 'batch'), 'seq', 'head'), parts along dimension 0
- bias_grad: float32 [96], P(('groups', 'head')), parts along dimension 0
- alog_grad: float32 [96], P(('groups', 'head')), parts along dimension 0
- residual_factor_cotangent: float32 [96], P(('groups', 'head')), parts along dimension 0
- gain_grad: float32 [6144], P(('groups', 'head')), parts along dimension 0
There are 2 independent parts, one for each index of `groups`. A program takes and returns all parts, laid end to end along the dimension named above; an argument that names none is the same for every part. Nothing has to cross between parts.
Inputs may be any that keep to these rules, and one draw needn't show every extreme that they name: `record_lengths`: each row's lengths sum to 2048; no record of a row has more than 1536 positions.
All inputs are finite; a program needn't handle non-finite values.
Results may differ from a plain program's by a relative error of at most 0.001.
Values sent between devices are 32-bit elements; how exact they have to be, the bound alone decides.
No kernel may reach another device: no remote copies, remote signals or barrier semaphores. Data moves between devices by JAX's collectives and lax.ppermute only.
A program may use at most 192 MiB of HBM per device.

v0:
```python
from functools import partial

import jax
import jax.numpy as jnp
from jax import lax
from jax.sharding import PartitionSpec as P

STATE = 128
HEADDIM = 64
SPAN = 256


highest = lax.Precision.HIGHEST
epsilon = 1e-05


def shifted(value, axis, steps):
    count = lax.axis_size(axis)
    leading, last = (max(0, -steps), min(count, count - steps))
    return lax.ppermute(value, axis, [(source, source + steps) for source in range(leading, last)])


def record_ids(record_lengths, element_places):
    starts = jnp.cumsum(record_lengths, axis=1) - record_lengths
    return jnp.sum((starts[:, None, :] <= element_places[None, :, None]).astype(jnp.int32), axis=2)


def decay_terms(raw_step, segment, prior_value, dt_bias, a_log):
    step_size = jax.nn.softplus(raw_step + dt_bias)
    cumul = jnp.cumsum(step_size * -jnp.exp(a_log), axis=0).T
    closing = segment[-1]
    inflow = jnp.exp(cumul) * (segment == prior_value).astype(jnp.float32)
    decay = jnp.exp(cumul[:, -1]) * (closing == prior_value).astype(jnp.float32)
    tail_weight = jnp.exp(cumul[:, -1:] - cumul) * (segment == closing).astype(jnp.float32)
    return (step_size, cumul, inflow, decay, tail_weight)


def block_step(state, block, dt_bias, a_log, d_skip):
    x_block, raw_step, b_block, c_block, segment, prior_value = block
    x_float = x_block.astype(jnp.float32)
    step_size, cumul, inflow, decay, tail_weight = decay_terms(
        raw_step, segment, prior_value, dt_bias, a_log
    )
    position = jnp.arange(segment.shape[0])
    same_rec = (segment[:, None] == segment[None, :]) & (position[:, None] >= position[None, :])
    log_gap = jnp.where(same_rec[None], cumul[:, :, None] - cumul[:, None, :], 0.0)
    scores = jnp.dot(c_block, b_block.T, precision=highest)
    mixing = jnp.where(same_rec[None], jnp.exp(log_gap), 0.0) * scores[None]
    rescaled_quantity = x_float * step_size[:, :, None]
    result = jnp.einsum("hij,jhp->ihp", mixing, rescaled_quantity, precision=highest)
    result = (
        result + jnp.einsum("in,hpn->ihp", c_block, state, precision=highest) * inflow.T[:, :, None]
    )
    result = result + d_skip[None, :, None] * x_float
    fresh = jnp.einsum(
        "jhp,jn->hpn", rescaled_quantity * tail_weight.T[:, :, None], b_block, precision=highest
    )
    return (decay[:, None, None] * state + fresh, result)


def inter_step(state, block, dt_bias, a_log):
    raw_step, c_block, segment, prior_value = block
    step_size, cumul, inflow, decay, tail_weight = decay_terms(
        raw_step, segment, prior_value, dt_bias, a_log
    )
    result = jnp.einsum("in,hpn->ihp", c_block, state, precision=highest) * inflow.T[:, :, None]
    return (decay[:, None, None] * state, result)


def block_decay(raw_step, segment, prior_value, dt_bias, a_log):
    return decay_terms(raw_step, segment, prior_value, dt_bias, a_log)[3]


def shards(
    x_inner,
    gating_branch_values,
    b_proj,
    c_proj,
    unbiased_step_size,
    record_lengths,
    dt_bias,
    a_log,
    d_skip,
    norm_gain,
    out_grad,
):
    rows, tokens, width = x_inner.shape
    heads = width // HEADDIM
    count = tokens // SPAN
    offset = lax.axis_index("seq") * tokens
    element_places = offset + jnp.arange(tokens, dtype=jnp.int32)
    segments = record_ids(record_lengths, element_places).reshape(rows, count, SPAN)
    prior_value = record_ids(record_lengths, offset + jnp.arange(count, dtype=jnp.int32) * SPAN - 1)
    x_blocks = x_inner.reshape(rows, count, SPAN, heads, HEADDIM)
    raw_blocks = unbiased_step_size.reshape(rows, count, SPAN, heads)
    b_blocks = b_proj.astype(jnp.float32).reshape(rows, count, SPAN, STATE)
    c_blocks = c_proj.astype(jnp.float32).reshape(rows, count, SPAN, STATE)
    empty = jnp.zeros((rows, heads, HEADDIM, STATE), jnp.float32)

    def forward(x_value, raw_value, b_value, c_value, step_bias_entry, alog_value, skip_value):

        def forward_one_row(x_rows, raw_rows, b_rows, c_rows, segment_rows, previous_rows):
            stepper = partial(
                block_step, dt_bias=step_bias_entry, a_log=alog_value, d_skip=skip_value
            )
            start = jnp.zeros((heads, HEADDIM, STATE), jnp.float32)
            final, result = lax.scan(
                stepper, start, (x_rows, raw_rows, b_rows, c_rows, segment_rows, previous_rows)
            )
            return (result, final)

        return jax.vmap(forward_one_row)(
            x_value, raw_value, b_value, c_value, segments, prior_value
        )

    (local_result, endings), backward = jax.vjp(
        forward, x_blocks, raw_blocks, b_blocks, c_blocks, dt_bias, a_log, d_skip
    )
    decays = jax.vmap(jax.vmap(partial(block_decay, dt_bias=dt_bias, a_log=a_log)))(
        raw_blocks, segments, prior_value
    )
    totals = jnp.prod(decays, axis=1)

    def relay(turn, arriving):
        return shifted(totals[:, :, None, None] * arriving + endings, "seq", 1)

    incoming = lax.fori_loop(0, lax.axis_size("seq") - 1, relay, empty)

    def inter_only(raw_value, c_value, step_bias_entry, alog_value, state_value):

        def inter_one_row(raw_rows, c_rows, state, segment_rows, previous_rows):
            stepper = partial(inter_step, dt_bias=step_bias_entry, a_log=alog_value)
            final, partial_out = lax.scan(
                stepper, state, (raw_rows, c_rows, segment_rows, previous_rows)
            )
            return (partial_out, final)

        return jax.vmap(inter_one_row)(raw_value, c_value, state_value, segments, prior_value)

    (carried_result, carried_final), inter_back = jax.vjp(
        inter_only, raw_blocks, c_blocks, dt_bias, a_log, incoming
    )
    result = local_result + carried_result
    flat = result.reshape(rows, tokens, width)
    z_float = gating_branch_values.astype(jnp.float32)
    sigma = jax.nn.sigmoid(z_float)
    gate = z_float * sigma
    gated = flat * gate
    grad_float = out_grad.astype(jnp.float32)
    weighted = grad_float * norm_gain
    square_sum, cross_sum = lax.psum(
        (jnp.sum(gated * gated, axis=-1), jnp.sum(weighted * gated, axis=-1)), "head"
    )
    total_width = width * lax.axis_size("head")
    scale = lax.rsqrt(square_sum / total_width + epsilon)[:, :, None]
    normed = (gated * scale * norm_gain).astype(jnp.bfloat16)
    gated_grad = weighted * scale - gated * (scale * scale * scale) * (
        cross_sum[:, :, None] / total_width
    )
    gain_part = jnp.sum(grad_float * gated * scale, axis=(0, 1))
    mixed_grad = gated_grad * gate
    z_grad = (gated_grad * flat * (sigma + z_float * sigma * (1.0 - sigma))).astype(jnp.bfloat16)
    mixed_blocks = mixed_grad.reshape(rows, count, SPAN, heads, HEADDIM)
    first = inter_back((mixed_blocks, jnp.zeros_like(carried_final)))
    own_grad = first[4]

    def relay_back(turn, leaving):
        return shifted(totals[:, :, None, None] * leaving + own_grad, "seq", -1)

    outgoing = lax.fori_loop(0, lax.axis_size("seq") - 1, relay_back, empty)
    second_operand = inter_back((jnp.zeros_like(carried_result), outgoing))
    x_part, raw_local, b_part, c_local, bias_local, alog_local, skip_part = backward(
        (mixed_blocks, outgoing)
    )
    raw_part = raw_local + first[0] + second_operand[0]
    c_part = c_local + first[1] + second_operand[1]
    bias_part = bias_local + first[2] + second_operand[2]
    alog_part = alog_local + first[3] + second_operand[3]
    b_total, c_total = lax.psum((b_part, c_part), "head")
    bias_grad, alog_grad, residual_factor_cotangent, gain_grad = lax.psum(
        (bias_part, alog_part, skip_part, gain_part), ("seq", "batch")
    )
    return (
        normed,
        x_part.reshape(rows, tokens, width),
        z_grad,
        b_total.reshape(rows, tokens, STATE),
        c_total.reshape(rows, tokens, STATE),
        raw_part.reshape(rows, tokens, heads),
        bias_grad,
        alog_grad,
        residual_factor_cotangent,
        gain_grad,
    )


def solution(mesh):
    placed = (
        P(("groups", "batch"), "seq", "head"),
        P(("groups", "batch"), "seq", "head"),
        P(("groups", "batch"), "seq", None),
        P(("groups", "batch"), "seq", None),
        P(("groups", "batch"), "seq", "head"),
        P(("groups", "batch"), None),
        P("head"),
        P("head"),
        P("head"),
        P("head"),
        P(("groups", "batch"), "seq", "head"),
    )
    return jax.shard_map(
        shards,
        mesh=mesh,
        in_specs=placed,
        out_specs=(
            P(("groups", "batch"), "seq", "head"),
            P(("groups", "batch"), "seq", "head"),
            P(("groups", "batch"), "seq", "head"),
            P(("groups", "batch"), "seq", None),
            P(("groups", "batch"), "seq", None),
            P(("groups", "batch"), "seq", "head"),
            P(("groups", "head")),
            P(("groups", "head")),
            P(("groups", "head")),
            P(("groups", "head")),
        ),
        check_vma=False,
    )
```

profile of v0, /device:TPU:0, one launch (start us, length us, event | category | flops | bytes accessed | tf_op | source)
XLA Modules:
  0.0 638.4 jit_solution(17664971069768408467)
XLA Ops:
  16.6 5.1 reshape.2601
  21.7 4.4 copy.399
  40.5 91.6 %while.196 = (s32[]{:T(128)}, f32[1,24,64,128]{3,2,1,0:T(8,128)S(1)}, f32[2,1,256,24,64]{2,4,3,1,0:T(8,128)}, f32[2,1,256,24]{2,3,1,0:T(8,128)}, f32[2,1,256,24]...) while((s32[]{:T(128)}, ...), condition=%wide.region_6.8_spmd.clone, body=%wide.region_3.7_spmd.clone.sunk | while | flops 2536453120 | bytes 132158992 | solution.py:107
  44.9 9.6 %multiply_dynamic-update-slice_fusion.2 = (f32[2,1,24,256,256]{4,3,2,1,0:T(8,128)}, f32[2,1,24,256,256]{4,3,2,1,0:T(8,128)}, f32[2,1,24,256,256]{4,3,2,1,0:T(8,128)}) fusion(f32[2,1,24,256,256]{4,3,2,1,0:T(8,128)} %get-tuple-element.5146, s32[]{:T(128)} %get-tuple-element.5128, f32[256,256]{1,0:T(8,128)S(1)} %get-tuple-element.4964, ...), kind=kLoop, calls=%fused_computation.40.clone.1 | loop fusion | flops 6291456 | bytes 19251712 | tf_op jit(solution)/shard_map/jvp(vmap())/while/body/jit(dynamic_update_index_in_dim)/dynamic_update_slice | solution.py:107
  66.3 8.4 %fusion.349 = f32[2,1,256,24,64]{2,4,3,1,0:T(8,128)} fusion(f32[2,1,256,24,64]{2,4,3,1,0:T(8,128)} %get-tuple-element.5130, s32[]{:T(128)} %get-tuple-element.5128, f32[256,24,64]{0,2,1:T(8,128)S(1)} %get-tuple-element.4963, f32[256,256]{1,0:T(8,128)S(1)} %get-tuple-element.4964, f32[24,256]{1,0:T(8,128)S(1)} %bitcast_add_fusion.8, ...), kind=kOutput, calls=%fused_computation.70.clone.1 | convolution fusion | flops 1217003520 | bytes 5146112 | tf_op jit(solution)/shard_map/jvp(vmap())/while/body/eval_jaxpr/hij,jhp->ihp/dot_general | solution.py:50
  90.5 9.6 %multiply_dynamic-update-slice_fusion.2 = (f32[2,1,24,256,256]{4,3,2,1,0:T(8,128)}, f32[2,1,24,256,256]{4,3,2,1,0:T(8,128)}, f32[2,1,24,256,256]{4,3,2,1,0:T(8,128)}) fusion(f32[2,1,24,256,256]{4,3,2,1,0:T(8,128)} %get-tuple-element.5146, s32[]{:T(128)} %get-tuple-element.5128, f32[256,256]{1,0:T(8,128)S(1)} %get-tuple-element.4964, ...), kind=kLoop, calls=%fused_computation.40.clone.1 | loop fusion | flops 6291456 | bytes 19251712 | tf_op jit(solution)/shard_map/jvp(vmap())/while/body/jit(dynamic_update_index_in_dim)/dynamic_update_slice | solution.py:107
  112.0 8.4 %fusion.349 = f32[2,1,256,24,64]{2,4,3,1,0:T(8,128)} fusion(f32[2,1,256,24,64]{2,4,3,1,0:T(8,128)} %get-tuple-element.5130, s32[]{:T(128)} %get-tuple-element.5128, f32[256,24,64]{0,2,1:T(8,128)S(1)} %get-tuple-element.4963, f32[256,256]{1,0:T(8,128)S(1)} %get-tuple-element.4964, f32[24,256]{1,0:T(8,128)S(1)} %bitcast_add_fusion.8, ...), kind=kOutput, calls=%fused_computation.70.clone.1 | convolution fusion | flops 1217003520 | bytes 5146112 | tf_op jit(solution)/shard_map/jvp(vmap())/while/body/eval_jaxpr/hij,jhp->ihp/dot_general | solution.py:50
  136.3 61.8 %while.193 = (s32[]{:T(128)}, f32[1,24,64,128]{3,2,1,0:T(8,128)S(1)}, f32[1,24]{1,0:T(1,128)S(1)}, f32[1,24,64,128]{3,2,1,0:T(8,128)S(1)}, s32[]{:T(128)}) while((s32[]{:T(128)}, f32[1,24,64,128]{3,2,1,0:T(8,128)S(1)}, f32[1,24]{1,0:T(1,128)S(1)}, f32[1,24,64,128]{3,2,1,0:T(8,128)S(1)}, s32[]{:T(128)}) %tuple.401), condition=%wide.region_11.13_spmd, body=%wide.region_10.12_spmd.sunk | while | flops 393218 | bytes 5505221 | solution.py:127
  136.4 5.0 collective-permute-start
  141.4 16.7 %collective-permute-done = f32[1,24,64,128]{3,2,1,0:T(8,128)S(1)} collective-permute-done((f32[1,24,64,128]{3,2,1,0:T(8,128)S(1)}, f32[1,24,64,128]{3,2,1,0:T(8,128)S(1)}, u32[]{:S(2)}, u32[]{:S(2)}) %collective-permute-start) | collective-permute-done | bytes 786464 | tf_op jit(solution)/shard_map/while/body/eval_jaxpr/ppermute | solution.py:20
  158.3 4.4 collective-permute-start
  162.7 15.8 %collective-permute-done = f32[1,24,64,128]{3,2,1,0:T(8,128)S(1)} collective-permute-done((f32[1,24,64,128]{3,2,1,0:T(8,128)S(1)}, f32[1,24,64,128]{3,2,1,0:T(8,128)S(1)}, u32[]{:S(2)}, u32[]{:S(2)}) %collective-permute-start) | collective-permute-done | bytes 786464 | tf_op jit(solution)/shard_map/while/body/eval_jaxpr/ppermute | solution.py:20
  178.7 4.4 collective-permute-start
  183.2 14.9 %collective-permute-done = f32[1,24,64,128]{3,2,1,0:T(8,128)S(1)} collective-permute-done((f32[1,24,64,128]{3,2,1,0:T(8,128)S(1)}, f32[1,24,64,128]{3,2,1,0:T(8,128)S(1)}, u32[]{:S(2)}, u32[]{:S(2)}) %collective-permute-start) | collective-permute-done | bytes 786464 | tf_op jit(solution)/shard_map/while/body/eval_jaxpr/ppermute | solution.py:20
  202.5 19.0 %while.194 = (s32[]{:T(128)}, f32[1,24,64,128]{3,2,1,0:T(8,128)S(1)}, f32[2,1,256,24,64]{2,4,3,1,0:T(8,128)}, f32[2,1,256,24]{2,0,3,1:T(2,128)S(1)}, f32[2,1,256...) while((s32[]{:T(128)}, ...), condition=%wide.region_15.17_spmd, body=%wide.region_12.16_spmd.sunk | while | flops 605454976 | bytes 8082055 | solution.py:133
  207.0 3.0 bitcast_dynamic-update-slice_fusion.17
  216.3 3.2 bitcast_dynamic-update-slice_fusion.17
  221.5 4.0 add.325
  225.5 4.2 copy.410
  229.7 4.1 add.326
  236.4 4.1 multiply_reduce_fusion.4
  245.7 4.0 fusion.246
  252.2 6.4 multiply_convert_fusion
  258.6 5.2 transpose_reshape.35
  268.3 46.2 %while.197 = (s32[]{:T(128)}, f32[24]{0:T(128)}, f32[24]{0:T(128)}, f32[1,24,64,128]{3,2,1,0:T(8,128)}, f32[2,1,256,24]{2,0,3,1:T(2,128)}, /*index=5*/f32[2,1,25...) while((s32[]{:T(128)}, f32[24]{0:T(128)}, f32[24]{0:T(128)}, ...), condition=%wide.region_27.29_spmd.clone, body=%wide.region_20.28_spmd.clone.sunk | while | flops 1211541760 | bytes 17379180 | solution.py:133
  287.0 3.3 fusion.362
  307.8 3.5 fusion.361
  311.2 3.3 fusion.362
  315.5 71.5 %while.195 = (s32[]{:T(128)}, f32[1,24,64,128]{3,2,1,0:T(8,128)}, f32[1,24]{1,0:T(1,128)}, f32[1,24,64,128]{3,2,1,0:T(8,128)}, s32[]{:T(128)}) while((s32[]{:T(128)}, f32[1,24,64,128]{3,2,1,0:T(8,128)}, f32[1,24]{1,0:T(1,128)}, f32[1,24,64,128]{3,2,1,0:T(8,128)}, s32[]{:T(128)}) %tuple.402), condition=%wide.region_29.31_spmd, body=%wide.region_28.30_spmd.sunk | while | flops 393218 | bytes 5505221 | solution.py:170
  319.1 21.3 %collective-permute-done.1 = f32[1,24,64,128]{3,2,1,0:T(8,128)} collective-permute-done((f32[1,24,64,128]{3,2,1,0:T(8,128)}, f32[1,24,64,128]{3,2,1,0:T(8,128)}, u32[]{:S(2)}, u32[]{:S(2)}) %collective-permute-start.1) | collective-permute-done | bytes 786464 | tf_op jit(solution)/shard_map/while/body/eval_jaxpr/ppermute | solution.py:20
  344.1 20.0 %collective-permute-done.1 = f32[1,24,64,128]{3,2,1,0:T(8,128)} collective-permute-done((f32[1,24,64,128]{3,2,1,0:T(8,128)}, f32[1,24,64,128]{3,2,1,0:T(8,128)}, u32[]{:S(2)}, u32[]{:S(2)}) %collective-permute-start.1) | collective-permute-done | bytes 786464 | tf_op jit(solution)/shard_map/while/body/eval_jaxpr/ppermute | solution.py:20
  367.8 19.1 %collective-permute-done.1 = f32[1,24,64,128]{3,2,1,0:T(8,128)} collective-permute-done((f32[1,24,64,128]{3,2,1,0:T(8,128)}, f32[1,24,64,128]{3,2,1,0:T(8,128)}, u32[]{:S(2)}, u32[]{:S(2)}) %collective-permute-start.1) | collective-permute-done | bytes 786464 | tf_op jit(solution)/shard_map/while/body/eval_jaxpr/ppermute | solution.py:20
  390.4 59.4 %while.199 = (s32[]{:T(128)}, f32[24]{0:T(128)}, f32[24]{0:T(128)}, f32[1,24,64,128]{3,2,1,0:T(8,128)}, f32[2,1,256,24]{2,0,3,1:T(2,128)}, /*index=5*/f32[2,1,25...) while((s32[]{:T(128)}, f32[24]{0:T(128)}, f32[24]{0:T(128)}, ...), condition=%wide.region_53.55_spmd.clone, body=%wide.region_46.54_spmd.clone.sunk | while | flops 1210368256 | bytes 12806403 | solution.py:133
  394.1 2.7 constant_dynamic-slice_fusion.44
  396.8 3.3 copy.562
  400.1 2.8 multiply_reduce_fusion.10
  403.7 3.2 reduce-window.136
  412.0 3.5 fusion.400
  415.4 4.4 fusion.401
  423.3 2.7 constant_dynamic-slice_fusion.44
  426.0 3.3 copy.562
  429.3 2.8 multiply_reduce_fusion.10
  433.0 3.2 reduce-window.136
  441.9 3.5 fusion.400
  445.4 4.4 fusion.401
  453.2 139.7 %while.198 = (s32[]{:T(128)}, f32[24]{0:T(128)}, f32[24]{0:T(128)}, f32[24]{0:T(128)}, f32[1,24,64,128]{3,2,1,0:T(8,128)}, /*index=5*/bf16[2,1,256,24,64]{2,4,3,...) while((s32[]{:T(128)}, f32[24]{0:T(128)}, f32[24]{0:T(128)}, ...), condition=%wide.region_44.46_spmd.clone, body=%wide.region_30.45_spmd.clone.sunk | while | flops 5053704192 | bytes 93027016 | solution.py:107
  453.5 3.9 fusion.373
  458.0 9.4 %fusion.374 = (f32[24]{0:T(128)}, f32[256,24]{0,1:T(8,128)S(1)}, f32[256,24]{0,1:T(8,128)}, f32[1,256,24,64]{1,3,2,0:T(8,128)}) fusion(f32[2,1,256,24,64]{2,4,3,1,0:T(8,128)S(1)} %copy-done.13, s32[]{:T(128)S(6)} %sub.230, f32[2,1,256,24,64]{2,4,3,1,0:T(8,128)S(1)} %get-tuple-element.5463, f32[2,1,256,24,64]{2,4,3,1,0:T(8,128)} %get-tuple-element.5474, ...), kind=kOutput, calls=%fused_computation.214.clone.1 | convolution fusion | flops 1211092992 | bytes 15804000 | tf_op jit(solution)/shard_map/transpose(jvp(vmap()))/while/body/eval_jaxpr/hij,jhp->ihp/dot_general | solution.py:50
  479.9 12.6 %fusion.378 = (f32[24,256]{1,0:T(8,128)}, f32[24,256]{1,0:T(8,128)}, f32[256,256]{1,0:T(8,128)}) fusion(f32[2,1,24,256,256]{4,3,2,1,0:T(8,128)} %get-tuple-element.5468, s32[]{:T(128)S(6)} %sub.230, f32[256,256]{1,0:T(8,128)S(1)} %dynamic-slice_bitcast_fusion.7, pred[2,1,24,256,256]{4,3,2,1,0:T(32,128)(4,1)} %get-tuple-element.5465, ...), kind=kOutput, calls=%fused_computation.306.clone.1 | convolution fusion | flops 1220464640 | bytes 17876480 | tf_op jit(solution)/shard_map/transpose(jvp(vmap()))/while/body/eval_jaxpr/hij,jhp->ihp/dot_general | solution.py:50
  508.0 2.7 fusion.386
  510.7 2.6 fusion.388
  514.4 3.8 fusion.387
  519.0 3.4 fusion.385
  522.4 3.9 fusion.373
  527.0 9.4 %fusion.374 = (f32[24]{0:T(128)}, f32[256,24]{0,1:T(8,128)S(1)}, f32[256,24]{0,1:T(8,128)}, f32[1,256,24,64]{1,3,2,0:T(8,128)}) fusion(f32[2,1,256,24,64]{2,4,3,1,0:T(8,128)S(1)} %copy-done.13, s32[]{:T(128)S(6)} %sub.230, f32[2,1,256,24,64]{2,4,3,1,0:T(8,128)S(1)} %get-tuple-element.5463, f32[2,1,256,24,64]{2,4,3,1,0:T(8,128)} %get-tuple-element.5474, ...), kind=kOutput, calls=%fused_computation.214.clone.1 | convolution fusion | flops 1211092992 | bytes 15804000 | tf_op jit(solution)/shard_map/transpose(jvp(vmap()))/while/body/eval_jaxpr/hij,jhp->ihp/dot_general | solution.py:50
  549.0 12.6 %fusion.378 = (f32[24,256]{1,0:T(8,128)}, f32[24,256]{1,0:T(8,128)}, f32[256,256]{1,0:T(8,128)}) fusion(f32[2,1,24,256,256]{4,3,2,1,0:T(8,128)} %get-tuple-element.5468, s32[]{:T(128)S(6)} %sub.230, f32[256,256]{1,0:T(8,128)S(1)} %dynamic-slice_bitcast_fusion.7, pred[2,1,24,256,256]{4,3,2,1,0:T(32,128)(4,1)} %get-tuple-element.5465, ...), kind=kOutput, calls=%fused_computation.306.clone.1 | convolution fusion | flops 1220464640 | bytes 17876480 | tf_op jit(solution)/shard_map/transpose(jvp(vmap()))/while/body/eval_jaxpr/hij,jhp->ihp/dot_general | solution.py:50
  578.5 2.7 fusion.386
  581.2 2.6 fusion.388
  584.9 3.8 fusion.387
  589.5 3.4 fusion.385
  595.5 20.3 %all-reduce.4 = (f32[24]{0:T(128)}, f32[24]{0:T(128)}, f32[24]{0:T(128)}, f32[1536]{0:T(1024)}) all-reduce(f32[24]{0:T(128)S(1)} %get-tuple-element.4106, f32[24]{0:T(128)S(1)} %get-tuple-element.4105, f32[24]{0:T(128)} %get-tuple-element.2410, ...), channel_id=1, replica_groups=mesh['groups'=2,'seq'=4,'batch'=2,'head'=2] {'seq','batch'}, use_global_device_ids=true, to_apply=%region_55.57 | all-reduce | flops 1608 | bytes 12864 | tf_op jit(solution)/shard_map/psum | solution.py:180
  617.3 3.5 copy.437
  620.7 2.9 reshape.2602
  623.7 2.7 copy.432
  (610 shorter events, 256.0 us)
Async XLA Ops:
  7.2 620.8 %all-reduce.8.cloned.1.call-start = ((), (), s32[]{:S(2)}) async-start(), calls=%async_computation | async-start | bytes 1048576 | tf_op jit(solution)/shard_map/psum | solution.py:179
  15.0 11.0 %copy-start.61 = (s32[2]{0:T(128)}, s32[2]{0:T(128)S(1)}, u32[]{:S(2)}) copy-start(s32[2]{0:T(128)S(1)} %fusion.254) | copy-start | bytes 28
  34.8 5.7 copy-start.32
  43.7 10.8 %copy-start.41 = (f32[2,1,1,256]{3,2,1,0:T(1,128)}, f32[2,1,1,256]{3,2,1,0:T(1,128)S(1)}, u32[]{:S(2)}) copy-start(f32[2,1,1,256]{3,2,1,0:T(1,128)S(1)} %get-tuple-element.5172) | copy-start | bytes 6148 | tf_op jit(solution)/shard_map/jvp(vmap())/while
  44.9 13.9 %copy-start.4 = (bf16[2,1,256,24,64]{2,4,3,1,0:T(8,128)(2,1)S(1)}, bf16[2,1,256,24,64]{2,4,3,1,0:T(8,128)(2,1)}, u32[]{:S(2)}) copy-start(bf16[2,1,256,24,64]{2,4,3,1,0:T(8,128)(2,1)} %get-tuple-element.5197) | copy-start | bytes 4718596 | tf_op jit(solution)/shard_map/jvp(vmap())/while
  44.9 13.9 %copy-start.6 = (f32[2,1,256,24,64]{2,4,3,1,0:T(8,128)S(1)}, f32[2,1,256,24,64]{2,4,3,1,0:T(8,128)}, u32[]{:S(2)}) copy-start(f32[2,1,256,24,64]{2,4,3,1,0:T(8,128)} %get-tuple-element.5147) | copy-start | bytes 9437188 | tf_op jit(solution)/shard_map/jvp(vmap())/while
  44.9 13.9 %copy-start.8 = (f32[2,1,256,24,64]{2,4,3,1,0:T(8,128)S(1)}, f32[2,1,256,24,64]{2,4,3,1,0:T(8,128)}, u32[]{:S(2)}) copy-start(f32[2,1,256,24,64]{2,4,3,1,0:T(8,128)} %get-tuple-element.5152) | copy-start | bytes 9437188 | tf_op jit(solution)/shard_map/jvp(vmap())/while
  44.9 14.0 %copy-start.11 = (f32[2,1,256,24,64]{2,4,3,1,0:T(8,128)S(1)}, f32[2,1,256,24,64]{2,4,3,1,0:T(8,128)}, u32[]{:S(2)}) copy-start(f32[2,1,256,24,64]{2,4,3,1,0:T(8,128)} %get-tuple-element.5145) | copy-start | bytes 9437188 | tf_op jit(solution)/shard_map/jvp(vmap())/while
  74.8 8.1 %copy-start.48 = (f32[24]{0:T(128)S(1)}, f32[24]{0:T(128)}, u32[]{:S(2)}) copy-start(f32[24]{0:T(128)} %get-tuple-element.4970) | copy-start | bytes 292 | tf_op jit(solution)/shard_map/jvp(vmap())/while
  74.8 8.1 %copy-start.49 = (f32[2,1,24]{2,1,0:T(1,128)S(1)}, f32[2,1,24]{2,1,0:T(1,128)}, u32[]{:S(2)}) copy-start(f32[2,1,24]{2,1,0:T(1,128)} %get-tuple-element.5135) | copy-start | bytes 580 | tf_op jit(solution)/shard_map/jvp(vmap())/while
  74.8 8.1 %copy-start.47 = (f32[24]{0:T(128)S(1)}, f32[24]{0:T(128)}, u32[]{:S(2)}) copy-start(f32[24]{0:T(128)} %get-tuple-element.4982) | copy-start | bytes 292 | tf_op jit(solution)/shard_map/jvp(vmap())/while
  74.8 8.1 %copy-start.57 = (f32[2,1,24,1,1]{2,4,3,1,0:T(1,128)S(1)}, f32[2,1,24,1,1]{2,4,3,1,0:T(1,128)}, u32[]{:S(2)}) copy-start(f32[2,1,24,1,1]{2,4,3,1,0:T(1,128)} %get-tuple-element.5153) | copy-start | bytes 580 | tf_op jit(solution)/shard_map/jvp(vmap())/while
  74.8 8.1 %copy-start.51 = (f32[2,1,1]{0,2,1:T(1,128)S(1)}, f32[2,1,1]{0,2,1:T(1,128)}, u32[]{:S(2)}) copy-start(f32[2,1,1]{0,2,1:T(1,128)} %get-tuple-element.5136) | copy-start | bytes 28 | tf_op jit(solution)/shard_map/jvp(vmap())/while
  74.8 10.8 %copy-start.22 = (f32[2,1,128,256]{2,3,1,0:T(8,128)S(1)}, f32[2,1,128,256]{2,3,1,0:T(8,128)}, u32[]{:S(2)}) copy-start(f32[2,1,128,256]{2,3,1,0:T(8,128)} %get-tuple-element.5140) | copy-start | bytes 786436 | tf_op jit(solution)/shard_map/jvp(vmap())/while
  74.8 11.5 %copy-start.42 = (f32[2,1,1,256]{3,2,1,0:T(1,128)S(1)}, f32[2,1,1,256]{3,2,1,0:T(1,128)}, u32[]{:S(2)}) copy-start(f32[2,1,1,256]{3,2,1,0:T(1,128)} %copy-done.41) | copy-start | bytes 6148 | tf_op jit(solution)/shard_map/jvp(vmap())/while
  89.3 10.8 %copy-start.41 = (f32[2,1,1,256]{3,2,1,0:T(1,128)}, f32[2,1,1,256]{3,2,1,0:T(1,128)S(1)}, u32[]{:S(2)}) copy-start(f32[2,1,1,256]{3,2,1,0:T(1,128)S(1)} %get-tuple-element.5172) | copy-start | bytes 6148 | tf_op jit(solution)/shard_map/jvp(vmap())/while
  90.5 14.0 %copy-start.4 = (bf16[2,1,256,24,64]{2,4,3,1,0:T(8,128)(2,1)S(1)}, bf16[2,1,256,24,64]{2,4,3,1,0:T(8,128)(2,1)}, u32[]{:S(2)}) copy-start(bf16[2,1,256,24,64]{2,4,3,1,0:T(8,128)(2,1)} %get-tuple-element.5197) | copy-start | bytes 4718596 | tf_op jit(solution)/shard_map/jvp(vmap())/while
  90.5 14.0 %copy-start.6 = (f32[2,1,256,24,64]{2,4,3,1,0:T(8,128)S(1)}, f32[2,1,256,24,64]{2,4,3,1,0:T(8,128)}, u32[]{:S(2)}) copy-start(f32[2,1,256,24,64]{2,4,3,1,0:T(8,128)} %get-tuple-element.5147) | copy-start | bytes 9437188 | tf_op jit(solution)/shard_map/jvp(vmap())/while
  90.5 14.0 %copy-start.8 = (f32[2,1,256,24,64]{2,4,3,1,0:T(8,128)S(1)}, f32[2,1,256,24,64]{2,4,3,1,0:T(8,128)}, u32[]{:S(2)}) copy-start(f32[2,1,256,24,64]{2,4,3,1,0:T(8,128)} %get-tuple-element.5152) | copy-start | bytes 9437188 | tf_op jit(solution)/shard_map/jvp(vmap())/while
  90.5 14.0 %copy-start.11 = (f32[2,1,256,24,64]{2,4,3,1,0:T(8,128)S(1)}, f32[2,1,256,24,64]{2,4,3,1,0:T(8,128)}, u32[]{:S(2)}) copy-start(f32[2,1,256,24,64]{2,4,3,1,0:T(8,128)} %get-tuple-element.5145) | copy-start | bytes 9437188 | tf_op jit(solution)/shard_map/jvp(vmap())/while
  120.5 8.1 %copy-start.48 = (f32[24]{0:T(128)S(1)}, f32[24]{0:T(128)}, u32[]{:S(2)}) copy-start(f32[24]{0:T(128)} %get-tuple-element.4970) | copy-start | bytes 292 | tf_op jit(solution)/shard_map/jvp(vmap())/while
  120.5 8.1 %copy-start.49 = (f32[2,1,24]{2,1,0:T(1,128)S(1)}, f32[2,1,24]{2,1,0:T(1,128)}, u32[]{:S(2)}) copy-start(f32[2,1,24]{2,1,0:T(1,128)} %get-tuple-element.5135) | copy-start | bytes 580 | tf_op jit(solution)/shard_map/jvp(vmap())/while
  120.5 8.1 %copy-start.47 = (f32[24]{0:T(128)S(1)}, f32[24]{0:T(128)}, u32[]{:S(2)}) copy-start(f32[24]{0:T(128)} %get-tuple-element.4982) | copy-start | bytes 292 | tf_op jit(solution)/shard_map/jvp(vmap())/while
  120.5 8.1 %copy-start.57 = (f32[2,1,24,1,1]{2,4,3,1,0:T(1,128)S(1)}, f32[2,1,24,1,1]{2,4,3,1,0:T(1,128)}, u32[]{:S(2)}) copy-start(f32[2,1,24,1,1]{2,4,3,1,0:T(1,128)} %get-tuple-element.5153) | copy-start | bytes 580 | tf_op jit(solution)/shard_map/jvp(vmap())/while
  120.5 8.1 %copy-start.51 = (f32[2,1,1]{0,2,1:T(1,128)S(1)}, f32[2,1,1]{0,2,1:T(1,128)}, u32[]{:S(2)}) copy-start(f32[2,1,1]{0,2,1:T(1,128)} %get-tuple-element.5136) | copy-start | bytes 28 | tf_op jit(solution)/shard_map/jvp(vmap())/while
  120.5 10.9 %copy-start.22 = (f32[2,1,128,256]{2,3,1,0:T(8,128)S(1)}, f32[2,1,128,256]{2,3,1,0:T(8,128)}, u32[]{:S(2)}) copy-start(f32[2,1,128,256]{2,3,1,0:T(8,128)} %get-tuple-element.5140) | copy-start | bytes 786436 | tf_op jit(solution)/shard_map/jvp(vmap())/while
  120.5 11.6 %copy-start.42 = (f32[2,1,1,256]{3,2,1,0:T(1,128)S(1)}, f32[2,1,1,256]{3,2,1,0:T(1,128)}, u32[]{:S(2)}) copy-start(f32[2,1,1,256]{3,2,1,0:T(1,128)} %copy-done.41) | copy-start | bytes 6148 | tf_op jit(solution)/shard_map/jvp(vmap())/while
  136.4 21.7 %collective-permute-start = (f32[1,24,64,128]{3,2,1,0:T(8,128)S(1)}, f32[1,24,64,128]{3,2,1,0:T(8,128)S(1)}, u32[]{:S(2)}, u32[]{:S(2)}) collective-permute-start(f32[1,24,64,128]{3,2,1,0:T(8,128)S(1)} %multiply_add_fusion.4), channel_id=1, source_target_pairs={{0,4},{4,8},{8,12},{1,5},{5,9},{9,13},{2,6},{6,10},{10,14},{3,7},{... | collective-permute-start | bytes 2359304 | tf_op jit(solution)/shard_map/while/body/eval_jaxpr/ppermute | solution.py:20
  158.3 20.3 %collective-permute-start = (f32[1,24,64,128]{3,2,1,0:T(8,128)S(1)}, f32[1,24,64,128]{3,2,1,0:T(8,128)S(1)}, u32[]{:S(2)}, u32[]{:S(2)}) collective-permute-start(f32[1,24,64,128]{3,2,1,0:T(8,128)S(1)} %multiply_add_fusion.4), channel_id=1, source_target_pairs={{0,4},{4,8},{8,12},{1,5},{5,9},{9,13},{2,6},{6,10},{10,14},{3,7},{... | collective-permute-start | bytes 2359304 | tf_op jit(solution)/shard_map/while/body/eval_jaxpr/ppermute | solution.py:20
  178.7 19.4 %collective-permute-start = (f32[1,24,64,128]{3,2,1,0:T(8,128)S(1)}, f32[1,24,64,128]{3,2,1,0:T(8,128)S(1)}, u32[]{:S(2)}, u32[]{:S(2)}) collective-permute-start(f32[1,24,64,128]{3,2,1,0:T(8,128)S(1)} %multiply_add_fusion.4), channel_id=1, source_target_pairs={{0,4},{4,8},{8,12},{1,5},{5,9},{9,13},{2,6},{6,10},{10,14},{3,7},{... | collective-permute-start | bytes 2359304 | tf_op jit(solution)/shard_map/while/body/eval_jaxpr/ppermute | solution.py:20
  277.1 13.1 %copy-start.38 = (f32[2,1,24]{2,1,0:T(1,128)S(1)}, f32[2,1,24]{2,1,0:T(1,128)}, u32[]{:S(2)}) copy-start(f32[2,1,24]{2,1,0:T(1,128)} %copy-done.37) | copy-start | bytes 580 | tf_op jit(solution)/shard_map/transpose(jvp(vmap()))/while
  277.1 13.1 %copy-start.54 = (f32[2,1,1]{0,2,1:T(1,128)S(1)}, f32[2,1,1]{0,2,1:T(1,128)}, u32[]{:S(2)}) copy-start(f32[2,1,1]{0,2,1:T(1,128)} %copy-done.53) | copy-start | bytes 28 | tf_op jit(solution)/shard_map/transpose(jvp(vmap()))/while
  299.4 15.1 %copy-start.38 = (f32[2,1,24]{2,1,0:T(1,128)S(1)}, f32[2,1,24]{2,1,0:T(1,128)}, u32[]{:S(2)}) copy-start(f32[2,1,24]{2,1,0:T(1,128)} %copy-done.37) | copy-start | bytes 580 | tf_op jit(solution)/shard_map/transpose(jvp(vmap()))/while
  299.4 15.1 %copy-start.54 = (f32[2,1,1]{0,2,1:T(1,128)S(1)}, f32[2,1,1]{0,2,1:T(1,128)}, u32[]{:S(2)}) copy-start(f32[2,1,1]{0,2,1:T(1,128)} %copy-done.53) | copy-start | bytes 28 | tf_op jit(solution)/shard_map/transpose(jvp(vmap()))/while
  305.1 6.2 copy-start.1
  317.8 22.6 %collective-permute-start.1 = (f32[1,24,64,128]{3,2,1,0:T(8,128)}, f32[1,24,64,128]{3,2,1,0:T(8,128)}, u32[]{:S(2)}, u32[]{:S(2)}) collective-permute-start(f32[1,24,64,128]{3,2,1,0:T(8,128)} %multiply_add_fusion.5), channel_id=1, source_target_pairs={{4,0},{8,4},{12,8},{5,1},{9,5},{13,9},{6,2},{10,6},{14,10},{7,3},{... | collective-permute-start | bytes 2359304 | tf_op jit(solution)/shard_map/while/body/eval_jaxpr/ppermute | solution.py:20
  342.8 21.3 %collective-permute-start.1 = (f32[1,24,64,128]{3,2,1,0:T(8,128)}, f32[1,24,64,128]{3,2,1,0:T(8,128)}, u32[]{:S(2)}, u32[]{:S(2)}) collective-permute-start(f32[1,24,64,128]{3,2,1,0:T(8,128)} %multiply_add_fusion.5), channel_id=1, source_target_pairs={{4,0},{8,4},{12,8},{5,1},{9,5},{13,9},{6,2},{10,6},{14,10},{7,3},{... | collective-permute-start | bytes 2359304 | tf_op jit(solution)/shard_map/while/body/eval_jaxpr/ppermute | solution.py:20
  366.5 20.4 %collective-permute-start.1 = (f32[1,24,64,128]{3,2,1,0:T(8,128)}, f32[1,24,64,128]{3,2,1,0:T(8,128)}, u32[]{:S(2)}, u32[]{:S(2)}) collective-permute-start(f32[1,24,64,128]{3,2,1,0:T(8,128)} %multiply_add_fusion.5), channel_id=1, source_target_pairs={{4,0},{8,4},{12,8},{5,1},{9,5},{13,9},{6,2},{10,6},{14,10},{7,3},{... | collective-permute-start | bytes 2359304 | tf_op jit(solution)/shard_map/while/body/eval_jaxpr/ppermute | solution.py:20
  390.6 9.5 %copy-start.39 = (f32[2,1,24]{2,1,0:T(1,128)}, f32[2,1,24]{2,1,0:T(1,128)S(1)}, u32[]{:S(2)}) copy-start(f32[2,1,24]{2,1,0:T(1,128)S(1)} %get-tuple-element.5544) | copy-start | bytes 580 | tf_op jit(solution)/shard_map/transpose(jvp(vmap()))/while
  390.6 9.5 %copy-start.55 = (f32[2,1,1]{0,2,1:T(1,128)}, f32[2,1,1]{0,2,1:T(1,128)S(1)}, u32[]{:S(2)}) copy-start(f32[2,1,1]{0,2,1:T(1,128)S(1)} %get-tuple-element.5543) | copy-start | bytes 28 | tf_op jit(solution)/shard_map/transpose(jvp(vmap()))/while
  403.7 16.1 %copy-start.40 = (f32[2,1,24]{2,1,0:T(1,128)S(1)}, f32[2,1,24]{2,1,0:T(1,128)}, u32[]{:S(2)}) copy-start(f32[2,1,24]{2,1,0:T(1,128)} %copy-done.39) | copy-start | bytes 580 | tf_op jit(solution)/shard_map/transpose(jvp(vmap()))/while
  403.7 16.1 %copy-start.56 = (f32[2,1,1]{0,2,1:T(1,128)S(1)}, f32[2,1,1]{0,2,1:T(1,128)}, u32[]{:S(2)}) copy-start(f32[2,1,1]{0,2,1:T(1,128)} %copy-done.55) | copy-start | bytes 28 | tf_op jit(solution)/shard_map/transpose(jvp(vmap()))/while
  419.8 9.5 %copy-start.39 = (f32[2,1,24]{2,1,0:T(1,128)}, f32[2,1,24]{2,1,0:T(1,128)S(1)}, u32[]{:S(2)}) copy-start(f32[2,1,24]{2,1,0:T(1,128)S(1)} %get-tuple-element.5544) | copy-start | bytes 580 | tf_op jit(solution)/shard_map/transpose(jvp(vmap()))/while
  419.8 9.5 %copy-start.55 = (f32[2,1,1]{0,2,1:T(1,128)}, f32[2,1,1]{0,2,1:T(1,128)S(1)}, u32[]{:S(2)}) copy-start(f32[2,1,1]{0,2,1:T(1,128)S(1)} %get-tuple-element.5543) | copy-start | bytes 28 | tf_op jit(solution)/shard_map/transpose(jvp(vmap()))/while
  433.0 16.8 %copy-start.40 = (f32[2,1,24]{2,1,0:T(1,128)S(1)}, f32[2,1,24]{2,1,0:T(1,128)}, u32[]{:S(2)}) copy-start(f32[2,1,24]{2,1,0:T(1,128)} %copy-done.39) | copy-start | bytes 580 | tf_op jit(solution)/shard_map/transpose(jvp(vmap()))/while
  433.0 16.8 %copy-start.56 = (f32[2,1,1]{0,2,1:T(1,128)S(1)}, f32[2,1,1]{0,2,1:T(1,128)}, u32[]{:S(2)}) copy-start(f32[2,1,1]{0,2,1:T(1,128)} %copy-done.55) | copy-start | bytes 28 | tf_op jit(solution)/shard_map/transpose(jvp(vmap()))/while
  498.9 11.8 %copy-start.18 = (f32[1,1,256,24,1]{2,0,4,3,1:T(1,128)S(1)}, f32[1,1,256,24,1]{2,0,4,3,1:T(1,128)}, u32[]{:S(2)}) copy-start(f32[1,1,256,24,1]{2,0,4,3,1:T(1,128)} %get-tuple-element.5062) | copy-start | bytes 73732 | tf_op jit(solution)/shard_map/transpose(jvp(vmap()))/while
  508.0 5.4 copy-start.24
  508.0 5.4 copy-start.27
  508.0 6.4 %copy-start.10 = (f32[2,1,256,24,64]{2,4,3,1,0:T(8,128)S(1)}, f32[2,1,256,24,64]{2,4,3,1,0:T(8,128)}, u32[]{:S(2)}) copy-start(f32[2,1,256,24,64]{2,4,3,1,0:T(8,128)} %get-tuple-element.5486) | copy-start | bytes 9437188 | tf_op jit(solution)/shard_map/transpose(jvp(vmap()))/while
  508.0 6.4 %copy-start.25 = (f32[2,1,256,128]{3,2,1,0:T(8,128)S(1)}, f32[2,1,256,128]{3,2,1,0:T(8,128)}, u32[]{:S(2)}) copy-start(f32[2,1,256,128]{3,2,1,0:T(8,128)} %get-tuple-element.5417) | copy-start | bytes 786436 | tf_op jit(solution)/shard_map/transpose(jvp(vmap()))/while
  510.7 8.3 %copy-start.35 = (f32[24]{0:T(128)S(1)}, f32[24]{0:T(128)}, u32[]{:S(2)}) copy-start(f32[24]{0:T(128)} %get-tuple-element.5061) | copy-start | bytes 292 | tf_op jit(solution)/shard_map/transpose(jvp(vmap()))/while
  510.7 8.3 %copy-start.44 = (f32[24]{0:T(128)S(1)}, f32[24]{0:T(128)}, u32[]{:S(2)}) copy-start(f32[24]{0:T(128)} %get-tuple-element.5413) | copy-start | bytes 292 | tf_op jit(solution)/shard_map/transpose(jvp(vmap()))/while
  510.7 8.3 %copy-start.59 = (f32[2,1,24,1,1]{2,4,3,1,0:T(1,128)S(1)}, f32[2,1,24,1,1]{2,4,3,1,0:T(1,128)}, u32[]{:S(2)}) copy-start(f32[2,1,24,1,1]{2,4,3,1,0:T(1,128)} %get-tuple-element.5481) | copy-start | bytes 580 | tf_op jit(solution)/shard_map/transpose(jvp(vmap()))/while
  568.0 13.2 %copy-start.18 = (f32[1,1,256,24,1]{2,0,4,3,1:T(1,128)S(1)}, f32[1,1,256,24,1]{2,0,4,3,1:T(1,128)}, u32[]{:S(2)}) copy-start(f32[1,1,256,24,1]{2,0,4,3,1:T(1,128)} %get-tuple-element.5062) | copy-start | bytes 73732 | tf_op jit(solution)/shard_map/transpose(jvp(vmap()))/while
  575.3 5.9 copy-start.3
  578.5 5.4 copy-start.15
  578.5 5.4 copy-start.24
  578.5 5.4 copy-start.27
  578.5 6.4 %copy-start.10 = (f32[2,1,256,24,64]{2,4,3,1,0:T(8,128)S(1)}, f32[2,1,256,24,64]{2,4,3,1,0:T(8,128)}, u32[]{:S(2)}) copy-start(f32[2,1,256,24,64]{2,4,3,1,0:T(8,128)} %get-tuple-element.5486) | copy-start | bytes 9437188 | tf_op jit(solution)/shard_map/transpose(jvp(vmap()))/while
  578.5 6.4 %copy-start.25 = (f32[2,1,256,128]{3,2,1,0:T(8,128)S(1)}, f32[2,1,256,128]{3,2,1,0:T(8,128)}, u32[]{:S(2)}) copy-start(f32[2,1,256,128]{3,2,1,0:T(8,128)} %get-tuple-element.5417) | copy-start | bytes 786436 | tf_op jit(solution)/shard_map/transpose(jvp(vmap()))/while
  581.2 8.3 %copy-start.35 = (f32[24]{0:T(128)S(1)}, f32[24]{0:T(128)}, u32[]{:S(2)}) copy-start(f32[24]{0:T(128)} %get-tuple-element.5061) | copy-start | bytes 292 | tf_op jit(solution)/shard_map/transpose(jvp(vmap()))/while
  581.2 8.3 %copy-start.44 = (f32[24]{0:T(128)S(1)}, f32[24]{0:T(128)}, u32[]{:S(2)}) copy-start(f32[24]{0:T(128)} %get-tuple-element.5413) | copy-start | bytes 292 | tf_op jit(solution)/shard_map/transpose(jvp(vmap()))/while
  581.2 8.3 %copy-start.59 = (f32[2,1,24,1,1]{2,4,3,1,0:T(1,128)S(1)}, f32[2,1,24,1,1]{2,4,3,1,0:T(1,128)}, u32[]{:S(2)}) copy-start(f32[2,1,24,1,1]{2,4,3,1,0:T(1,128)} %get-tuple-element.5481) | copy-start | bytes 580 | tf_op jit(solution)/shard_map/transpose(jvp(vmap()))/while
  (53 other events, 172.9 us)
Sparse Core Ops, SparseCore 0:
  594.9 18.5 all-reduce.7
where the time goes:
time: 647 us; the launch traced here: 638 us
  local copies, waits for them, and re-layouts  178 us (28%)
  other arithmetic  153 us (24%)
  matrix products  135 us (21%)
  waiting for transfers between devices  108 us (17%)
  blocking collectives  25.3 us (4%)
  starting transfers between devices  17.7 us (3%)
  between operations  14.7 us (2%)
    ppermute x6, waiting for transfers between devices, shifted(): lax.ppermute(value, axis, [(source, source + steps) for source in range(l...  108 us
    dot_general x6, matrix products, block_step(): jnp.einsum('hij,jhp->ihp', mixing, rescaled_quantity, precision=highest)  60.8 us
    dot_general x10, matrix products, inter_step(): jnp.einsum('in,hpn->ihp', c_block, state, precision=highest)  34.2 us
    another operation x103, local copies, waits for them, and re-layouts  34 us
    dynamic_update_slice x18, other arithmetic, forward_one_row(): lax.scan(stepper, start, (x_rows, raw_rows, b_rows, c_rows, segment_rows,...  32.5 us
    unnamed x41, local copies, waits for them, and re-layouts  29.6 us
    dynamic_slice x28, local copies, waits for them, and re-layouts, inter_one_row(): lax.scan(stepper, state, (raw_rows, c_rows, segment_rows, previous_rows))  28.5 us
    dynamic_update_slice x44, local copies, waits for them, and re-layouts, forward_one_row(): lax.scan(stepper, start, (x_rows, raw_rows, b_rows, c_rows, segment_rows,...  26.5 us
  transfers between devices with their start and end apart: 7, of which 6 were waited for; matrix products, arithmetic and copies ran while one was open for 2% of the time, Pallas kernels for 0%

commit v1 on v0

v1 whole, which is shorter than its diff:
```python
from functools import partial

import jax
import jax.numpy as jnp
from jax import lax
from jax.experimental import pallas as pl
from jax.experimental.pallas import tpu as pltpu
from jax.sharding import PartitionSpec as P

STATE = 128
HEADDIM = 64
BLOCK = 128
LANES = 128
GROUP = 32
COLS = 256
CHUNKS = 3
EPSILON = 1e-05
HIGHEST = lax.Precision.HIGHEST
F32 = jnp.float32
BF16 = jnp.bfloat16
VMEM_LIMIT = 56 * 1024 * 1024


def mm(a, b):
    return jnp.dot(a, b, preferred_element_type=F32)


def mm_nt(a, b):
    return lax.dot_general(a, b, (((1,), (1,)), ((), ())), preferred_element_type=F32)


def mm_tn(a, b):
    return lax.dot_general(a, b, (((0,), (0,)), ((), ())), preferred_element_type=F32)


def split(value):
    high = value.astype(BF16)
    return high, (value - high.astype(F32)).astype(BF16)


def iota(shape, axis):
    return lax.broadcasted_iota(jnp.int32, shape, axis)


def pieces(value):
    high = value.astype(BF16).astype(F32)
    rest = value - high
    middle = rest.astype(BF16).astype(F32)
    lane = iota(value.shape, 1)
    chosen = jnp.where(lane < GROUP, high, jnp.where(lane < 2 * GROUP, middle, rest - middle))
    return jnp.where(lane < 3 * GROUP, chosen, 0.0).astype(BF16)


def head_rows(spread, heads):
    tile = (iota((heads, LANES), 1) % GROUP == iota((heads, LANES), 0)).astype(F32)
    return jnp.dot(jnp.broadcast_to(spread, (8, heads)), tile, precision=HIGHEST, preferred_element_type=F32)[0:1]


def count_starts(lengths, position):
    start = jnp.int32(0)
    total = (start <= position).astype(jnp.int32)
    for k in range(1, lengths.shape[0]):
        start = start + lengths[k - 1]
        total = total + (start <= position).astype(jnp.int32)
    return total


def segments(lengths, offset, block):
    base = offset[0] + block * BLOCK
    column = count_starts(lengths, base + iota((BLOCK, 1), 0))
    row = count_starts(lengths, base + iota((1, BLOCK), 1))
    return column, row, count_starts(lengths, base - 1), count_starts(lengths, base + BLOCK - 1)


def prepare_kernel(lengths, offset, raw, bias, alog, x, b, oh, e, total, ends, decs, prefix, step, cum, sig, rows, state, run):
    block = pl.program_id(0)
    heads = raw.shape[1]

    @pl.when(block == 0)
    def _():
        state[...] = jnp.zeros_like(state)
        run[...] = jnp.ones_like(run)

    segment, _, prior, last = segments(lengths, offset, block)
    value = raw[...] + bias[...]
    small = jnp.exp(-jnp.abs(value))
    ratio = small / (2.0 + small)
    square = ratio * ratio
    series = jnp.full_like(square, 1.0 / 19.0)
    for odd in (17, 15, 13, 11, 9, 7, 5, 3, 1):
        series = series * square + 1.0 / odd
    soft = jnp.maximum(value, 0.0) + 2.0 * ratio * series
    inverse = 1.0 / (1.0 + small)
    sigma = jnp.where(value >= 0.0, inverse, small * inverse)
    tile = (iota((heads, LANES), 1) % GROUP == iota((heads, LANES), 0)).astype(F32)
    spread = partial(jnp.dot, precision=HIGHEST, preferred_element_type=F32)
    steps = spread(soft, tile)
    rate = steps * -jnp.exp(head_rows(alog[...], heads))
    lower = (iota((BLOCK, BLOCK), 0) >= iota((BLOCK, BLOCK), 1)).astype(F32)
    cumul = spread(lower, rate)
    step[...] = steps
    cum[...] = cumul
    sig[...] = spread(sigma, tile)
    rows[0] = cumul.T[:GROUP]
    rows[1] = steps.T[:GROUP]
    closing = cumul[BLOCK - 1 : BLOCK, :]
    weight = jnp.exp(closing - cumul) * (segment == last).astype(F32) * steps
    decay = jnp.exp(closing) * (last == prior).astype(F32)
    weights = pieces(weight)
    decays = pieces(jnp.broadcast_to(decay, (8, LANES)))
    width = x.shape[1]
    chunk = e.shape[2]
    for at in range(0, width, COLS):
        col = slice(at, at + COLS)
        high, low = split(x[:, col].astype(F32) * mm(weights, oh[:, col]))
        dec = mm(decays, oh[:, col])[0:1]
        fresh = dec * state[:, col] + (mm_tn(b[...], high) + mm_tn(b[...], low))
        state[:, col] = fresh
        ends[0, :, col] = fresh
        decs[0, :, col] = dec
        product = run[:, col] * dec
        run[:, col] = product
        prefix[0, :, col] = product

    @pl.when(block == pl.num_programs(0) - 1)
    def _():
        for c in range(e.shape[0]):
            e[c] = state[:, c * chunk : (c + 1) * chunk]
            total[c] = run[:, c * chunk : (c + 1) * chunk]


def diagonal_kernel(lengths, offset, cum, rows, x, b, c, out):
    block = pl.program_id(0)
    seg_column, seg_row, _, _ = segments(lengths, offset, block)
    mask = (seg_column == seg_row) & (iota((BLOCK, BLOCK), 0) > iota((BLOCK, BLOCK), 1))
    scores = jnp.where(mask, mm_nt(c[...], b[...]), 0.0)
    left = iota((BLOCK, LANES), 1) < HEADDIM
    for pair in range(x.shape[1] // LANES):
        col = slice(pair * LANES, (pair + 1) * LANES)
        parts = []
        for h in (2 * pair, 2 * pair + 1):
            gap = cum[:, h : h + 1] - rows[0, h : h + 1, :]
            parts.append(split(jnp.exp(jnp.minimum(gap, 0.0)) * scores * rows[1, h : h + 1, :]))
        pair_x = x[:, col]
        zero = jnp.zeros_like(pair_x)
        both = jnp.concatenate([jnp.where(left, pair_x, zero), jnp.where(left, zero, pair_x)], axis=0)
        high = jnp.concatenate([parts[0][0], parts[1][0]], axis=1)
        low = jnp.concatenate([parts[0][1], parts[1][1]], axis=1)
        out[:, col] = mm(high, both) + mm(low, both)


def output_kernel(lengths, offset, sin, ends, prefix, cum, step, x, z, g, b, c, diag, dskip, gain, oh, yp, stats, full, state):
    block = pl.program_id(0)

    @pl.when(block == 0)
    def _():
        state[...] = sin[...]

    segment, _, prior, _ = segments(lengths, offset, block)
    inflow = pieces(jnp.exp(cum[...]) * (segment == prior).astype(F32))
    own = jnp.sum(b[...].astype(F32) * c[...].astype(F32), axis=1, keepdims=True)
    coefficient = pieces(head_rows(dskip[...], dskip.shape[1]) + step[...] * own)
    square = jnp.zeros((BLOCK, COLS), F32)
    cross = jnp.zeros((BLOCK, COLS), F32)
    for at in range(0, x.shape[1], COLS):
        col = slice(at, at + COLS)
        high, low = split(state[:, col])
        carried = mm(c[...], high) + mm(c[...], low)
        partial_out = mm(inflow, oh[:, col]) * carried + diag[:, col]
        yp[:, col] = partial_out
        y = partial_out + mm(coefficient, oh[:, col]) * x[:, col].astype(F32)
        zf = z[:, col].astype(F32)
        gated = y * (zf / (1.0 + jnp.exp(-zf)))
        square = square + gated * gated
        cross = cross + g[:, col].astype(F32) * gain[:, col] * gated
        after = ends[0, :, col] + prefix[0, :, col] * sin[:, col]
        full[0, :, col] = after
        state[:, col] = after
    lane = iota((BLOCK, LANES), 1)
    sums = jnp.where(lane == 0, jnp.sum(square, axis=1, keepdims=True), 0.0)
    stats[...] = sums + jnp.where(lane == 1, jnp.sum(cross, axis=1, keepdims=True), 0.0)


def norm_kernel(lengths, offset, mine, other, cum, step, x, z, g, b, c, yp, dskip, gain, oh, decs, normed, zgrad, dyh, dyl, rho1, rho3, gpart, starts, own_grad, state, *, total_width):
    turn = pl.program_id(0)
    block = pl.num_programs(0) - 1 - turn

    @pl.when(turn == 0)
    def _():
        state[...] = jnp.zeros_like(state)
        gpart[...] = jnp.zeros_like(gpart)

    segment, _, prior, _ = segments(lengths, offset, block)
    inflow = pieces(jnp.exp(cum[...]) * (segment == prior).astype(F32))
    own = jnp.sum(b[...].astype(F32) * c[...].astype(F32), axis=1, keepdims=True)
    coefficient = pieces(head_rows(dskip[...], dskip.shape[1]) + step[...] * own)
    both = mine[...] + other[...]
    mean = both[:, 0:1] / total_width + EPSILON
    scale = lax.rsqrt(mean)
    scale = scale * (1.5 - 0.5 * mean * scale * scale)
    factor = scale * scale * scale * (both[:, 1:2] / total_width)
    first = jnp.zeros((BLOCK, LANES), F32)
    third = jnp.zeros((BLOCK, LANES), F32)
    for at in range(0, x.shape[1], COLS):
        col = slice(at, at + COLS)
        xf = x[:, col].astype(F32)
        partial_out = yp[:, col]
        y = partial_out + mm(coefficient, oh[:, col]) * xf
        zf = z[:, col].astype(F32)
        sigma = 1.0 / (1.0 + jnp.exp(-zf))
        gate = zf * sigma
        gated = y * gate
        scaled = gated * scale
        gf = g[:, col].astype(F32)
        normed[:, col] = (scaled * gain[:, col]).astype(BF16)
        gpart[:, col] += jnp.sum(gf * scaled, axis=0, keepdims=True)
        grad = gf * gain[:, col] * scale - gated * factor
        zgrad[:, col] = (grad * y * (sigma + gate * (1.0 - sigma))).astype(BF16)
        dy = grad * gate
        high, low = split(dy)
        dyh[:, col] = high
        dyl[:, col] = low
        high, low = split(dy * partial_out)
        first = first + (mm_nt(high, oh[:, col]) + mm_nt(low, oh[:, col]))
        high, low = split(dy * xf)
        third = third + (mm_nt(high, oh[:, col]) + mm_nt(low, oh[:, col]))
        high, low = split(dy * mm(inflow, oh[:, col]))
        back = decs[0, :, col] * state[:, col] + (mm_tn(c[...], high) + mm_tn(c[...], low))
        state[:, col] = back
        starts[0, :, col] = back
    rho1[...] = first
    rho3[...] = third

    @pl.when(turn == pl.num_programs(0) - 1)
    def _():
        chunk = own_grad.shape[2]
        for k in range(own_grad.shape[0]):
            own_grad[k] = state[:, k * chunk : (k + 1) * chunk]


def diagonal_back_kernel(lengths, offset, cum, rows, step, x, b, c, dyh, dyl, rho3, sin, full, oh, du, db, dc):
    block = pl.program_id(0)
    seg_column, seg_row, prior, _ = segments(lengths, offset, block)
    mask = (seg_column == seg_row) & (iota((BLOCK, BLOCK), 1) > iota((BLOCK, BLOCK), 0))
    scores = mm_nt(b[...], c[...])
    left = iota((BLOCK, LANES), 1) < HEADDIM
    score_grad = jnp.zeros((BLOCK, BLOCK), F32)
    carried_c = jnp.zeros((BLOCK, STATE), F32)
    inflow = pieces(jnp.exp(cum[...]) * (seg_column == prior).astype(F32))
    for pair in range(x.shape[1] // LANES):
        col = slice(pair * LANES, (pair + 1) * LANES)
        pair_x, high_dy, low_dy = x[:, col], dyh[:, col], dyl[:, col]
        zero = jnp.zeros_like(pair_x)
        x0, x1 = jnp.where(left, pair_x, zero), jnp.where(left, zero, pair_x)
        lhs = jnp.concatenate([jnp.concatenate([x0, x0], axis=1), jnp.concatenate([x1, x1], axis=1)], axis=0)
        products = mm_nt(lhs, jnp.concatenate([high_dy, low_dy], axis=1))
        parts = []
        for e in (0, 1):
            h = 2 * pair + e
            gap = rows[0, h : h + 1, :] - cum[:, h : h + 1]
            decay = jnp.where(mask, jnp.exp(jnp.minimum(gap, 0.0)), 0.0)
            score_grad = score_grad + decay * products[e * BLOCK : (e + 1) * BLOCK] * step[:, h : h + 1]
            parts.append(split(decay * scores))
        high = jnp.concatenate([parts[0][0], parts[1][0]], axis=1)
        low = jnp.concatenate([parts[0][1], parts[1][1]], axis=1)
        both_high = jnp.concatenate([jnp.where(left, high_dy, zero), jnp.where(left, zero, high_dy)], axis=0)
        both_low = jnp.concatenate([jnp.where(left, low_dy, zero), jnp.where(left, zero, low_dy)], axis=0)
        du[:, col] = mm(high, both_high) + (mm(low, both_high) + mm(high, both_low))
    for at in range(0, x.shape[1], COLS):
        col = slice(at, at + COLS)
        dy = dyh[:, col].astype(F32) + dyl[:, col].astype(F32)
        high, low = split(dy * mm(inflow, oh[:, col]))
        entering = jnp.where(block == 0, sin[:, col], full[0, :, col])
        s_high, s_low = split(entering)
        carried_c = carried_c + (mm_nt(high, s_high) + (mm_nt(low, s_high) + mm_nt(high, s_low)))
    lane = iota((BLOCK, LANES), 1)
    own = jnp.sum(jnp.where(lane < GROUP, rho3[...] * step[...], 0.0), axis=1, keepdims=True)
    high, low = split(score_grad)
    db[...] = mm(high, c[...]) + mm(low, c[...]) + own * c[...].astype(F32)
    dc[...] = carried_c + (mm_tn(high, b[...]) + mm_tn(low, b[...])) + own * b[...].astype(F32)


def input_kernel(lengths, offset, sout, starts, decs, full, cum, step, sig, x, b, c, dyh, dyl, diag, rho1, rho3, dskip, alog, oh, dbd, xgrad, db, draw, sums, state, run):
    turn = pl.program_id(0)
    block = pl.num_programs(0) - 1 - turn

    @pl.when(turn == 0)
    def _():
        state[...] = sout[...]
        run[...] = jnp.ones_like(run)
        sums[...] = jnp.zeros_like(sums)

    segment, _, _, last = segments(lengths, offset, block)
    steps = step[...]
    closing = cum[BLOCK - 1 : BLOCK, :]
    tail = pieces(jnp.exp(closing - cum[...]) * (segment == last).astype(F32))
    own = jnp.sum(b[...].astype(F32) * c[...].astype(F32), axis=1, keepdims=True)
    coefficient = pieces(head_rows(dskip[...], dskip.shape[1]) + steps * own)
    step_pieces = pieces(steps)
    second = jnp.zeros((BLOCK, LANES), F32)
    carried_b = jnp.zeros((BLOCK, STATE), F32)
    inner = jnp.zeros((8, LANES), F32)
    for at in range(0, x.shape[1], COLS):
        col = slice(at, at + COLS)
        leaving = state[:, col]
        s_high, s_low = split(leaving)
        weight = mm(tail, oh[:, col])
        step_wide = mm(step_pieces, oh[:, col])
        xf = x[:, col].astype(F32)
        du = diag[:, col] + weight * (mm(b[...], s_high) + mm(b[...], s_low))
        dy = dyh[:, col].astype(F32) + dyl[:, col].astype(F32)
        xgrad[:, col] = (step_wide * du + mm(coefficient, oh[:, col]) * dy).astype(BF16)
        high, low = split(xf * du)
        second = second + (mm_nt(high, oh[:, col]) + mm_nt(low, oh[:, col]))
        high, low = split(xf * (weight * step_wide))
        carried_b = carried_b + (mm_nt(high, s_high) + (mm_nt(low, s_high) + mm_nt(high, s_low)))
        overlap = jnp.sum((full[0, :, col] * leaving).reshape(STATE // 8, 8, COLS), axis=0)
        high, low = split(overlap)
        inner = inner + (mm_nt(high, oh[:, col]) + mm_nt(low, oh[:, col]))
        product = run[:, col] * decs[0, :, col]
        run[:, col] = product
        state[:, col] = starts[0, :, col] + product * sout[:, col]
    db[...] = dbd[...] + carried_b
    upper = (iota((BLOCK, BLOCK), 1) >= iota((BLOCK, BLOCK), 0)).astype(F32)
    rate_grad = jnp.dot(upper, rho1[...] - steps * second, precision=HIGHEST, preferred_element_type=F32)
    rate_grad = rate_grad + jnp.sum(inner, axis=0, keepdims=True)
    speed = jnp.exp(head_rows(alog[...], alog.shape[1]))
    raw_grad = (second + own * rho3[...] - speed * rate_grad) * sig[...]
    draw[...] = raw_grad[:, : draw.shape[1]]
    row = iota((8, LANES), 0)
    bias_row = jnp.where(row == 0, jnp.sum(raw_grad, axis=0, keepdims=True), 0.0)
    alog_row = jnp.where(row == 1, jnp.sum(rate_grad * steps * -speed, axis=0, keepdims=True), 0.0)
    skip_row = jnp.where(row == 2, jnp.sum(rho3[...], axis=0, keepdims=True), 0.0)
    sums[...] += bias_row + alog_row + skip_row


def relay(own, total, axis, forward):
    count = lax.axis_size(axis)
    index = lax.axis_index(axis)
    rank = index if forward else count - 1 - index
    pairs = [(i, i + 1) if forward else (i + 1, i) for i in range(count - 1)]
    chunks = own.shape[0]
    arriving = jnp.zeros(own.shape[1:], F32)
    received = []
    for turn in range(chunks + count - 2):
        at = jnp.clip(turn - rank, 0, chunks - 1)
        message = lax.dynamic_index_in_dim(own, at, 0, False) + lax.dynamic_index_in_dim(total, at, 0, False) * arriving
        arriving = lax.ppermute(message, axis, pairs)
        received.append(arriving)
    stacked = jnp.stack(received)
    picked = [
        lax.dynamic_index_in_dim(stacked, jnp.clip(k + rank - 1, 0, len(received) - 1), 0, False)
        for k in range(chunks)
    ]
    return jnp.concatenate(picked, axis=1)


def shards(x, z, b, c, raw, lengths, bias, alog, dskip, gain, grad):
    _, tokens, width = x.shape
    heads = width // HEADDIM
    blocks = tokens // BLOCK
    chunk = width // CHUNKS
    x, z, grad = (v.reshape(tokens, width) for v in (x, z, grad))
    b, c = b.reshape(tokens, STATE), c.reshape(tokens, STATE)
    raw = raw.reshape(tokens, heads)
    lengths = lengths.reshape(-1)
    bias, alog, dskip = (v.reshape(1, heads) for v in (bias, alog, dskip))
    gain = gain.reshape(1, width)
    offset = jnp.reshape(lax.axis_index("seq") * tokens, (1,)).astype(jnp.int32)
    lane = jnp.arange(LANES)[:, None]
    oh = ((lane % GROUP == jnp.arange(width)[None, :] // HEADDIM) & (lane < 3 * GROUP)).astype(BF16)

    def call(kernel, reverse, ins, outs, scratch, name):
        place = (lambda i: blocks - 1 - i) if reverse else (lambda i: i)

        def spec(kind, shape):
            if kind == "smem":
                return pl.BlockSpec(memory_space=pltpu.SMEM)
            if kind == "tok":
                return pl.BlockSpec((BLOCK, shape[1]), lambda i: (place(i), 0))
            if kind == "blk":
                return pl.BlockSpec((1,) + tuple(shape[1:]), lambda i: (place(i), 0, 0))
            if kind == "prev":
                return pl.BlockSpec((1,) + tuple(shape[1:]), lambda i: (jnp.maximum(place(i) - 1, 0), 0, 0))
            if kind == "row":
                return pl.BlockSpec((2, GROUP, BLOCK), lambda i: (0, 0, place(i)))
            return pl.BlockSpec(tuple(shape), lambda i: (0,) * len(shape))

        return pl.pallas_call(
            kernel,
            grid=(blocks,),
            in_specs=[spec(kind, value.shape) for kind, value in ins],
            out_specs=[spec(kind, shape) for kind, shape, _ in outs],
            out_shape=[jax.ShapeDtypeStruct(shape, dtype) for _, shape, dtype in outs],
            scratch_shapes=[pltpu.VMEM(shape, F32) for shape in scratch],
            compiler_params=pltpu.CompilerParams(
                dimension_semantics=("arbitrary",), vmem_limit_bytes=VMEM_LIMIT
            ),
            name=name,
        )(*[value for _, value in ins])

    wide = (tokens, width)
    narrow = (tokens, LANES)
    states = (blocks, STATE, width)
    line = (blocks, 1, width)
    where = [("smem", lengths), ("smem", offset)]
    e, total, ends, decs, prefix, step, cum, sig, rows = call(
        prepare_kernel, False,
        where + [("tok", raw), ("all", bias), ("all", alog), ("tok", x), ("tok", b), ("all", oh)],
        [("all", (CHUNKS, STATE, chunk), F32), ("all", (CHUNKS, 1, chunk), F32), ("blk", states, F32),
         ("blk", line, F32), ("blk", line, F32), ("tok", narrow, F32), ("tok", narrow, F32), ("tok", narrow, F32),
         ("row", (2, GROUP, tokens), F32)],
        [(STATE, width), (1, width)], "prepare",
    )
    sin = relay(e, total, "seq", True)
    (diag,) = call(
        diagonal_kernel, False,
        where + [("tok", cum), ("row", rows), ("tok", x), ("tok", b), ("tok", c)],
        [("tok", wide, F32)], [], "diagonal",
    )
    yp, stats, full = call(
        output_kernel, False,
        where + [("all", sin), ("blk", ends), ("blk", prefix), ("tok", cum), ("tok", step), ("tok", x), ("tok", z), ("tok", grad),
                 ("tok", b), ("tok", c), ("tok", diag), ("all", dskip), ("all", gain), ("all", oh)],
        [("tok", wide, F32), ("tok", narrow, F32), ("blk", states, F32)],
        [(STATE, width)], "output",
    )
    both = lax.axis_size("head")
    if both == 2:
        other = lax.ppermute(stats, "head", [(0, 1), (1, 0)])
    else:
        other = lax.psum(stats, "head") - stats
    normed, zgrad, dyh, dyl, rho1, rho3, gpart, starts, own_grad = call(
        partial(norm_kernel, total_width=float(width * both)), True,
        where + [("tok", stats), ("tok", other), ("tok", cum), ("tok", step), ("tok", x), ("tok", z), ("tok", grad), ("tok", b),
                 ("tok", c), ("tok", yp), ("all", dskip), ("all", gain), ("all", oh), ("blk", decs)],
        [("tok", wide, BF16), ("tok", wide, BF16), ("tok", wide, BF16), ("tok", wide, BF16), ("tok", narrow, F32),
         ("tok", narrow, F32), ("all", (1, width), F32), ("blk", states, F32), ("all", (CHUNKS, STATE, chunk), F32)],
        [(STATE, width)], "norm",
    )
    sout = relay(own_grad, total, "seq", False)
    du, dbd, dc = call(
        diagonal_back_kernel, False,
        where + [("tok", cum), ("row", rows), ("tok", step), ("tok", x), ("tok", b), ("tok", c), ("tok", dyh), ("tok", dyl),
                 ("tok", rho3), ("all", sin), ("prev", full), ("all", oh)],
        [("tok", wide, F32), ("tok", narrow, F32), ("tok", narrow, F32)], [], "diagonal_back",
    )
    xgrad, db, draw, sums = call(
        input_kernel, True,
        where + [("all", sout), ("blk", starts), ("blk", decs), ("blk", full), ("tok", cum), ("tok", step), ("tok", sig), ("tok", x),
                 ("tok", b), ("tok", c), ("tok", dyh), ("tok", dyl), ("tok", du), ("tok", rho1), ("tok", rho3), ("all", dskip),
                 ("all", alog), ("all", oh), ("tok", dbd)],
        [("tok", wide, BF16), ("tok", narrow, F32), ("tok", (tokens, heads), F32), ("all", (8, LANES), F32)],
        [(STATE, width), (1, width)], "input",
    )
    db, dc = lax.psum((db, dc), "head")
    sums, gpart = lax.psum((sums, gpart), ("seq", "batch"))
    return (
        normed[None],
        xgrad[None],
        zgrad[None],
        db[None],
        dc[None],
        draw[None],
        sums[0, :heads],
        sums[1, :heads],
        sums[2, :heads],
        gpart[0],
    )


def solution(mesh):
    wide = P(("groups", "batch"), "seq", "head")
    shared = P(("groups", "batch"), "seq", None)
    part = P(("groups", "head"))
    head = P("head")
    return jax.shard_map(
        shards,
        mesh=mesh,
        in_specs=(wide, wide, shared, shared, wide, P(("groups", "batch"), None), head, head, head, head, wide),
        out_specs=(wide, wide, wide, shared, shared, wide, part, part, part, part),
        check_vma=False,
    )
```

time: 647 us -> 211 us (0.33); the launches traced: 638 us -> 210 us
  local copies, waits for them, and re-layouts: 178 us -> 8.82 us
  other arithmetic: 153 us -> 8.09 us
  matrix products: 135 us -> 0 us
  Pallas kernels: 0 us -> 63.2 us
  waiting for transfers between devices: 108 us -> 52.5 us
  starting transfers between devices: 17.7 us -> 28.4 us
  blocking collectives: 25.3 us -> 35 us
    dot_general x34 -> x0, matrix products: 135 us -> none  [the longest x6 60.8 us: block_step(): jnp.einsum('hij,jhp->ihp', mixing, rescaled_quantity, precision=highest)]
    pallas_call x0 -> x6, Pallas kernels: none -> 63.2 us  [call(): pl.pallas_call(kernel, grid=(blocks,), in_specs=[spec(kind, value.shape)...]
    ppermute x6 -> x11, waiting for transfers between devices: 108 us -> 52.5 us  [the longest x10 50.7 us: relay(): arriving = lax.ppermute(message, axis, pairs)]
    another operation x106 -> x2, local copies, waits for them, and re-layouts: 45 us -> 0.04 us  [relay(): stacked = jnp.stack(received)]
    reduce_sum x22 -> x0, other arithmetic: 38.6 us -> none  [the longest x4 10.1 us: inter_step(): jnp.einsum('in,hpn->ihp', c_block, state, precision=highest)]
    dynamic_update_slice x18 -> x0, other arithmetic: 32.5 us -> none  [forward_one_row(): lax.scan(stepper, start, (x_rows, raw_rows, b_rows, c_rows, segment_rows,...]
    dynamic_slice x32 -> x0, local copies, waits for them, and re-layouts: 32.5 us -> none  [the longest x28 28.5 us: inter_one_row(): lax.scan(stepper, state, (raw_rows, c_rows, segment_rows, previous_rows))]
    dynamic_update_slice x44 -> x0, local copies, waits for them, and re-layouts: 26.5 us -> none  [forward_one_row(): lax.scan(stepper, start, (x_rows, raw_rows, b_rows, c_rows, segment_rows,...]
  transfers between devices with their start and end apart: 7 -> 12, of which waited for: 6 -> 9; matrix products, arithmetic and copies ran while one was open for 2% -> 1% of each run, Pallas kernels for 0% -> 9%
where the time goes in v1:
time: 211 us; the launch traced here: 210 us
  Pallas kernels  63.2 us (30%)
  waiting for transfers between devices  52.5 us (25%)
  blocking collectives  35 us (17%)
  starting transfers between devices  28.4 us (13%)
  between operations  14.4 us (7%)
  local copies, waits for them, and re-layouts  8.82 us (4%)
  other arithmetic  8.09 us (4%)
    pallas_call x6, Pallas kernels, call(): pl.pallas_call(kernel, grid=(blocks,), in_specs=[spec(kind, value.shape)...  63.2 us
    ppermute x10, waiting for transfers between devices, relay(): arriving = lax.ppermute(message, axis, pairs)  50.7 us
    psum x1, blocking collectives, shards(): sums, gpart = lax.psum((sums, gpart), ('seq', 'batch'))  35 us
    ppermute x10, starting transfers between devices, relay(): arriving = lax.ppermute(message, axis, pairs)  28.3 us
    unnamed x22, local copies, waits for them, and re-layouts  7.54 us
    add x10, other arithmetic, relay(): lax.dynamic_index_in_dim(own, at, 0, False)  4.25 us
  transfers between devices with their start and end apart: 12, of which 9 were waited for; matrix products, arithmetic and copies ran while one was open for 1% of the time, Pallas kernels for 9%

profile of v1, /device:TPU:0, one launch (start us, length us, event | category | flops | bytes accessed | tf_op | source)
XLA Modules:
  0.0 210.4 jit_solution(10955814539040533869)
XLA Ops:
  7.2 0.0 all-reduce.4.cloned.1.call-start
  7.3 1.6 copy.21
  8.9 0.9 and_convert_fusion.oh
  9.8 8.6 %prepare.1 = (f32[3,128,512]{2,1,0:T(8,128)}, f32[3,1,512]{2,1,0:T(1,128)}, f32[4,128,1536]{2,1,0:T(8,128)}, f32[4,1,1536]{2,1,0:T(1,128)}, f32[4,1,1536]{2,1,0:...) custom-call(s32[2]{0:T(128)} %bitcast.110, s32[1]{0:T(128)} %bitcast.1.offset, ...), custom_call_target="tpu_custom_call" | custom-call | tf_op jit(solution)/shard_map/prepare/pallas_call | solution.py:389
  18.4 0.0 copy-start
  18.4 0.0 copy-start.3
  18.5 0.9 constant_dynamic-slice_fusion
  19.4 1.0 bitcast_add_fusion.9
  20.4 4.9 %collective-permute-start = (f32[128,512]{1,0:T(8,128)S(1)}, f32[128,512]{1,0:T(8,128)S(1)}, u32[]{:S(2)}, u32[]{:S(2)}) collective-permute-start(f32[128,512]{1,0:T(8,128)S(1)} %bitcast_add_fusion.9), channel_id=1, source_target_pairs={{0,4},{4,8},{8,12},{1,5},{5,9},{9,13},{2,6},{6,10},{10,14},{3,7},{... | collective-permute-start | bytes 786440 | tf_op jit(solution)/shard_map/ppermute | solution.py:348
  25.3 5.5 %collective-permute-done = f32[128,512]{1,0:T(8,128)S(1)} collective-permute-done((f32[128,512]{1,0:T(8,128)S(1)}, f32[128,512]{1,0:T(8,128)S(1)}, u32[]{:S(2)}, u32[]{:S(2)}) %collective-permute-start) | collective-permute-done | bytes 262176 | tf_op jit(solution)/shard_map/ppermute | solution.py:348
  30.9 1.0 bitcast_add_fusion.8
  31.8 4.4 %collective-permute-start.1 = (f32[128,512]{1,0:T(8,128)S(1)}, f32[128,512]{1,0:T(8,128)S(1)}, u32[]{:S(2)}, u32[]{:S(2)}) collective-permute-start(f32[128,512]{1,0:T(8,128)S(1)} %bitcast_add_fusion.8), channel_id=1, source_target_pairs={{0,4},{4,8},{8,12},{1,5},{5,9},{9,13},{2,6},{6,10},{10,14},{3,7},{... | collective-permute-start | bytes 786440 | tf_op jit(solution)/shard_map/ppermute | solution.py:348
  36.3 4.7 %collective-permute-done.1 = f32[128,512]{1,0:T(8,128)S(1)} collective-permute-done((f32[128,512]{1,0:T(8,128)S(1)}, f32[128,512]{1,0:T(8,128)S(1)}, u32[]{:S(2)}, u32[]{:S(2)}) %collective-permute-start.1) | collective-permute-done | bytes 262176 | tf_op jit(solution)/shard_map/ppermute | solution.py:348
  40.9 0.0 copy-done
  41.0 4.4 %collective-permute-start.2 = (f32[128,512]{1,0:T(8,128)S(1)}, f32[128,512]{1,0:T(8,128)S(1)}, u32[]{:S(2)}, u32[]{:S(2)}) collective-permute-start(f32[128,512]{1,0:T(8,128)S(1)} %bitcast_add_fusion.7), channel_id=1, source_target_pairs={{0,4},{4,8},{8,12},{1,5},{5,9},{9,13},{2,6},{6,10},{10,14},{3,7},{... | collective-permute-start | bytes 786440 | tf_op jit(solution)/shard_map/ppermute | solution.py:348
  45.4 0.0 copy-done.3
  45.4 0.6 reshape.138.gain
  46.0 6.1 %diagonal.1.diag = f32[512,1536]{1,0:T(8,128)} custom-call(s32[2]{0:T(128)} %bitcast.111, s32[1]{0:T(128)} %bitcast.1.offset, f32[512,128]{1,0:T(8,128)} %get-tuple-element.42.cum, f32[2,32,512]{2,1,0:T(8,128)} %get-tuple-element.44.rows, bf16[512,1536]{1,0:T(8,128)(2,1)} %bitcast.86, bf16[512,128]{1,0:T(8,128)(2,1)} %bitcast.96, bf16[512,128]{1,0:T(8,128)(2,1)} %bitcast.101), custom_call_target="tpu_custom_call" | custom-call | tf_op jit(solution)/shard_map/diagonal/pallas_call | solution.py:389
  52.1 0.0 collective-permute-done.2
  52.1 3.5 %collective-permute-start.3 = (f32[128,512]{1,0:T(8,128)S(1)}, f32[128,512]{1,0:T(8,128)S(1)}, u32[]{:S(2)}, u32[]{:S(2)}) collective-permute-start(f32[128,512]{1,0:T(8,128)S(1)} %bitcast_add_fusion.6), channel_id=1, source_target_pairs={{0,4},{4,8},{8,12},{1,5},{5,9},{9,13},{2,6},{6,10},{10,14},{3,7},{... | collective-permute-start | bytes 786440 | tf_op jit(solution)/shard_map/ppermute | solution.py:348
  55.7 3.8 %collective-permute-done.3 = f32[128,512]{1,0:T(8,128)S(1)} collective-permute-done((f32[128,512]{1,0:T(8,128)S(1)}, f32[128,512]{1,0:T(8,128)S(1)}, u32[]{:S(2)}, u32[]{:S(2)}) %collective-permute-start.3) | collective-permute-done | bytes 262176 | tf_op jit(solution)/shard_map/ppermute | solution.py:348
  59.5 4.4 %collective-permute-start.4 = (f32[128,512]{1,0:T(8,128)S(1)}, f32[128,512]{1,0:T(8,128)S(1)}, u32[]{:S(2)}, u32[]{:S(2)}) collective-permute-start(f32[128,512]{1,0:T(8,128)S(1)} %bitcast_add_fusion.5), channel_id=1, source_target_pairs={{0,4},{4,8},{8,12},{1,5},{5,9},{9,13},{2,6},{6,10},{10,14},{3,7},{... | collective-permute-start | bytes 786440 | tf_op jit(solution)/shard_map/ppermute | solution.py:348
  64.0 3.8 %collective-permute-done.4 = f32[128,512]{1,0:T(8,128)S(1)} collective-permute-done((f32[128,512]{1,0:T(8,128)S(1)}, f32[128,512]{1,0:T(8,128)S(1)}, u32[]{:S(2)}, u32[]{:S(2)}) %collective-permute-start.4) | collective-permute-done | bytes 262176 | tf_op jit(solution)/shard_map/ppermute | solution.py:348
  67.8 0.1 dynamic-slice_bitcast_fusion.5
  67.9 0.9 pad_maximum_fusion.sin
  68.8 9.3 %output.1 = (f32[512,1536]{1,0:T(8,128)}, f32[512,128]{1,0:T(8,128)}, f32[4,128,1536]{2,1,0:T(8,128)}) custom-call(s32[2]{0:T(128)} %bitcast.112, s32[1]{0:T(128)} %bitcast.1.offset, f32[128,1536]{1,0:T(8,128)} %pad_maximum_fusion.sin, f32[4,128,1536]{2,1,0:T(8,128)} %get-tuple-element.40.ends, f32[4,1,1536]{2,1,0:T(1,128)} %get-tuple-element.41.prefix, ...), custom_call_target="tpu_custom_call" | custom-call | tf_op jit(solution)/shard_map/output/pallas_call | solution.py:389
  78.1 0.1 collective-permute-start.5
  78.2 1.7 collective-permute-done.5.other
  79.9 0.0 copy-start.2
  79.9 0.7 copy-done.2
  80.6 14.3 %norm.1 = (bf16[512,1536]{1,0:T(8,128)(2,1)}, bf16[512,1536]{1,0:T(8,128)(2,1)}, bf16[512,1536]{1,0:T(8,128)(2,1)}, bf16[512,1536]{1,0:T(8,128)(2,1)}, f32[512,1...) custom-call(s32[2]{0:T(128)} %bitcast.113, ...), custom_call_target="tpu_custom_call" | custom-call | tf_op jit(solution)/shard_map/norm/pallas_call | solution.py:389
  95.0 0.0 copy-start.1
  95.0 1.0 bitcast_add_fusion.4
  96.0 1.3 collective-permute-start.6
  97.3 9.7 %collective-permute-done.6 = f32[128,512]{1,0:T(8,128)S(1)} collective-permute-done((f32[128,512]{1,0:T(8,128)S(1)}, f32[128,512]{1,0:T(8,128)S(1)}, u32[]{:S(2)}, u32[]{:S(2)}) %collective-permute-start.6) | collective-permute-done | bytes 262176 | tf_op jit(solution)/shard_map/ppermute | solution.py:348
  107.0 1.0 bitcast_add_fusion.3
  108.0 1.3 collective-permute-start.7
  109.3 8.4 %collective-permute-done.7 = f32[128,512]{1,0:T(8,128)S(1)} collective-permute-done((f32[128,512]{1,0:T(8,128)S(1)}, f32[128,512]{1,0:T(8,128)S(1)}, u32[]{:S(2)}, u32[]{:S(2)}) %collective-permute-start.7) | collective-permute-done | bytes 262176 | tf_op jit(solution)/shard_map/ppermute | solution.py:348
  117.7 0.0 copy-done.1
  117.8 1.3 collective-permute-start.8
  119.1 12.7 %diagonal_back.1 = (f32[512,1536]{1,0:T(8,128)}, f32[512,128]{1,0:T(8,128)}, f32[512,128]{1,0:T(8,128)}) custom-call(s32[2]{0:T(128)} %bitcast.114, s32[1]{0:T(128)} %bitcast.1.offset, f32[512,128]{1,0:T(8,128)} %get-tuple-element.42.cum, f32[2,32,512]{2,1,0:T(8,128)} %get-tuple-element.44.rows, f32[512,128]{1,0:T(8,128)} %get-tuple-element.43.step, ...), custom_call_target="tpu_custom_call" | custom-call | tf_op jit(solution)/shard_map/diagonal_back/pallas_call | solution.py:389
  131.7 0.0 collective-permute-done.8
  131.8 1.3 collective-permute-start.9
  133.2 8.1 %collective-permute-done.9 = f32[128,512]{1,0:T(8,128)S(1)} collective-permute-done((f32[128,512]{1,0:T(8,128)S(1)}, f32[128,512]{1,0:T(8,128)S(1)}, u32[]{:S(2)}, u32[]{:S(2)}) %collective-permute-start.9) | collective-permute-done | bytes 262176 | tf_op jit(solution)/shard_map/ppermute | solution.py:348
  141.3 1.5 collective-permute-start.10
  142.8 6.7 %collective-permute-done.10 = f32[128,512]{1,0:T(8,128)S(1)} collective-permute-done((f32[128,512]{1,0:T(8,128)S(1)}, f32[128,512]{1,0:T(8,128)S(1)}, u32[]{:S(2)}, u32[]{:S(2)}) %collective-permute-start.10) | collective-permute-done | bytes 262176 | tf_op jit(solution)/shard_map/ppermute | solution.py:348
  149.6 0.1 dynamic-slice_bitcast_fusion.2
  149.7 1.0 pad_maximum_fusion.1.sout
  150.7 0.0 copy-start.4
  150.7 12.3 %input.1 = (bf16[512,1536]{1,0:T(8,128)(2,1)}, f32[512,128]{1,0:T(8,128)}, f32[512,24]{1,0:T(8,128)}, f32[8,128]{1,0:T(8,128)}) custom-call(s32[2]{0:T(128)} %bitcast.115, s32[1]{0:T(128)} %bitcast.1.offset, f32[128,1536]{1,0:T(8,128)} %pad_maximum_fusion.1.sout, f32[4,128,1536]{2,1,0:T(8,128)} %get-tuple-element.50.starts, ...), custom_call_target="tpu_custom_call" | custom-call | tf_op jit(solution)/shard_map/input/pallas_call | solution.py:389
  162.9 0.0 all-reduce.4.cloned.1.call-update
  163.0 0.0 copy-done.4
  163.0 1.7 copy.22
  164.7 35.0 %all-reduce = (f32[8,128]{1,0:T(8,128)S(1)}, f32[1536]{0:T(1024)}) all-reduce(f32[8,128]{1,0:T(8,128)} %get-tuple-element.64, f32[1536]{0:T(1024)S(1)} %reduce), channel_id=1, replica_groups=mesh['groups'=2,'seq'=4,'batch'=2,'head'=2] {'seq','batch'}, use_global_device_ids=true, to_apply=%region_2.3 | all-reduce | flops 2560 | bytes 20480 | tf_op jit(solution)/shard_map/psum | solution.py:457
  199.7 0.5 slice_bitcast_fusion
  200.2 0.0 all-reduce.4.cloned.1.call-done
  200.2 1.7 copy.33
  201.9 1.7 copy.34
  (20 shorter events, 0.5 us)
Async XLA Ops:
  7.2 193.1 %all-reduce.4.cloned.1.call-start = ((), (), s32[]{:S(2)}) async-start(), calls=%async_computation | async-start | bytes 1048576 | tf_op jit(solution)/shard_map/psum | solution.py:456
  18.4 22.5 %copy-start = (f32[3,128,512]{2,1,0:T(8,128)S(1)}, f32[3,128,512]{2,1,0:T(8,128)}, u32[]{:S(2)}) copy-start(f32[3,128,512]{2,1,0:T(8,128)} %get-tuple-element.38) | copy-start | bytes 2359300
  18.4 26.9 %copy-start.3 = (f32[1536]{0:T(1024)S(1)}, f32[1536]{0:T(1024)}, u32[]{:S(2)}) copy-start(f32[1536]{0:T(1024)} %param.20) | copy-start | bytes 18436
  20.4 10.5 %collective-permute-start = (f32[128,512]{1,0:T(8,128)S(1)}, f32[128,512]{1,0:T(8,128)S(1)}, u32[]{:S(2)}, u32[]{:S(2)}) collective-permute-start(f32[128,512]{1,0:T(8,128)S(1)} %bitcast_add_fusion.9), channel_id=1, source_target_pairs={{0,4},{4,8},{8,12},{1,5},{5,9},{9,13},{2,6},{6,10},{10,14},{3,7},{... | collective-permute-start | bytes 786440 | tf_op jit(solution)/shard_map/ppermute | solution.py:348
  31.8 9.1 %collective-permute-start.1 = (f32[128,512]{1,0:T(8,128)S(1)}, f32[128,512]{1,0:T(8,128)S(1)}, u32[]{:S(2)}, u32[]{:S(2)}) collective-permute-start(f32[128,512]{1,0:T(8,128)S(1)} %bitcast_add_fusion.8), channel_id=1, source_target_pairs={{0,4},{4,8},{8,12},{1,5},{5,9},{9,13},{2,6},{6,10},{10,14},{3,7},{... | collective-permute-start | bytes 786440 | tf_op jit(solution)/shard_map/ppermute | solution.py:348
  41.0 11.1 %collective-permute-start.2 = (f32[128,512]{1,0:T(8,128)S(1)}, f32[128,512]{1,0:T(8,128)S(1)}, u32[]{:S(2)}, u32[]{:S(2)}) collective-permute-start(f32[128,512]{1,0:T(8,128)S(1)} %bitcast_add_fusion.7), channel_id=1, source_target_pairs={{0,4},{4,8},{8,12},{1,5},{5,9},{9,13},{2,6},{6,10},{10,14},{3,7},{... | collective-permute-start | bytes 786440 | tf_op jit(solution)/shard_map/ppermute | solution.py:348
  52.1 7.3 %collective-permute-start.3 = (f32[128,512]{1,0:T(8,128)S(1)}, f32[128,512]{1,0:T(8,128)S(1)}, u32[]{:S(2)}, u32[]{:S(2)}) collective-permute-start(f32[128,512]{1,0:T(8,128)S(1)} %bitcast_add_fusion.6), channel_id=1, source_target_pairs={{0,4},{4,8},{8,12},{1,5},{5,9},{9,13},{2,6},{6,10},{10,14},{3,7},{... | collective-permute-start | bytes 786440 | tf_op jit(solution)/shard_map/ppermute | solution.py:348
  59.5 8.3 %collective-permute-start.4 = (f32[128,512]{1,0:T(8,128)S(1)}, f32[128,512]{1,0:T(8,128)S(1)}, u32[]{:S(2)}, u32[]{:S(2)}) collective-permute-start(f32[128,512]{1,0:T(8,128)S(1)} %bitcast_add_fusion.5), channel_id=1, source_target_pairs={{0,4},{4,8},{8,12},{1,5},{5,9},{9,13},{2,6},{6,10},{10,14},{3,7},{... | collective-permute-start | bytes 786440 | tf_op jit(solution)/shard_map/ppermute | solution.py:348
  78.1 1.8 collective-permute-start.5
  79.9 0.7 copy-start.2
  95.0 22.8 %copy-start.1 = (f32[3,128,512]{2,1,0:T(8,128)S(1)}, f32[3,128,512]{2,1,0:T(8,128)}, u32[]{:S(2)}) copy-start(f32[3,128,512]{2,1,0:T(8,128)} %get-tuple-element.49) | copy-start | bytes 2359300
  96.0 11.0 %collective-permute-start.6 = (f32[128,512]{1,0:T(8,128)S(1)}, f32[128,512]{1,0:T(8,128)S(1)}, u32[]{:S(2)}, u32[]{:S(2)}) collective-permute-start(f32[128,512]{1,0:T(8,128)S(1)} %bitcast_add_fusion.4), channel_id=1, source_target_pairs={{4,0},{8,4},{12,8},{5,1},{9,5},{13,9},{6,2},{10,6},{14,10},{7,3},{... | collective-permute-start | bytes 786440 | tf_op jit(solution)/shard_map/ppermute | solution.py:348
  108.0 9.7 %collective-permute-start.7 = (f32[128,512]{1,0:T(8,128)S(1)}, f32[128,512]{1,0:T(8,128)S(1)}, u32[]{:S(2)}, u32[]{:S(2)}) collective-permute-start(f32[128,512]{1,0:T(8,128)S(1)} %bitcast_add_fusion.3), channel_id=1, source_target_pairs={{4,0},{8,4},{12,8},{5,1},{9,5},{13,9},{6,2},{10,6},{14,10},{7,3},{... | collective-permute-start | bytes 786440 | tf_op jit(solution)/shard_map/ppermute | solution.py:348
  117.8 14.0 %collective-permute-start.8 = (f32[128,512]{1,0:T(8,128)S(1)}, f32[128,512]{1,0:T(8,128)S(1)}, u32[]{:S(2)}, u32[]{:S(2)}) collective-permute-start(f32[128,512]{1,0:T(8,128)S(1)} %bitcast_add_fusion.2), channel_id=1, source_target_pairs={{4,0},{8,4},{12,8},{5,1},{9,5},{13,9},{6,2},{10,6},{14,10},{7,3},{... | collective-permute-start | bytes 786440 | tf_op jit(solution)/shard_map/ppermute | solution.py:348
  131.8 9.5 %collective-permute-start.9 = (f32[128,512]{1,0:T(8,128)S(1)}, f32[128,512]{1,0:T(8,128)S(1)}, u32[]{:S(2)}, u32[]{:S(2)}) collective-permute-start(f32[128,512]{1,0:T(8,128)S(1)} %bitcast_add_fusion.1), channel_id=1, source_target_pairs={{4,0},{8,4},{12,8},{5,1},{9,5},{13,9},{6,2},{10,6},{14,10},{7,3},{... | collective-permute-start | bytes 786440 | tf_op jit(solution)/shard_map/ppermute | solution.py:348
  141.3 8.3 %collective-permute-start.10 = (f32[128,512]{1,0:T(8,128)S(1)}, f32[128,512]{1,0:T(8,128)S(1)}, u32[]{:S(2)}, u32[]{:S(2)}) collective-permute-start(f32[128,512]{1,0:T(8,128)S(1)} %bitcast_add_fusion), channel_id=1, source_target_pairs={{4,0},{8,4},{12,8},{5,1},{9,5},{13,9},{6,2},{10,6},{14,10},{7,3},{... | collective-permute-start | bytes 786440 | tf_op jit(solution)/shard_map/ppermute | solution.py:348
  150.7 12.3 %copy-start.4 = (f32[1,1536]{1,0:T(1,128)S(1)}, f32[1,1536]{1,0:T(1,128)}, u32[]{:S(2)}) copy-start(f32[1,1536]{1,0:T(1,128)} %get-tuple-element.65) | copy-start | bytes 18436
Sparse Core Ops, SparseCore 0:
  163.1 18.7 all-reduce.3

commit v2 on v1

--- a/solution.py
+++ b/solution.py
@@ -13,12 +13,14 @@
 LANES = 128
 GROUP = 32
 COLS = 256
-CHUNKS = 3
+CHUNKS = 4
+LAG = 2
+PARTS = 3
 EPSILON = 1e-05
 HIGHEST = lax.Precision.HIGHEST
 F32 = jnp.float32
 BF16 = jnp.bfloat16
-VMEM_LIMIT = 56 * 1024 * 1024
+VMEM_LIMIT = 60 * 1024 * 1024
 
 
 def mm(a, b):
@@ -74,7 +76,7 @@
 
 def prepare_kernel(lengths, offset, raw, bias, alog, x, b, oh, e, total, ends, decs, prefix, step, cum, sig, rows, state, run):
     block = pl.program_id(0)
-    heads = raw.shape[1]
+    heads = raw.shape[0]
 
     @pl.when(block == 0)
     def _():
@@ -93,16 +95,16 @@
     inverse = 1.0 / (1.0 + small)
     sigma = jnp.where(value >= 0.0, inverse, small * inverse)
     tile = (iota((heads, LANES), 1) % GROUP == iota((heads, LANES), 0)).astype(F32)
-    spread = partial(jnp.dot, precision=HIGHEST, preferred_element_type=F32)
+    spread = partial(lax.dot_general, dimension_numbers=(((0,), (0,)), ((), ())), precision=HIGHEST, preferred_element_type=F32)
     steps = spread(soft, tile)
     rate = steps * -jnp.exp(head_rows(alog[...], heads))
     lower = (iota((BLOCK, BLOCK), 0) >= iota((BLOCK, BLOCK), 1)).astype(F32)
-    cumul = spread(lower, rate)
+    cumul = jnp.dot(lower, rate, precision=HIGHEST, preferred_element_type=F32)
     step[...] = steps
     cum[...] = cumul
     sig[...] = spread(sigma, tile)
     rows[0] = cumul.T[:GROUP]
-    rows[1] = steps.T[:GROUP]
+    rows[1, :heads] = soft
     closing = cumul[BLOCK - 1 : BLOCK, :]
     weight = jnp.exp(closing - cumul) * (segment == last).astype(F32) * steps
     decay = jnp.exp(closing) * (last == prior).astype(F32)
@@ -149,7 +151,7 @@
         out[:, col] = mm(high, both) + mm(low, both)
 
 
-def output_kernel(lengths, offset, sin, ends, prefix, cum, step, x, z, g, b, c, diag, dskip, gain, oh, yp, stats, full, state):
+def output_kernel(lengths, offset, sin, ends, prefix, cum, step, x, z, g, b, c, diag, dskip, gain, oh, yp, stats, state):
     block = pl.program_id(0)
 
     @pl.when(block == 0)
@@ -173,9 +175,7 @@
         gated = y * (zf / (1.0 + jnp.exp(-zf)))
         square = square + gated * gated
         cross = cross + g[:, col].astype(F32) * gain[:, col] * gated
-        after = ends[0, :, col] + prefix[0, :, col] * sin[:, col]
-        full[0, :, col] = after
-        state[:, col] = after
+        state[:, col] = ends[0, :, col] + prefix[0, :, col] * sin[:, col]
     lane = iota((BLOCK, LANES), 1)
     sums = jnp.where(lane == 0, jnp.sum(square, axis=1, keepdims=True), 0.0)
     stats[...] = sums + jnp.where(lane == 1, jnp.sum(cross, axis=1, keepdims=True), 0.0)
@@ -238,49 +238,59 @@
             own_grad[k] = state[:, k * chunk : (k + 1) * chunk]
 
 
-def diagonal_back_kernel(lengths, offset, cum, rows, step, x, b, c, dyh, dyl, rho3, sin, full, oh, du, db, dc):
+def diagonal_back_kernel(lengths, offset, cum, rows, step, x, b, c, dyh, dyl, sin, ends, prefix, oh, *rest, part, last):
+    if last:
+        score_in, carried_in, rho3, du, db, dc = rest
+    elif part:
+        score_in, carried_in, du, score_out, carried_out = rest
+    else:
+        du, score_out, carried_out = rest
     block = pl.program_id(0)
     seg_column, seg_row, prior, _ = segments(lengths, offset, block)
     mask = (seg_column == seg_row) & (iota((BLOCK, BLOCK), 1) > iota((BLOCK, BLOCK), 0))
     scores = mm_nt(b[...], c[...])
     left = iota((BLOCK, LANES), 1) < HEADDIM
-    score_grad = jnp.zeros((BLOCK, BLOCK), F32)
-    carried_c = jnp.zeros((BLOCK, STATE), F32)
+    score_grad = score_in[...] if part else jnp.zeros((BLOCK, BLOCK), F32)
+    carried_c = carried_in[...] if part else jnp.zeros((BLOCK, STATE), F32)
     inflow = pieces(jnp.exp(cum[...]) * (seg_column == prior).astype(F32))
-    for pair in range(x.shape[1] // LANES):
+    pairs = x.shape[1] // LANES
+    for pair in range(pairs):
         col = slice(pair * LANES, (pair + 1) * LANES)
         pair_x, high_dy, low_dy = x[:, col], dyh[:, col], dyl[:, col]
         zero = jnp.zeros_like(pair_x)
-        x0, x1 = jnp.where(left, pair_x, zero), jnp.where(left, zero, pair_x)
-        lhs = jnp.concatenate([jnp.concatenate([x0, x0], axis=1), jnp.concatenate([x1, x1], axis=1)], axis=0)
-        products = mm_nt(lhs, jnp.concatenate([high_dy, low_dy], axis=1))
+        top = jnp.concatenate([jnp.where(left, high_dy, zero), jnp.where(left, low_dy, zero)], axis=1)
+        bottom = jnp.concatenate([jnp.where(left, zero, high_dy), jnp.where(left, zero, low_dy)], axis=1)
+        both = jnp.concatenate([top, bottom], axis=0)
+        products = mm_nt(jnp.concatenate([pair_x, pair_x], axis=1), both)
         parts = []
         for e in (0, 1):
-            h = 2 * pair + e
+            h = 2 * (part * pairs + pair) + e
             gap = rows[0, h : h + 1, :] - cum[:, h : h + 1]
             decay = jnp.where(mask, jnp.exp(jnp.minimum(gap, 0.0)), 0.0)
-            score_grad = score_grad + decay * products[e * BLOCK : (e + 1) * BLOCK] * step[:, h : h + 1]
+            score_grad = score_grad + decay * products[:, e * BLOCK : (e + 1) * BLOCK] * step[:, h : h + 1]
             parts.append(split(decay * scores))
-        high = jnp.concatenate([parts[0][0], parts[1][0]], axis=1)
-        low = jnp.concatenate([parts[0][1], parts[1][1]], axis=1)
-        both_high = jnp.concatenate([jnp.where(left, high_dy, zero), jnp.where(left, zero, high_dy)], axis=0)
-        both_low = jnp.concatenate([jnp.where(left, low_dy, zero), jnp.where(left, zero, low_dy)], axis=0)
-        du[:, col] = mm(high, both_high) + (mm(low, both_high) + mm(high, both_low))
+        high = mm(jnp.concatenate([parts[0][0], parts[1][0]], axis=1), both)
+        low = mm(jnp.concatenate([parts[0][1], parts[1][1]], axis=1), both[:, :LANES])
+        du[:, col] = high[:, :LANES] + (high[:, LANES:] + low)
     for at in range(0, x.shape[1], COLS):
         col = slice(at, at + COLS)
         dy = dyh[:, col].astype(F32) + dyl[:, col].astype(F32)
         high, low = split(dy * mm(inflow, oh[:, col]))
-        entering = jnp.where(block == 0, sin[:, col], full[0, :, col])
+        entering = jnp.where(block == 0, sin[:, col], ends[0, :, col] + prefix[0, :, col] * sin[:, col])
         s_high, s_low = split(entering)
         carried_c = carried_c + (mm_nt(high, s_high) + (mm_nt(low, s_high) + mm_nt(high, s_low)))
-    lane = iota((BLOCK, LANES), 1)
-    own = jnp.sum(jnp.where(lane < GROUP, rho3[...] * step[...], 0.0), axis=1, keepdims=True)
-    high, low = split(score_grad)
-    db[...] = mm(high, c[...]) + mm(low, c[...]) + own * c[...].astype(F32)
-    dc[...] = carried_c + (mm_tn(high, b[...]) + mm_tn(low, b[...])) + own * b[...].astype(F32)
-
-
-def input_kernel(lengths, offset, sout, starts, decs, full, cum, step, sig, x, b, c, dyh, dyl, diag, rho1, rho3, dskip, alog, oh, dbd, xgrad, db, draw, sums, state, run):
+    if last:
+        lane = iota((BLOCK, LANES), 1)
+        own = jnp.sum(jnp.where(lane < GROUP, rho3[...] * step[...], 0.0), axis=1, keepdims=True)
+        high, low = split(score_grad)
+        db[...] = mm(high, c[...]) + mm(low, c[...]) + own * c[...].astype(F32)
+        dc[...] = carried_c + (mm_tn(high, b[...]) + mm_tn(low, b[...])) + own * b[...].astype(F32)
+    else:
+        score_out[...] = score_grad
+        carried_out[...] = carried_c
+
+
+def input_kernel(lengths, offset, sout, sin, starts, decs, ends, prefix, cum, step, sig, x, b, c, dyh, dyl, diag0, diag1, diag2, rho1, rho3, dskip, alog, oh, dbd, dc_mine, dc_other, gpart, xgrad, db, dc, draw, sums, state, run, small):
     turn = pl.program_id(0)
     block = pl.num_programs(0) - 1 - turn
 
@@ -288,7 +298,7 @@
     def _():
         state[...] = sout[...]
         run[...] = jnp.ones_like(run)
-        sums[...] = jnp.zeros_like(sums)
+        small[...] = jnp.zeros_like(small)
 
     segment, _, _, last = segments(lengths, offset, block)
     steps = step[...]
@@ -307,52 +317,70 @@
         weight = mm(tail, oh[:, col])
         step_wide = mm(step_pieces, oh[:, col])
         xf = x[:, col].astype(F32)
-        du = diag[:, col] + weight * (mm(b[...], s_high) + mm(b[...], s_low))
+        span = x.shape[1] // PARTS
+        within = slice(at % span, at % span + COLS)
+        du = (diag0, diag1, diag2)[at // span][:, within] + weight * (mm(b[...], s_high) + mm(b[...], s_low))
         dy = dyh[:, col].astype(F32) + dyl[:, col].astype(F32)
         xgrad[:, col] = (step_wide * du + mm(coefficient, oh[:, col]) * dy).astype(BF16)
         high, low = split(xf * du)
         second = second + (mm_nt(high, oh[:, col]) + mm_nt(low, oh[:, col]))
         high, low = split(xf * (weight * step_wide))
         carried_b = carried_b + (mm_nt(high, s_high) + (mm_nt(low, s_high) + mm_nt(high, s_low)))
-        overlap = jnp.sum((full[0, :, col] * leaving).reshape(STATE // 8, 8, COLS), axis=0)
+        whole = ends[0, :, col] + prefix[0, :, col] * sin[:, col]
+        overlap = jnp.sum((whole * leaving).reshape(STATE // 8, 8, COLS), axis=0)
         high, low = split(overlap)
         inner = inner + (mm_nt(high, oh[:, col]) + mm_nt(low, oh[:, col]))
         product = run[:, col] * decs[0, :, col]
         run[:, col] = product
         state[:, col] = starts[0, :, col] + product * sout[:, col]
     db[...] = dbd[...] + carried_b
+    dc[...] = dc_mine[...] + dc_other[...]
     upper = (iota((BLOCK, BLOCK), 1) >= iota((BLOCK, BLOCK), 0)).astype(F32)
     rate_grad = jnp.dot(upper, rho1[...] - steps * second, precision=HIGHEST, preferred_element_type=F32)
     rate_grad = rate_grad + jnp.sum(inner, axis=0, keepdims=True)
     speed = jnp.exp(head_rows(alog[...], alog.shape[1]))
     raw_grad = (second + own * rho3[...] - speed * rate_grad) * sig[...]
-    draw[...] = raw_grad[:, : draw.shape[1]]
+    draw[...] = raw_grad.T[: draw.shape[0]]
     row = iota((8, LANES), 0)
     bias_row = jnp.where(row == 0, jnp.sum(raw_grad, axis=0, keepdims=True), 0.0)
     alog_row = jnp.where(row == 1, jnp.sum(rate_grad * steps * -speed, axis=0, keepdims=True), 0.0)
     skip_row = jnp.where(row == 2, jnp.sum(rho3[...], axis=0, keepdims=True), 0.0)
-    sums[...] += bias_row + alog_row + skip_row
-
-
-def relay(own, total, axis, forward):
+    small[...] += bias_row + alog_row + skip_row
+
+    @pl.when(turn == pl.num_programs(0) - 1)
+    def _():
+        for k in range(sums.shape[0]):
+            sums[k, :8] = small[...]
+            for r in range(x.shape[1] // LANES):
+                sums[k, 8 + r : 9 + r] = gpart[:, r * LANES : (r + 1) * LANES]
+
+
+def relay(own, total, axis, forward, work=None):
     count = lax.axis_size(axis)
     index = lax.axis_index(axis)
     rank = index if forward else count - 1 - index
-    pairs = [(i, i + 1) if forward else (i + 1, i) for i in range(count - 1)]
     chunks = own.shape[0]
-    arriving = jnp.zeros(own.shape[1:], F32)
+    steps = chunks + LAG * (count - 2)
     received = []
-    for turn in range(chunks + count - 2):
-        at = jnp.clip(turn - rank, 0, chunks - 1)
-        message = lax.dynamic_index_in_dim(own, at, 0, False) + lax.dynamic_index_in_dim(total, at, 0, False) * arriving
-        arriving = lax.ppermute(message, axis, pairs)
-        received.append(arriving)
+    message = None
+    for turn in range(steps):
+        at = jnp.clip(turn - LAG * rank, 0, chunks - 1)
+        mine = lax.dynamic_index_in_dim(own, at, 0, False)
+        if turn >= LAG:
+            arrived, _ = lax.optimization_barrier((received[turn - LAG], message))
+            mine = mine + lax.dynamic_index_in_dim(total, at, 0, False) * arrived
+        message = mine
+        ranks = [r for r in range(count - 1) if 0 <= turn - LAG * r < chunks]
+        pairs = [(r, r + 1) if forward else (count - 1 - r, count - 2 - r) for r in ranks]
+        received.append(lax.ppermute(message, axis, pairs))
+        if work and turn % LAG == LAG - 1 and turn // LAG < PARTS:
+            work(turn // LAG, message)
     stacked = jnp.stack(received)
     picked = [
-        lax.dynamic_index_in_dim(stacked, jnp.clip(k + rank - 1, 0, len(received) - 1), 0, False)
+        lax.dynamic_index_in_dim(stacked, jnp.clip(k + LAG * (rank - 1), 0, steps - 1), 0, False)
         for k in range(chunks)
     ]
-    return jnp.concatenate(picked, axis=1)
+    return jnp.where(rank > 0, jnp.concatenate(picked, axis=1), 0.0)
 
 
 def shards(x, z, b, c, raw, lengths, bias, alog, dskip, gain, grad):
@@ -362,15 +390,16 @@
     chunk = width // CHUNKS
     x, z, grad = (v.reshape(tokens, width) for v in (x, z, grad))
     b, c = b.reshape(tokens, STATE), c.reshape(tokens, STATE)
-    raw = raw.reshape(tokens, heads)
+    raw = raw.reshape(tokens, heads).T
     lengths = lengths.reshape(-1)
-    bias, alog, dskip = (v.reshape(1, heads) for v in (bias, alog, dskip))
+    bias = bias.reshape(heads, 1)
+    alog, dskip = (v.reshape(1, heads) for v in (alog, dskip))
     gain = gain.reshape(1, width)
     offset = jnp.reshape(lax.axis_index("seq") * tokens, (1,)).astype(jnp.int32)
     lane = jnp.arange(LANES)[:, None]
     oh = ((lane % GROUP == jnp.arange(width)[None, :] // HEADDIM) & (lane < 3 * GROUP)).astype(BF16)
 
-    def call(kernel, reverse, ins, outs, scratch, name):
+    def call(kernel, reverse, ins, outs, scratch, name, part=0):
         place = (lambda i: blocks - 1 - i) if reverse else (lambda i: i)
 
         def spec(kind, shape):
@@ -382,6 +411,15 @@
                 return pl.BlockSpec((1,) + tuple(shape[1:]), lambda i: (place(i), 0, 0))
             if kind == "prev":
                 return pl.BlockSpec((1,) + tuple(shape[1:]), lambda i: (jnp.maximum(place(i) - 1, 0), 0, 0))
+            if kind in ("cols", "hold", "prevs"):
+                span = shape[-1] // PARTS
+                return {
+                    "cols": pl.BlockSpec((BLOCK, span), lambda i: (place(i), part)),
+                    "hold": pl.BlockSpec((shape[0], span), lambda i: (0, part)),
+                    "prevs": pl.BlockSpec((1, shape[1], span), lambda i: (jnp.maximum(place(i) - 1, 0), 0, part)),
+                }[kind]
+            if kind == "raw":
+                return pl.BlockSpec((shape[0], BLOCK), lambda i: (0, place(i)))
             if kind == "row":
                 return pl.BlockSpec((2, GROUP, BLOCK), lambda i: (0, 0, place(i)))
             return pl.BlockSpec(tuple(shape), lambda i: (0,) * len(shape))
@@ -406,7 +444,7 @@
     where = [("smem", lengths), ("smem", offset)]
     e, total, ends, decs, prefix, step, cum, sig, rows = call(
         prepare_kernel, False,
-        where + [("tok", raw), ("all", bias), ("all", alog), ("tok", x), ("tok", b), ("all", oh)],
+        where + [("raw", raw), ("all", bias), ("all", alog), ("tok", x), ("tok", b), ("all", oh)],
         [("all", (CHUNKS, STATE, chunk), F32), ("all", (CHUNKS, 1, chunk), F32), ("blk", states, F32),
          ("blk", line, F32), ("blk", line, F32), ("tok", narrow, F32), ("tok", narrow, F32), ("tok", narrow, F32),
          ("row", (2, GROUP, tokens), F32)],
@@ -418,18 +456,16 @@
         where + [("tok", cum), ("row", rows), ("tok", x), ("tok", b), ("tok", c)],
         [("tok", wide, F32)], [], "diagonal",
     )
-    yp, stats, full = call(
+    yp, stats = call(
         output_kernel, False,
         where + [("all", sin), ("blk", ends), ("blk", prefix), ("tok", cum), ("tok", step), ("tok", x), ("tok", z), ("tok", grad),
                  ("tok", b), ("tok", c), ("tok", diag), ("all", dskip), ("all", gain), ("all", oh)],
-        [("tok", wide, F32), ("tok", narrow, F32), ("blk", states, F32)],
+        [("tok", wide, F32), ("tok", narrow, F32)],
         [(STATE, width)], "output",
     )
     both = lax.axis_size("head")
-    if both == 2:
-        other = lax.ppermute(stats, "head", [(0, 1), (1, 0)])
-    else:
-        other = lax.psum(stats, "head") - stats
+    exchange = partial(lax.ppermute, axis_name="head", perm=[(0, 1), (1, 0)])
+    other = exchange(stats)
     normed, zgrad, dyh, dyl, rho1, rho3, gpart, starts, own_grad = call(
         partial(norm_kernel, total_width=float(width * both)), True,
         where + [("tok", stats), ("tok", other), ("tok", cum), ("tok", step), ("tok", x), ("tok", z), ("tok", grad), ("tok", b),
@@ -438,34 +474,50 @@
          ("tok", narrow, F32), ("all", (1, width), F32), ("blk", states, F32), ("all", (CHUNKS, STATE, chunk), F32)],
         [(STATE, width)], "norm",
     )
-    sout = relay(own_grad, total, "seq", False)
-    du, dbd, dc = call(
-        diagonal_back_kernel, False,
-        where + [("tok", cum), ("row", rows), ("tok", step), ("tok", x), ("tok", b), ("tok", c), ("tok", dyh), ("tok", dyl),
-                 ("tok", rho3), ("all", sin), ("prev", full), ("all", oh)],
-        [("tok", wide, F32), ("tok", narrow, F32), ("tok", narrow, F32)], [], "diagonal_back",
-    )
-    xgrad, db, draw, sums = call(
+    du, carry = [], []
+
+    def back_part(part, message):
+        last = part == PARTS - 1
+        high, low = dyh, dyl
+        if part:
+            high, low, _ = lax.optimization_barrier((dyh, dyl, message))
+        span = width // PARTS
+        out = call(
+            partial(diagonal_back_kernel, part=part, last=last), False,
+            where + [("tok", cum), ("row", rows), ("tok", step), ("cols", x), ("tok", b), ("tok", c), ("cols", high), ("cols", low),
+                     ("hold", sin), ("prevs", ends), ("prevs", prefix), ("hold", oh)]
+            + [("tok", value) for value in carry] + ([("tok", rho3)] if last else []),
+            [("tok", (tokens, span), F32), ("tok", narrow, F32), ("tok", narrow, F32)], [], "diagonal_back", part,
+        )
+        du.append(out[0])
+        carry[:] = out[1:]
+
+    sout = relay(own_grad, total, "seq", False, back_part)
+    dbd, dc = carry
+    dc_other = exchange(dc)
+    members = lax.axis_size(("seq", "batch"))
+    xgrad, db, dc, draw, sums = call(
         input_kernel, True,
-        where + [("all", sout), ("blk", starts), ("blk", decs), ("blk", full), ("tok", cum), ("tok", step), ("tok", sig), ("tok", x),
-                 ("tok", b), ("tok", c), ("tok", dyh), ("tok", dyl), ("tok", du), ("tok", rho1), ("tok", rho3), ("all", dskip),
-                 ("all", alog), ("all", oh), ("tok", dbd)],
-        [("tok", wide, BF16), ("tok", narrow, F32), ("tok", (tokens, heads), F32), ("all", (8, LANES), F32)],
-        [(STATE, width), (1, width)], "input",
-    )
-    db, dc = lax.psum((db, dc), "head")
-    sums, gpart = lax.psum((sums, gpart), ("seq", "batch"))
+        where + [("all", sout), ("all", sin), ("blk", starts), ("blk", decs), ("blk", ends), ("blk", prefix), ("tok", cum), ("tok", step),
+                 ("tok", sig), ("tok", x), ("tok", b), ("tok", c), ("tok", dyh), ("tok", dyl), ("tok", du[0]), ("tok", du[1]), ("tok", du[2]), ("tok", rho1), ("tok", rho3),
+                 ("all", dskip), ("all", alog), ("all", oh), ("tok", dbd), ("tok", dc), ("tok", dc_other), ("all", gpart)],
+        [("tok", wide, BF16), ("tok", narrow, F32), ("tok", narrow, F32), ("raw", (heads, tokens), F32),
+         ("all", (members, 8 + width // LANES, LANES), F32)],
+        [(STATE, width), (1, width), (8, LANES)], "input",
+    )
+    db = db + exchange(db)
+    sums = jnp.sum(lax.all_to_all(sums, ("seq", "batch"), 0, 0), axis=0)
     return (
         normed[None],
         xgrad[None],
         zgrad[None],
         db[None],
         dc[None],
-        draw[None],
+        draw.T[None],
         sums[0, :heads],
         sums[1, :heads],
         sums[2, :heads],
-        gpart[0],
+        sums[8:].reshape(width),
     )
 
 

time: 211 us -> 150 us (0.71)
  blocking collectives: 35 us -> 0 us
  between operations: 14.4 us -> 1.27 us
  waiting for transfers between devices: 52.5 us -> 41.3 us
  Pallas kernels: 63.2 us -> 69.7 us
  starting transfers between devices: 28.4 us -> 25.1 us
  other arithmetic: 8.09 us -> 4.96 us
    psum x1 -> x0, blocking collectives: 35 us -> none  [shards(): sums, gpart = lax.psum((sums, gpart), ('seq', 'batch'))]
    ppermute x11 -> x19, waiting for transfers between devices: 52.5 us -> 34.4 us  [the longest x16 32.6 us: relay(): received.append(lax.ppermute(message, axis, pairs))]
    all_to_all x0 -> x1, waiting for transfers between devices: none -> 6.98 us  [shards(): sums = jnp.sum(lax.all_to_all(sums, ('seq', 'batch'), 0, 0), axis=0)]
    ppermute x11 -> x19, starting transfers between devices: 28.3 us -> 21.8 us  [the longest x16 21.4 us: relay(): received.append(lax.ppermute(message, axis, pairs))]
    pallas_call x6 -> x8, Pallas kernels: 63.2 us -> 69.7 us  [call(): pl.pallas_call(kernel, grid=(blocks,), in_specs=[spec(kind, value.shape)...]
    unnamed x22 -> x26, local copies, waits for them, and re-layouts: 7.54 us -> 1.63 us
    add x10 -> x12, other arithmetic: 4.25 us -> 0.33 us  [relay(): mine = mine + lax.dynamic_index_in_dim(total, at, 0, False) * arrived]
    all_to_all x0 -> x1, starting transfers between devices: none -> 3.37 us  [shards(): sums = jnp.sum(lax.all_to_all(sums, ('seq', 'batch'), 0, 0), axis=0)]
  transfers between devices with their start and end apart: 12 -> 20, of which waited for: 9 -> 8; matrix products, arithmetic and copies ran while one was open for 1% -> 2% of each run, Pallas kernels for 9% -> 17%
where the time goes in v2:
time: 150 us; the launch traced here: 149 us
  Pallas kernels  69.7 us (46%)
  waiting for transfers between devices  41.3 us (28%)
  starting transfers between devices  25.1 us (17%)
  local copies, waits for them, and re-layouts  7.03 us (5%)
  other arithmetic  4.96 us (3%)
    pallas_call x8, Pallas kernels, call(): pl.pallas_call(kernel, grid=(blocks,), in_specs=[spec(kind, value.shape)...  69.7 us
    ppermute x16, waiting for transfers between devices, relay(): received.append(lax.ppermute(message, axis, pairs))  32.6 us
    ppermute x16, starting transfers between devices, relay(): received.append(lax.ppermute(message, axis, pairs))  21.4 us
    all_to_all x1, waiting for transfers between devices, shards(): sums = jnp.sum(lax.all_to_all(sums, ('seq', 'batch'), 0, 0), axis=0)  6.98 us
    all_to_all x1, starting transfers between devices, shards(): sums = jnp.sum(lax.all_to_all(sums, ('seq', 'batch'), 0, 0), axis=0)  3.37 us
  transfers between devices with their start and end apart: 20, of which 8 were waited for; matrix products, arithmetic and copies ran while one was open for 2% of the time, Pallas kernels for 17%

profile of v2, /device:TPU:0, one launch (start us, length us, event | category | flops | bytes accessed | tf_op | source)
XLA Modules:
  0.0 149.4 jit_solution(4325051813661520846)
XLA Ops:
  0.7 1.3 copy.21.bias
  2.0 0.9 and_convert_fusion.oh
  3.0 9.0 %prepare.1 = (f32[4,128,384]{2,1,0:T(8,128)}, f32[4,1,384]{2,1,0:T(1,128)}, f32[4,128,1536]{2,1,0:T(8,128)}, f32[4,1,1536]{2,1,0:T(1,128)}, f32[4,1,1536]{2,1,0:...) custom-call(s32[2]{0:T(128)} %bitcast.138, s32[1]{0:T(128)} %bitcast.1.offset, ...), custom_call_target="tpu_custom_call" | custom-call | tf_op jit(solution)/shard_map/prepare/pallas_call | solution.py:427
  12.0 1.1 dynamic-slice_bitcast_fusion.10
  13.0 4.9 %collective-permute-start = (f32[128,384]{1,0:T(8,128)S(1)}, f32[128,384]{1,0:T(8,128)S(1)}, u32[]{:S(2)}, u32[]{:S(2)}) collective-permute-start(f32[128,384]{1,0:T(8,128)S(1)} %get-tuple-element.133), channel_id=1, source_target_pairs={{0,4},{1,5},{2,6},{3,7},{16,20},{17,21},{18,22},{19,23}} | collective-permute-start | bytes 589832 | tf_op jit(solution)/shard_map/ppermute | solution.py:375
  18.0 1.3 collective-permute-start.1
  19.4 0.6 reshape.139.gain
  20.0 6.2 %diagonal.1.diag = f32[512,1536]{1,0:T(8,128)} custom-call(s32[2]{0:T(128)} %bitcast.139, s32[1]{0:T(128)} %bitcast.1.offset, f32[512,128]{1,0:T(8,128)} %get-tuple-element.70.cum, f32[2,32,512]{2,1,0:T(8,128)} %get-tuple-element.72.rows, bf16[512,1536]{1,0:T(8,128)(2,1)} %bitcast.111, bf16[512,128]{1,0:T(8,128)(2,1)} %bitcast.119, bf16[512,128]{1,0:T(8,128)(2,1)} %bitcast.126), custom_call_target="tpu_custom_call" | custom-call | tf_op jit(solution)/shard_map/diagonal/pallas_call | solution.py:427
  26.1 0.1 fusion.14
  26.2 0.0 collective-permute-done
  26.3 1.4 collective-permute-start.2
  27.7 0.0 collective-permute-done.1
  27.8 3.0 %collective-permute-start.3 = (f32[128,384]{1,0:T(8,128)S(1)}, f32[128,384]{1,0:T(8,128)S(1)}, u32[]{:S(2)}, u32[]{:S(2)}) collective-permute-start(f32[128,384]{1,0:T(8,128)S(1)} %bitcast_add_fusion.10), channel_id=1, source_target_pairs={{0,4},{4,8},{1,5},{5,9},{2,6},{6,10},{3,7},{7,11},{16,20},{20,24},... | collective-permute-start | bytes 589832 | tf_op jit(solution)/shard_map/ppermute | solution.py:375
  30.8 2.2 %collective-permute-done.2 = f32[128,384]{1,0:T(8,128)S(1)} collective-permute-done((f32[128,384]{1,0:T(8,128)S(1)}, f32[128,384]{1,0:T(8,128)S(1)}, u32[]{:S(2)}, u32[]{:S(2)}) %collective-permute-start.2) | collective-permute-done | bytes 196640 | tf_op jit(solution)/shard_map/ppermute | solution.py:375
  33.0 0.7 collective-permute-start.4
  33.7 2.2 %collective-permute-done.3 = f32[128,384]{1,0:T(8,128)S(1)} collective-permute-done((f32[128,384]{1,0:T(8,128)S(1)}, f32[128,384]{1,0:T(8,128)S(1)}, u32[]{:S(2)}, u32[]{:S(2)}) %collective-permute-start.3) | collective-permute-done | bytes 196640 | tf_op jit(solution)/shard_map/ppermute | solution.py:375
  36.0 0.7 collective-permute-start.5
  36.7 0.0 collective-permute-done.4
  36.7 0.7 collective-permute-start.6
  37.4 0.0 collective-permute-done.5
  37.5 0.7 collective-permute-start.7
  38.2 0.0 collective-permute-done.6
  38.2 0.0 collective-permute-done.7
  38.3 0.1 dynamic-slice_bitcast_fusion.9
  38.3 1.0 maximum_select_fusion.sin
  39.3 8.5 %output.1 = (f32[512,1536]{1,0:T(8,128)}, f32[512,128]{1,0:T(8,128)}) custom-call(s32[2]{0:T(128)} %bitcast.140, s32[1]{0:T(128)} %bitcast.1.offset, f32[128,1536]{1,0:T(8,128)} %maximum_select_fusion.sin, f32[4,128,1536]{2,1,0:T(8,128)} %get-tuple-element.68.ends, f32[4,1,1536]{2,1,0:T(1,128)} %get-tuple-element.69.prefix, ...), custom_call_target="tpu_custom_call" | custom-call | tf_op jit(solution)/shard_map/output/pallas_call | solution.py:427
  47.9 0.1 collective-permute-start.8
  48.0 1.7 %collective-permute-done.8.other = f32[512,128]{1,0:T(8,128)S(1)} collective-permute-done((f32[512,128]{1,0:T(8,128)}, f32[512,128]{1,0:T(8,128)S(1)}, u32[]{:S(2)}, u32[]{:S(2)}) %collective-permute-start.8) | collective-permute-done | bytes 262176 | tf_op jit(solution)/shard_map/ppermute | solution.py:468
  49.7 0.7 copy-done.3
  50.4 14.3 %norm.1 = (bf16[512,1536]{1,0:T(8,128)(2,1)}, bf16[512,1536]{1,0:T(8,128)(2,1)}, bf16[512,1536]{1,0:T(8,128)(2,1)}, bf16[512,1536]{1,0:T(8,128)(2,1)}, f32[512,1...) custom-call(s32[2]{0:T(128)} %bitcast.141, ...), custom_call_target="tpu_custom_call" | custom-call | tf_op jit(solution)/shard_map/norm/pallas_call | solution.py:427
  64.6 1.1 dynamic-slice_bitcast_fusion.4
  65.7 0.7 collective-permute-start.9
  66.4 0.7 collective-permute-start.10
  67.1 0.0 copy-start.1
  67.1 6.3 %diagonal_back.3 = (f32[512,512]{1,0:T(8,128)}, f32[512,128]{1,0:T(8,128)}, f32[512,128]{1,0:T(8,128)}) custom-call(s32[2]{0:T(128)} %bitcast.142, s32[1]{0:T(128)} %bitcast.1.offset, f32[512,128]{1,0:T(8,128)} %get-tuple-element.70.cum, f32[2,32,512]{2,1,0:T(8,128)} %get-tuple-element.72.rows, f32[512,128]{1,0:T(8,128)} %get-tuple-element.71.step, ...), custom_call_target="tpu_custom_call" | custom-call | tf_op jit(solution)/shard_map/diagonal_back/pallas_call | solution.py:427
  73.3 0.0 collective-permute-done.9
  73.4 0.7 collective-permute-start.11
  74.1 0.0 collective-permute-done.10
  74.1 0.7 collective-permute-start.12
  74.8 6.3 %diagonal_back.4 = (f32[512,512]{1,0:T(8,128)}, f32[512,128]{1,0:T(8,128)}, f32[512,128]{1,0:T(8,128)}) custom-call(s32[2]{0:T(128)} %bitcast.143, s32[1]{0:T(128)} %bitcast.1.offset, f32[512,128]{1,0:T(8,128)} %get-tuple-element.70.cum, f32[2,32,512]{2,1,0:T(8,128)} %get-tuple-element.72.rows, f32[512,128]{1,0:T(8,128)} %get-tuple-element.71.step, ...), custom_call_target="tpu_custom_call" | custom-call | tf_op jit(solution)/shard_map/diagonal_back/pallas_call | solution.py:427
  81.1 0.0 collective-permute-done.11
  81.2 1.3 collective-permute-start.13
  82.5 0.0 collective-permute-done.12
  82.5 1.3 collective-permute-start.14
  83.8 6.2 %diagonal_back.5 = (f32[512,512]{1,0:T(8,128)}, f32[512,128]{1,0:T(8,128)}, f32[512,128]{1,0:T(8,128)}) custom-call(s32[2]{0:T(128)} %bitcast.144, s32[1]{0:T(128)} %bitcast.1.offset, f32[512,128]{1,0:T(8,128)} %get-tuple-element.70.cum, f32[2,32,512]{2,1,0:T(8,128)} %get-tuple-element.72.rows, f32[512,128]{1,0:T(8,128)} %get-tuple-element.71.step, ...), custom_call_target="tpu_custom_call" | custom-call | tf_op jit(solution)/shard_map/diagonal_back/pallas_call | solution.py:427
  90.0 0.2 collective-permute-start.17
  90.3 13.7 %collective-permute-done.13 = f32[128,384]{1,0:T(8,128)S(1)} collective-permute-done((f32[128,384]{1,0:T(8,128)S(1)}, f32[128,384]{1,0:T(8,128)S(1)}, u32[]{:S(2)}, u32[]{:S(2)}) %collective-permute-start.13) | collective-permute-done | bytes 196640 | tf_op jit(solution)/shard_map/ppermute | solution.py:375
  104.0 1.3 collective-permute-start.15
  105.3 3.2 %collective-permute-done.14 = f32[128,384]{1,0:T(8,128)S(1)} collective-permute-done((f32[128,384]{1,0:T(8,128)S(1)}, f32[128,384]{1,0:T(8,128)S(1)}, u32[]{:S(2)}, u32[]{:S(2)}) %collective-permute-start.14) | collective-permute-done | bytes 196640 | tf_op jit(solution)/shard_map/ppermute | solution.py:375
  108.5 1.5 collective-permute-start.16
  110.0 7.3 %collective-permute-done.15 = f32[128,384]{1,0:T(8,128)S(1)} collective-permute-done((f32[128,384]{1,0:T(8,128)S(1)}, f32[128,384]{1,0:T(8,128)S(1)}, u32[]{:S(2)}, u32[]{:S(2)}) %collective-permute-start.15) | collective-permute-done | bytes 196640 | tf_op jit(solution)/shard_map/ppermute | solution.py:375
  117.4 4.0 %collective-permute-done.16 = f32[128,384]{1,0:T(8,128)S(1)} collective-permute-done((f32[128,384]{1,0:T(8,128)S(1)}, f32[128,384]{1,0:T(8,128)S(1)}, u32[]{:S(2)}, u32[]{:S(2)}) %collective-permute-start.16) | collective-permute-done | bytes 196640 | tf_op jit(solution)/shard_map/ppermute | solution.py:375
  121.4 0.1 dynamic-slice_bitcast_fusion.3
  121.5 1.0 maximum_select_fusion.1.sout
  122.5 0.0 collective-permute-done.17.dc_other
  122.5 0.7 copy-done.2
  123.2 13.0 %input.1 = (bf16[512,1536]{1,0:T(8,128)(2,1)}, f32[512,128]{1,0:T(8,128)}, f32[512,128]{1,0:T(8,128)}, f32[24,512]{1,0:T(8,128)}, f32[8,20,128]{2,1,0:T(8,128)}) custom-call(s32[2]{0:T(128)} %bitcast.145, s32[1]{0:T(128)} %bitcast.1.offset, f32[128,1536]{1,0:T(8,128)} %maximum_select_fusion.1.sout, f32[128,1536]{1,0:T(8,128)} %maximum_select_fusion.sin, ...), custom_call_target="tpu_custom_call" | custom-call | tf_op jit(solution)/shard_map/input/pallas_call | solution.py:427
  136.1 3.4 %all-to-all-start = ((f32[8,20,128]{2,1,0:T(8,128)}), f32[8,20,128]{2,1,0:T(8,128)S(1)}, u32[]{:S(2)}, u32[]{:S(2)}) async-start(f32[8,20,128]{2,1,0:T(8,128)} %get-tuple-element.109), calls=%async_computation | async-start | bytes 196608 | tf_op jit(solution)/shard_map/all_to_all | solution.py:509
  139.5 0.1 collective-permute-start.18
  139.6 7.0 %all-to-all-done = f32[8,20,128]{2,1,0:T(8,128)S(1)} async-done(((f32[8,20,128]{2,1,0:T(8,128)}), f32[8,20,128]{2,1,0:T(8,128)S(1)}, u32[]{:S(2)}, u32[]{:S(2)}) %all-to-all-start) | async-done | bytes 81952 | tf_op jit(solution)/shard_map/all_to_all | solution.py:509
  146.6 0.5 slice_bitcast_fusion.1
  147.1 0.6 slice_bitcast_fusion
  147.7 0.0 collective-permute-done.18
  147.7 1.7 %add_bitcast_fusion = f32[1,512,128]{2,1,0:T(8,128)} fusion(f32[512,128]{1,0:T(8,128)} %get-tuple-element.106, f32[512,128]{1,0:T(8,128)S(1)} %collective-permute-done.18), kind=kLoop, calls=%fused_computation.3 | loop fusion | flops 65536 | bytes 786432 | tf_op jit(solution)/shard_map/broadcast_in_dim | solution.py:514
  (41 shorter events, 0.6 us)
Async XLA Ops:
  3.0 16.4 %copy-start.5 = (f32[1536]{0:T(1024)S(1)}, f32[1536]{0:T(1024)}, u32[]{:S(2)}) copy-start(f32[1536]{0:T(1024)} %param.20) | copy-start | bytes 18436
  13.0 13.2 %collective-permute-start = (f32[128,384]{1,0:T(8,128)S(1)}, f32[128,384]{1,0:T(8,128)S(1)}, u32[]{:S(2)}, u32[]{:S(2)}) collective-permute-start(f32[128,384]{1,0:T(8,128)S(1)} %get-tuple-element.133), channel_id=1, source_target_pairs={{0,4},{1,5},{2,6},{3,7},{16,20},{17,21},{18,22},{19,23}} | collective-permute-start | bytes 589832 | tf_op jit(solution)/shard_map/ppermute | solution.py:375
  18.0 9.7 %collective-permute-start.1 = (f32[128,384]{1,0:T(8,128)S(1)}, f32[128,384]{1,0:T(8,128)S(1)}, u32[]{:S(2)}, u32[]{:S(2)}) collective-permute-start(f32[128,384]{1,0:T(8,128)S(1)} %get-tuple-element.132), channel_id=1, source_target_pairs={{0,4},{1,5},{2,6},{3,7},{16,20},{17,21},{18,22},{19,23}} | collective-permute-start | bytes 589832 | tf_op jit(solution)/shard_map/ppermute | solution.py:375
  20.0 6.2 %copy-start.4 = (f32[4,1,384]{2,1,0:T(1,128)S(1)}, f32[4,1,384]{2,1,0:T(1,128)}, u32[]{:S(2)}) copy-start(f32[4,1,384]{2,1,0:T(1,128)} %get-tuple-element.61) | copy-start | bytes 18436
  20.0 6.3 %copy-start = (f32[4,128,384]{2,1,0:T(8,128)S(1)}, f32[4,128,384]{2,1,0:T(8,128)}, u32[]{:S(2)}) copy-start(f32[4,128,384]{2,1,0:T(8,128)} %get-tuple-element.60) | copy-start | bytes 2359300
  26.3 6.7 %collective-permute-start.2 = (f32[128,384]{1,0:T(8,128)S(1)}, f32[128,384]{1,0:T(8,128)S(1)}, u32[]{:S(2)}, u32[]{:S(2)}) collective-permute-start(f32[128,384]{1,0:T(8,128)S(1)} %bitcast_add_fusion.11), channel_id=1, source_target_pairs={{0,4},{4,8},{1,5},{5,9},{2,6},{6,10},{3,7},{7,11},{16,20},{20,24},... | collective-permute-start | bytes 589832 | tf_op jit(solution)/shard_map/ppermute | solution.py:375
  27.8 8.2 %collective-permute-start.3 = (f32[128,384]{1,0:T(8,128)S(1)}, f32[128,384]{1,0:T(8,128)S(1)}, u32[]{:S(2)}, u32[]{:S(2)}) collective-permute-start(f32[128,384]{1,0:T(8,128)S(1)} %bitcast_add_fusion.10), channel_id=1, source_target_pairs={{0,4},{4,8},{1,5},{5,9},{2,6},{6,10},{3,7},{7,11},{16,20},{20,24},... | collective-permute-start | bytes 589832 | tf_op jit(solution)/shard_map/ppermute | solution.py:375
  33.0 3.7 %collective-permute-start.4 = (f32[128,384]{1,0:T(8,128)S(1)}, f32[128,384]{1,0:T(8,128)S(1)}, u32[]{:S(2)}, u32[]{:S(2)}) collective-permute-start(f32[128,384]{1,0:T(8,128)S(1)} %bitcast_add_fusion.9), channel_id=1, source_target_pairs={{4,8},{8,12},{5,9},{9,13},{6,10},{10,14},{7,11},{11,15},{20,24},{2... | collective-permute-start | bytes 589832 | tf_op jit(solution)/shard_map/ppermute | solution.py:375
  36.0 1.5 collective-permute-start.5
  36.7 1.5 collective-permute-start.6
  37.5 0.8 collective-permute-start.7
  47.9 1.8 %collective-permute-start.8 = (f32[512,128]{1,0:T(8,128)}, f32[512,128]{1,0:T(8,128)S(1)}, u32[]{:S(2)}, u32[]{:S(2)}) collective-permute-start(f32[512,128]{1,0:T(8,128)} %get-tuple-element.73.mine), channel_id=1, source_target_pairs={{0,1},{1,0},{2,3},{3,2},{4,5},{5,4},{6,7},{7,6},{8,9},{9,8},{10,11... | collective-permute-start | bytes 786440 | tf_op jit(solution)/shard_map/ppermute | solution.py:468
  49.7 0.7 copy-start.3
  65.7 7.7 %collective-permute-start.9 = (f32[128,384]{1,0:T(8,128)S(1)}, f32[128,384]{1,0:T(8,128)S(1)}, u32[]{:S(2)}, u32[]{:S(2)}) collective-permute-start(f32[128,384]{1,0:T(8,128)S(1)} %get-tuple-element.131), channel_id=1, source_target_pairs={{12,8},{13,9},{14,10},{15,11},{28,24},{29,25},{30,26},{31,27}} | collective-permute-start | bytes 589832 | tf_op jit(solution)/shard_map/ppermute | solution.py:375
  66.4 7.7 %collective-permute-start.10 = (f32[128,384]{1,0:T(8,128)S(1)}, f32[128,384]{1,0:T(8,128)S(1)}, u32[]{:S(2)}, u32[]{:S(2)}) collective-permute-start(f32[128,384]{1,0:T(8,128)S(1)} %get-tuple-element.130), channel_id=1, source_target_pairs={{12,8},{13,9},{14,10},{15,11},{28,24},{29,25},{30,26},{31,27}} | collective-permute-start | bytes 589832 | tf_op jit(solution)/shard_map/ppermute | solution.py:375
  67.1 6.3 %copy-start.1 = (f32[4,128,384]{2,1,0:T(8,128)S(1)}, f32[4,128,384]{2,1,0:T(8,128)}, u32[]{:S(2)}) copy-start(f32[4,128,384]{2,1,0:T(8,128)} %get-tuple-element.77) | copy-start | bytes 2359300
  73.4 7.7 %collective-permute-start.11 = (f32[128,384]{1,0:T(8,128)S(1)}, f32[128,384]{1,0:T(8,128)S(1)}, u32[]{:S(2)}, u32[]{:S(2)}) collective-permute-start(f32[128,384]{1,0:T(8,128)S(1)} %bitcast_add_fusion.5), channel_id=1, source_target_pairs={{12,8},{8,4},{13,9},{9,5},{14,10},{10,6},{15,11},{11,7},{28,24},{2... | collective-permute-start | bytes 589832 | tf_op jit(solution)/shard_map/ppermute | solution.py:375
  74.1 8.3 %collective-permute-start.12 = (f32[128,384]{1,0:T(8,128)S(1)}, f32[128,384]{1,0:T(8,128)S(1)}, u32[]{:S(2)}, u32[]{:S(2)}) collective-permute-start(f32[128,384]{1,0:T(8,128)S(1)} %bitcast_add_fusion.4), channel_id=1, source_target_pairs={{12,8},{8,4},{13,9},{9,5},{14,10},{10,6},{15,11},{11,7},{28,24},{2... | collective-permute-start | bytes 589832 | tf_op jit(solution)/shard_map/ppermute | solution.py:375
  81.2 22.8 %collective-permute-start.13 = (f32[128,384]{1,0:T(8,128)S(1)}, f32[128,384]{1,0:T(8,128)S(1)}, u32[]{:S(2)}, u32[]{:S(2)}) collective-permute-start(f32[128,384]{1,0:T(8,128)S(1)} %bitcast_add_fusion.3), channel_id=1, source_target_pairs={{8,4},{4,0},{9,5},{5,1},{10,6},{6,2},{11,7},{7,3},{24,20},{20,16},... | collective-permute-start | bytes 589832 | tf_op jit(solution)/shard_map/ppermute | solution.py:375
  82.5 26.0 %collective-permute-start.14 = (f32[128,384]{1,0:T(8,128)S(1)}, f32[128,384]{1,0:T(8,128)S(1)}, u32[]{:S(2)}, u32[]{:S(2)}) collective-permute-start(f32[128,384]{1,0:T(8,128)S(1)} %bitcast_add_fusion.2), channel_id=1, source_target_pairs={{8,4},{4,0},{9,5},{5,1},{10,6},{6,2},{11,7},{7,3},{24,20},{20,16},... | collective-permute-start | bytes 589832 | tf_op jit(solution)/shard_map/ppermute | solution.py:375
  90.0 32.4 %collective-permute-start.17 = (f32[512,128]{1,0:T(8,128)}, f32[512,128]{1,0:T(8,128)S(1)}, u32[]{:S(2)}, u32[]{:S(2)}) collective-permute-start(f32[512,128]{1,0:T(8,128)} %get-tuple-element.102.dc_mine), channel_id=1, source_target_pairs={{0,1},{1,0},{2,3},{3,2},{4,5},{5,4},{6,7},{7,6},{8,9},{9,8},{10,11... | collective-permute-start | bytes 786440 | tf_op jit(solution)/shard_map/ppermute | solution.py:497
  104.0 13.4 %collective-permute-start.15 = (f32[128,384]{1,0:T(8,128)S(1)}, f32[128,384]{1,0:T(8,128)S(1)}, u32[]{:S(2)}, u32[]{:S(2)}) collective-permute-start(f32[128,384]{1,0:T(8,128)S(1)} %bitcast_add_fusion.1), channel_id=1, source_target_pairs={{4,0},{5,1},{6,2},{7,3},{20,16},{21,17},{22,18},{23,19}} | collective-permute-start | bytes 589832 | tf_op jit(solution)/shard_map/ppermute | solution.py:375
  108.5 12.9 %collective-permute-start.16 = (f32[128,384]{1,0:T(8,128)S(1)}, f32[128,384]{1,0:T(8,128)S(1)}, u32[]{:S(2)}, u32[]{:S(2)}) collective-permute-start(f32[128,384]{1,0:T(8,128)S(1)} %bitcast_add_fusion), channel_id=1, source_target_pairs={{4,0},{5,1},{6,2},{7,3},{20,16},{21,17},{22,18},{23,19}} | collective-permute-start | bytes 589832 | tf_op jit(solution)/shard_map/ppermute | solution.py:375
  122.5 0.7 copy-start.2
  136.1 10.4 %all-to-all-start = ((f32[8,20,128]{2,1,0:T(8,128)}), f32[8,20,128]{2,1,0:T(8,128)S(1)}, u32[]{:S(2)}, u32[]{:S(2)}) async-start(f32[8,20,128]{2,1,0:T(8,128)} %get-tuple-element.109), calls=%async_computation | async-start | bytes 196608 | tf_op jit(solution)/shard_map/all_to_all | solution.py:509
  139.5 8.2 %collective-permute-start.18 = (f32[512,128]{1,0:T(8,128)}, f32[512,128]{1,0:T(8,128)S(1)}, u32[]{:S(2)}, u32[]{:S(2)}) collective-permute-start(f32[512,128]{1,0:T(8,128)} %get-tuple-element.106), channel_id=1, source_target_pairs={{0,1},{1,0},{2,3},{3,2},{4,5},{5,4},{6,7},{7,6},{8,9},{9,8},{10,11... | collective-permute-start | bytes 786440 | tf_op jit(solution)/shard_map/ppermute | solution.py:508

commit v3 on v2

v3 whole, which is shorter than its diff:
```python
from functools import partial

import jax
import jax.numpy as jnp
import numpy as np
from jax import lax
from jax.experimental import pallas as pl
from jax.experimental.pallas import tpu as pltpu
from jax.sharding import PartitionSpec as P

STATE = 128
HEADDIM = 64
BLOCK = 128
LANES = 128
GROUP = 32
COLS = 256
HALF_CHUNKS = 2
LAG = 2
EPSILON = 1e-05
HIGHEST = lax.Precision.HIGHEST
F32 = jnp.float32
BF16 = jnp.bfloat16
VMEM_LIMIT = 60 * 1024 * 1024


def mm(a, b):
    return jnp.dot(a, b, preferred_element_type=F32)


def mm_nt(a, b):
    return lax.dot_general(a, b, (((1,), (1,)), ((), ())), preferred_element_type=F32)


def mm_tn(a, b):
    return lax.dot_general(a, b, (((0,), (0,)), ((), ())), preferred_element_type=F32)


def split(value):
    high = value.astype(BF16)
    return high, (value - high.astype(F32)).astype(BF16)


def iota(shape, axis):
    return lax.broadcasted_iota(jnp.int32, shape, axis)


def pieces(value):
    high = value.astype(BF16).astype(F32)
    rest = value - high
    middle = rest.astype(BF16).astype(F32)
    lane = iota(value.shape, 1)
    chosen = jnp.where(lane < GROUP, high, jnp.where(lane < 2 * GROUP, middle, rest - middle))
    return jnp.where(lane < 3 * GROUP, chosen, 0.0).astype(BF16)


def head_rows(spread, heads):
    tile = (iota((heads, LANES), 1) % GROUP == iota((heads, LANES), 0)).astype(F32)
    return jnp.dot(jnp.broadcast_to(spread, (8, heads)), tile, precision=HIGHEST, preferred_element_type=F32)[0:1]


def count_starts(lengths, position):
    start = jnp.int32(0)
    total = (start <= position).astype(jnp.int32)
    for k in range(1, lengths.shape[0]):
        start = start + lengths[k - 1]
        total = total + (start <= position).astype(jnp.int32)
    return total


def segments(lengths, offset, block):
    base = offset[0] + block * BLOCK
    column = count_starts(lengths, base + iota((BLOCK, 1), 0))
    row = count_starts(lengths, base + iota((1, BLOCK), 1))
    return column, row, count_starts(lengths, base - 1), count_starts(lengths, base + BLOCK - 1)


def local_states(weights, decays, x, b, oh, e, total, ends, decs, prefix, state, run):
    for at in range(0, x.shape[1], COLS):
        col = slice(at, at + COLS)
        high, low = split(x[:, col].astype(F32) * mm(weights, oh[:, col]))
        dec = mm(decays, oh[:, col])[0:1]
        fresh = dec * state[:, col] + (mm_tn(b[...], high) + mm_tn(b[...], low))
        state[:, col] = fresh
        ends[0, :, col] = fresh
        decs[0, :, col] = dec
        product = run[:, col] * dec
        run[:, col] = product
        prefix[0, :, col] = product

    @pl.when(pl.program_id(0) == pl.num_programs(0) - 1)
    def _():
        chunk = e.shape[2]
        for k in range(e.shape[0]):
            e[k] = state[:, k * chunk : (k + 1) * chunk]
            total[k] = run[:, k * chunk : (k + 1) * chunk]


def clear_states(state, run):
    @pl.when(pl.program_id(0) == 0)
    def _():
        state[...] = jnp.zeros_like(state)
        run[...] = jnp.ones_like(run)


def weigh(cumul, steps, segment, prior, last):
    closing = cumul[BLOCK - 1 : BLOCK, :]
    weight = jnp.exp(closing - cumul) * (segment == last).astype(F32) * steps
    decay = jnp.exp(closing) * (last == prior).astype(F32)
    return pieces(weight), pieces(jnp.broadcast_to(decay, (8, LANES)))


def prepare_kernel(lengths, offset, raw, bias, alog, x, b, oh, e, total, ends, decs, prefix, step, cum, sig, rows, state, run):
    heads = raw.shape[0]
    clear_states(state, run)
    segment, _, prior, last = segments(lengths, offset, pl.program_id(0))
    same = iota((heads, heads), 0) == iota((heads, heads), 1)
    shift = jnp.sum(jnp.where(same, jnp.broadcast_to(bias[...], (heads, heads)), 0.0), axis=1, keepdims=True)
    value = raw[...] + shift
    small = jnp.exp(-jnp.abs(value))
    ratio = small / (2.0 + small)
    square = ratio * ratio
    series = jnp.full_like(square, 1.0 / 19.0)
    for odd in (17, 15, 13, 11, 9, 7, 5, 3, 1):
        series = series * square + 1.0 / odd
    soft = jnp.maximum(value, 0.0) + 2.0 * ratio * series
    inverse = 1.0 / (1.0 + small)
    sigma = jnp.where(value >= 0.0, inverse, small * inverse)
    tile = (iota((heads, LANES), 1) % GROUP == iota((heads, LANES), 0)).astype(F32)
    spread = partial(lax.dot_general, dimension_numbers=(((0,), (0,)), ((), ())), precision=HIGHEST, preferred_element_type=F32)
    steps = spread(soft, tile)
    rate = steps * -jnp.exp(head_rows(alog[...], heads))
    lower = (iota((BLOCK, BLOCK), 0) >= iota((BLOCK, BLOCK), 1)).astype(F32)
    cumul = jnp.dot(lower, rate, precision=HIGHEST, preferred_element_type=F32)
    step[...] = steps
    cum[...] = cumul
    sig[...] = spread(sigma, tile)
    rows[0] = cumul.T[:GROUP]
    rows[1] = steps.T[:GROUP]
    weights, decays = weigh(cumul, steps, segment, prior, last)
    local_states(weights, decays, x, b, oh, e, total, ends, decs, prefix, state, run)


def states_kernel(lengths, offset, cum, step, x, b, oh, e, total, ends, decs, prefix, state, run):
    clear_states(state, run)
    segment, _, prior, last = segments(lengths, offset, pl.program_id(0))
    weights, decays = weigh(cum[...], step[...], segment, prior, last)
    local_states(weights, decays, x, b, oh, e, total, ends, decs, prefix, state, run)


def diagonal_kernel(lengths, offset, cum, rows, x, b, c, out, *, first):
    block = pl.program_id(0)
    seg_column, seg_row, _, _ = segments(lengths, offset, block)
    mask = (seg_column == seg_row) & (iota((BLOCK, BLOCK), 0) > iota((BLOCK, BLOCK), 1))
    scores = jnp.where(mask, mm_nt(c[...], b[...]), 0.0)
    left = iota((BLOCK, LANES), 1) < HEADDIM
    for pair in range(x.shape[1] // LANES):
        col = slice(pair * LANES, (pair + 1) * LANES)
        parts = []
        for h in (first + 2 * pair, first + 2 * pair + 1):
            gap = cum[:, h : h + 1] - rows[0, h : h + 1, :]
            parts.append(split(jnp.exp(jnp.minimum(gap, 0.0)) * scores * rows[1, h : h + 1, :]))
        pair_x = x[:, col]
        zero = jnp.zeros_like(pair_x)
        both = jnp.concatenate([jnp.where(left, pair_x, zero), jnp.where(left, zero, pair_x)], axis=0)
        high = jnp.concatenate([parts[0][0], parts[1][0]], axis=1)
        low = jnp.concatenate([parts[0][1], parts[1][1]], axis=1)
        out[:, col] = mm(high, both) + mm(low, both)


def output_kernel(lengths, offset, sin, ends, prefix, cum, step, x, z, g, b, c, diag, dskip, gain, oh, before, yp, stats, state):
    block = pl.program_id(0)

    @pl.when(block == 0)
    def _():
        state[...] = sin[...]

    segment, _, prior, _ = segments(lengths, offset, block)
    inflow = pieces(jnp.exp(cum[...]) * (segment == prior).astype(F32))
    own = jnp.sum(b[...].astype(F32) * c[...].astype(F32), axis=1, keepdims=True)
    coefficient = pieces(head_rows(dskip[...], dskip.shape[1]) + step[...] * own)
    square = jnp.zeros((BLOCK, COLS), F32)
    cross = jnp.zeros((BLOCK, COLS), F32)
    for at in range(0, x.shape[1], COLS):
        col = slice(at, at + COLS)
        high, low = split(state[:, col])
        carried = mm(c[...], high) + mm(c[...], low)
        partial_out = mm(inflow, oh[:, col]) * carried + diag[:, col]
        yp[:, col] = partial_out
        y = partial_out + mm(coefficient, oh[:, col]) * x[:, col].astype(F32)
        zf = z[:, col].astype(F32)
        gated = y * (zf / (1.0 + jnp.exp(-zf)))
        square = square + gated * gated
        cross = cross + g[:, col].astype(F32) * gain[:, col] * gated
        state[:, col] = ends[0, :, col] + prefix[0, :, col] * sin[:, col]
    lane = iota((BLOCK, LANES), 1)
    sums = jnp.where(lane == 0, jnp.sum(square, axis=1, keepdims=True), 0.0)
    sums = sums + jnp.where(lane == 1, jnp.sum(cross, axis=1, keepdims=True), 0.0)
    stats[...] = sums if before is None else before[...] + sums


def norm_kernel(lengths, offset, mine, other, cum, step, x, z, g, b, c, yp, dskip, gain, oh, decs, _n, _z, normed, zgrad, dyh, dyl, gpart, starts, own_grad, state, *, total_width):
    turn = pl.program_id(0)
    block = pl.num_programs(0) - 1 - turn

    @pl.when(turn == 0)
    def _():
        state[...] = jnp.zeros_like(state)
        gpart[...] = jnp.zeros_like(gpart)

    segment, _, prior, _ = segments(lengths, offset, block)
    inflow = pieces(jnp.exp(cum[...]) * (segment == prior).astype(F32))
    own = jnp.sum(b[...].astype(F32) * c[...].astype(F32), axis=1, keepdims=True)
    coefficient = pieces(head_rows(dskip[...], dskip.shape[1]) + step[...] * own)
    both = mine[...] + other[...]
    mean = both[:, 0:1] / total_width + EPSILON
    scale = lax.rsqrt(mean)
    scale = scale * (1.5 - 0.5 * mean * scale * scale)
    factor = scale * scale * scale * (both[:, 1:2] / total_width)
    for at in range(0, x.shape[1], COLS):
        col = slice(at, at + COLS)
        xf = x[:, col].astype(F32)
        y = yp[:, col] + mm(coefficient, oh[:, col]) * xf
        zf = z[:, col].astype(F32)
        sigma = 1.0 / (1.0 + jnp.exp(-zf))
        gate = zf * sigma
        gated = y * gate
        scaled = gated * scale
        gf = g[:, col].astype(F32)
        normed[:, col] = (scaled * gain[:, col]).astype(BF16)
        gpart[:, col] += jnp.sum(gf * scaled, axis=0, keepdims=True)
        grad = gf * gain[:, col] * scale - gated * factor
        zgrad[:, col] = (grad * y * (sigma + gate * (1.0 - sigma))).astype(BF16)
        dy = grad * gate
        high, low = split(dy)
        dyh[:, col] = high
        dyl[:, col] = low
        high, low = split(dy * mm(inflow, oh[:, col]))
        back = decs[0, :, col] * state[:, col] + (mm_tn(c[...], high) + mm_tn(c[...], low))
        state[:, col] = back
        starts[0, :, col] = back

    @pl.when(turn == pl.num_programs(0) - 1)
    def _():
        chunk = own_grad.shape[2]
        for k in range(own_grad.shape[0]):
            own_grad[k] = state[:, k * chunk : (k + 1) * chunk]


def diagonal_back_kernel(lengths, offset, cum, rows, step, x, b, c, dyh, dyl, yp, sin, ends, prefix, oh, dskip, *rest, part, last):
    count = 5 if part else 0
    before, xpart, after = rest[:count], rest[count], rest[count + 1 :]
    block = pl.program_id(0)
    seg_column, seg_row, prior, _ = segments(lengths, offset, block)
    mask = (seg_column == seg_row) & (iota((BLOCK, BLOCK), 1) > iota((BLOCK, BLOCK), 0))
    scores = mm_nt(b[...], c[...])
    left = iota((BLOCK, LANES), 1) < HEADDIM
    sums = [value[...] for value in before] if part else [jnp.zeros((BLOCK, LANES), F32)] * 5
    score_grad, carried_c, rho1, rho2, rho3 = sums
    own_score = jnp.sum(b[...].astype(F32) * c[...].astype(F32), axis=1, keepdims=True)
    coefficient = pieces(head_rows(dskip[...], dskip.shape[1]) + step[...] * own_score)
    step_pieces = pieces(step[...])
    du_pairs = []
    inflow = pieces(jnp.exp(cum[...]) * (seg_column == prior).astype(F32))
    pairs = x.shape[1] // LANES
    for pair in range(pairs):
        col = slice(pair * LANES, (pair + 1) * LANES)
        pair_x, high_dy, low_dy = x[:, col], dyh[:, col], dyl[:, col]
        zero = jnp.zeros_like(pair_x)
        top = jnp.concatenate([jnp.where(left, high_dy, zero), jnp.where(left, low_dy, zero)], axis=1)
        bottom = jnp.concatenate([jnp.where(left, zero, high_dy), jnp.where(left, zero, low_dy)], axis=1)
        both = jnp.concatenate([top, bottom], axis=0)
        products = mm_nt(jnp.concatenate([pair_x, pair_x], axis=1), both)
        parts = []
        for e in (0, 1):
            h = 2 * (part * pairs + pair) + e
            gap = rows[0, h : h + 1, :] - cum[:, h : h + 1]
            decay = jnp.where(mask, jnp.exp(jnp.minimum(gap, 0.0)), 0.0)
            score_grad = score_grad + decay * products[:, e * BLOCK : (e + 1) * BLOCK] * step[:, h : h + 1]
            parts.append(split(decay * scores))
        high = mm(jnp.concatenate([parts[0][0], parts[1][0]], axis=1), both)
        low = mm(jnp.concatenate([parts[0][1], parts[1][1]], axis=1), both[:, :LANES])
        du_pairs.append(high[:, :LANES] + (high[:, LANES:] + low))
    dy = dyh[...].astype(F32) + dyl[...].astype(F32)
    du = jnp.concatenate(du_pairs, axis=1)
    xf = x[...].astype(F32)
    high, low = split(dy * mm(inflow, oh[...]))
    entering = jnp.where(block == 0, sin[...], ends[0] + prefix[0] * sin[...])
    s_high, s_low = split(entering)
    carried_c = carried_c + (mm_nt(high, s_high) + (mm_nt(low, s_high) + mm_nt(high, s_low)))
    xpart[...] = mm(step_pieces, oh[...]) * du + mm(coefficient, oh[...]) * dy
    high, low = split(dy * yp[...])
    rho1 = rho1 + (mm_nt(high, oh[...]) + mm_nt(low, oh[...]))
    high, low = split(xf * du)
    rho2 = rho2 + (mm_nt(high, oh[...]) + mm_nt(low, oh[...]))
    high, low = split(dy * xf)
    rho3 = rho3 + (mm_nt(high, oh[...]) + mm_nt(low, oh[...]))
    if last:
        lane = iota((BLOCK, LANES), 1)
        own = jnp.sum(jnp.where(lane < GROUP, rho3 * step[...], 0.0), axis=1, keepdims=True)
        high, low = split(score_grad)
        score_grad = mm(high, c[...]) + mm(low, c[...]) + own * c[...].astype(F32)
        carried_c = carried_c + (mm_tn(high, b[...]) + mm_tn(low, b[...])) + own * b[...].astype(F32)
    for ref, value in zip(after, (score_grad, carried_c, rho1, rho2, rho3)):
        ref[...] = value


def input_kernel(lengths, offset, sout, sin, starts, decs, ends, prefix, cum, step, x, b, part0, part1, oh, *rest, final):
    if final:
        _, db_in, scaled_in, inner_in, c, rho1, rho2, rho3, sig, alog, dbd, dc_mine, dc_other, gpart0, gpart1 = rest[:15]
        xgrad, db, dc, draw, sums, state, run, small = rest[15:]
    else:
        xgrad, db, scaled_out, inner_out, state, run = rest
    turn = pl.program_id(0)
    block = pl.num_programs(0) - 1 - turn

    @pl.when(turn == 0)
    def _():
        state[...] = sout[...]
        run[...] = jnp.ones_like(run)
        if final:
            small[...] = jnp.zeros_like(small)

    segment, _, prior, last = segments(lengths, offset, block)
    steps = step[...]
    weights, _ = weigh(cum[...], steps, segment, prior, last)
    scaled = scaled_in[...] if final else jnp.zeros((BLOCK, LANES), F32)
    carried_b = db_in[...] if final else jnp.zeros((BLOCK, STATE), F32)
    inner = inner_in[0] if final else jnp.zeros((8, LANES), F32)
    span = part0.shape[1]
    for at, part in ((0, part0), (span, part1)):
        col = slice(at, at + span)
        leaving = state[:, col]
        s_high, s_low = split(leaving)
        wide = mm(weights, oh[:, col])
        xf = x[:, col].astype(F32)
        du = wide * (mm(b[...], s_high) + mm(b[...], s_low))
        xgrad[:, col] = (part[...] + du).astype(BF16)
        high, low = split(xf * du)
        scaled = scaled + (mm_nt(high, oh[:, col]) + mm_nt(low, oh[:, col]))
        high, low = split(xf * wide)
        carried_b = carried_b + (mm_nt(high, s_high) + (mm_nt(low, s_high) + mm_nt(high, s_low)))
        whole = ends[0, :, col] + prefix[0, :, col] * sin[:, col]
        overlap = jnp.sum((whole * leaving).reshape(STATE // 8, 8, span), axis=0)
        high, low = split(overlap)
        inner = inner + (mm_nt(high, oh[:, col]) + mm_nt(low, oh[:, col]))
        product = run[:, col] * decs[0, :, col]
        run[:, col] = product
        state[:, col] = starts[0, :, col] + product * sout[:, col]
    if not final:
        db[...] = carried_b
        scaled_out[...] = scaled
        inner_out[0] = inner
        return
    db[...] = dbd[...] + carried_b
    dc[...] = dc_mine[...] + dc_other[...]
    own = jnp.sum(b[...].astype(F32) * c[...].astype(F32), axis=1, keepdims=True)
    second = rho2[...] + jnp.where(steps > 0.0, scaled / steps, 0.0)
    upper = (iota((BLOCK, BLOCK), 1) >= iota((BLOCK, BLOCK), 0)).astype(F32)
    rate_grad = jnp.dot(upper, rho1[...] - steps * rho2[...] - scaled, precision=HIGHEST, preferred_element_type=F32)
    rate_grad = rate_grad + jnp.sum(inner, axis=0, keepdims=True)
    speed = jnp.exp(head_rows(alog[...], alog.shape[1]))
    raw_grad = (second + own * rho3[...] - speed * rate_grad) * sig[...]
    draw[...] = raw_grad.T[: draw.shape[0]]
    row = iota((8, LANES), 0)
    bias_row = jnp.where(row == 0, jnp.sum(raw_grad, axis=0, keepdims=True), 0.0)
    alog_row = jnp.where(row == 1, jnp.sum(rate_grad * steps * -speed, axis=0, keepdims=True), 0.0)
    skip_row = jnp.where(row == 2, jnp.sum(rho3[...], axis=0, keepdims=True), 0.0)
    small[...] += bias_row + alog_row + skip_row

    @pl.when(turn == pl.num_programs(0) - 1)
    def _():
        rows = gpart0.shape[1] // LANES
        for k in range(sums.shape[0]):
            sums[k, :8] = small[...]
            for r in range(rows):
                sums[k, 8 + r : 9 + r] = gpart0[:, r * LANES : (r + 1) * LANES]
                sums[k, 8 + rows + r : 9 + rows + r] = gpart1[:, r * LANES : (r + 1) * LANES]


def relay(own, total, axis, forward, work):
    count = lax.axis_size(axis)
    index = lax.axis_index(axis)
    rank = index if forward else count - 1 - index
    chunks = 2 * HALF_CHUNKS
    steps = chunks + LAG * (count - 2)
    received, halves, message = [], None, None

    def chunk(pair, at):
        picked = [lax.dynamic_index_in_dim(v, jnp.clip(at - k * HALF_CHUNKS, 0, HALF_CHUNKS - 1), 0, False) for k, v in enumerate(pair)]
        return jnp.where(at < HALF_CHUNKS, picked[0], picked[1])

    def half(which):
        turns = received[: steps - LAG] if which == 0 else received
        stacked = jnp.stack(turns)
        at = [k + which * HALF_CHUNKS + LAG * (rank - 1) for k in range(HALF_CHUNKS)]
        picked = [lax.dynamic_index_in_dim(stacked, jnp.clip(k, 0, len(turns) - 1), 0, False) for k in at]
        return jnp.where(rank > 0, jnp.concatenate(picked, axis=1), 0.0)

    for turn in range(steps):
        if turn < LAG:
            mine = own[turn]
            if message is not None:
                mine, _ = lax.optimization_barrier((mine, message))
        else:
            at = jnp.clip(turn - LAG * rank, 0, chunks - 1)
            arrived, _ = lax.optimization_barrier((received[turn - LAG], message))
            mine = chunk(halves[0], at) + chunk(halves[1], at) * arrived
        message = mine
        ranks = [r for r in range(count - 1) if 0 <= turn - LAG * r < chunks]
        pairs = [(r, r + 1) if forward else (count - 1 - r, count - 2 - r) for r in ranks]
        received.append(lax.ppermute(message, axis, pairs))
        if turn == LAG - 1:
            second = work(0, message, None)
            halves = (own, second[0]), (total, second[1])
        elif turn == steps - 1:
            first = half(0)
            work(-1, message, first)
        elif turn % LAG == LAG - 1 and turn < 6:
            work(turn // LAG, message, None)
    return first, half(1)


def one_hot(width):
    lane = np.arange(LANES)[:, None]
    return np.logical_and(lane % GROUP == np.arange(width)[None, :] // HEADDIM, lane < 3 * GROUP)


def shards(x, z, b, c, raw, lengths, bias, alog, dskip, gain, grad):
    _, tokens, width = x.shape
    heads = width // HEADDIM
    blocks = tokens // BLOCK
    span, quarter = width // 2, width // 4
    chunk = span // HALF_CHUNKS
    x, z, grad = (v.reshape(tokens, width) for v in (x, z, grad))
    b, c = b.reshape(tokens, STATE), c.reshape(tokens, STATE)
    raw = raw.reshape(tokens, heads).T
    lengths = lengths.reshape(-1)
    bias, alog, dskip = (v.reshape(1, heads) for v in (bias, alog, dskip))
    gain = gain.reshape(1, width)
    offset = jnp.reshape(lax.axis_index("seq") * tokens, (1,)).astype(jnp.int32)
    oh = jnp.asarray(one_hot(width), BF16)

    def tied(message):
        return [("smem", lengths), ("smem", lax.optimization_barrier((offset, message))[0])]

    def call(kernel, reverse, ins, outs, scratch, name, aliases=None):
        place = (lambda i: blocks - 1 - i) if reverse else (lambda i: i)

        def spec(kind, shape):
            kind, step, at = kind if isinstance(kind, tuple) else (kind, shape[-1], 0)
            if kind == "smem":
                return pl.BlockSpec(memory_space=pltpu.SMEM)
            if kind == "any":
                return pl.BlockSpec(memory_space=pl.ANY)
            if kind == "tok":
                return pl.BlockSpec((BLOCK, step), lambda i: (place(i), at))
            if kind == "blk":
                return pl.BlockSpec((1, shape[1], step), lambda i: (place(i), 0, at))
            if kind == "prev":
                return pl.BlockSpec((1, shape[1], step), lambda i: (jnp.maximum(place(i) - 1, 0), 0, at))
            if kind == "raw":
                return pl.BlockSpec((shape[0], BLOCK), lambda i: (0, place(i)))
            if kind == "row":
                return pl.BlockSpec((2, GROUP, BLOCK), lambda i: (0, 0, place(i)))
            return pl.BlockSpec(tuple(shape[:-1]) + (step,), lambda i: (0,) * (len(shape) - 1) + (at,))

        return pl.pallas_call(
            kernel,
            grid=(blocks,),
            in_specs=[spec(kind, value.shape) for kind, value in ins],
            out_specs=[spec(kind, shape) for kind, shape, _ in outs],
            out_shape=[jax.ShapeDtypeStruct(shape, dtype) for _, shape, dtype in outs],
            scratch_shapes=[pltpu.VMEM(shape, F32) for shape in scratch],
            input_output_aliases=aliases or {},
            compiler_params=pltpu.CompilerParams(
                dimension_semantics=("arbitrary",), vmem_limit_bytes=VMEM_LIMIT
            ),
            name=name,
        )(*[value for _, value in ins])

    wide = (tokens, width)
    half = (tokens, span)
    narrow = (tokens, LANES)
    states = (blocks, STATE, span)
    line = (blocks, 1, span)
    own_outs = [("all", (HALF_CHUNKS, STATE, chunk), F32), ("all", (HALF_CHUNKS, 1, chunk), F32), ("blk", states, F32),
                ("blk", line, F32), ("blk", line, F32)]
    first = call(
        prepare_kernel, False,
        [("smem", lengths), ("smem", offset), ("raw", raw), ("all", bias), ("all", alog), (("tok", span, 0), x), ("tok", b), (("all", span, 0), oh)],
        own_outs + [("tok", narrow, F32), ("tok", narrow, F32), ("tok", narrow, F32), ("row", (2, GROUP, tokens), F32)],
        [(STATE, span), (1, span)], "prepare",
    )
    step, cum, sig, rows = first[5:]
    locals_ = [first[:5], None]
    diag, sin, yp, stats = [None, None], [None, None], [None, None], None

    def diagonal(where, h):
        (diag[h],) = call(
            partial(diagonal_kernel, first=h * heads // 2), False,
            where + [("tok", cum), ("row", rows), (("tok", span, h), x), ("tok", b), ("tok", c)],
            [("tok", half, F32)], [], "diagonal",
        )

    def output(where, h):
        kernel = output_kernel if h else (lambda *refs: output_kernel(*refs[:16], None, *refs[16:]))
        _, _, ends, _, prefix = locals_[h]
        yp[h], total = call(
            kernel, False,
            where + [("all", sin[h]), ("blk", ends), ("blk", prefix), ("tok", cum), ("tok", step)]
            + [(("tok", span, h), v) for v in (x, z, grad)]
            + [("tok", b), ("tok", c), ("tok", diag[h]), ("all", dskip), (("all", span, h), gain), (("all", span, h), oh)]
            + ([("tok", stats)] if h else []),
            [("tok", half, F32), ("tok", narrow, F32)], [(STATE, span)], "output",
        )
        return total

    def forward_work(slot, message, arrived):
        nonlocal stats
        where = tied(message)
        if slot == 0:
            locals_[1] = call(
                states_kernel, False,
                where + [("tok", cum), ("tok", step), (("tok", span, 1), x), ("tok", b), (("all", span, 1), oh)],
                own_outs, [(STATE, span), (1, span)], "states",
            )
            diagonal(where, 0)
            return locals_[1]
        if slot == 1:
            diagonal(where, 1)
        if slot == -1:
            sin[0] = arrived
            stats = output(where, 0)

    _, sin[1] = relay(locals_[0][0], locals_[0][1], "seq", True, forward_work)
    plain = [("smem", lengths), ("smem", offset)]
    stats = output(plain, 1)
    exchange = partial(lax.ppermute, axis_name="head", perm=[(0, 1), (1, 0)])
    other = exchange(stats)
    total_width = float(width * lax.axis_size("head"))
    norms = [None, None]

    def norm(where, h):
        kernel = partial(norm_kernel, total_width=total_width)
        ins = where + [("tok", stats), ("tok", other), ("tok", cum), ("tok", step)]
        ins = ins + [(("tok", span, h), v) for v in (x, z, grad)]
        ins = ins + [("tok", b), ("tok", c), ("tok", yp[h]), ("all", dskip), (("all", span, h), gain), (("all", span, h), oh), ("blk", locals_[h][3])]
        aliases = {}
        if h:
            aliases = {len(ins): 0, len(ins) + 1: 1}
            ins = ins + [("any", v) for v in norms[0][:2]]
        else:
            inner = kernel
            kernel = lambda *refs: inner(*refs[:16], None, None, *refs[16:])
        norms[h] = call(
            kernel, True, ins,
            [(("tok", span, h), wide, BF16), (("tok", span, h), wide, BF16), ("tok", half, BF16), ("tok", half, BF16),
             ("all", (1, span), F32), ("blk", states, F32), ("all", (HALF_CHUNKS, STATE, chunk), F32)],
            [(STATE, span)], "norm", aliases,
        )

    norm(plain, 0)
    xparts, carry, partly = [], [], []

    def back(where, q):
        h, sub = q // 2, q % 2
        _, _, ends, _, prefix = locals_[h]
        _, _, dyh, dyl = norms[h][:4]
        out = call(
            partial(diagonal_back_kernel, part=q, last=q == 3), False,
            where + [("tok", cum), ("row", rows), ("tok", step), (("tok", quarter, q), x), ("tok", b), ("tok", c)]
            + [(("tok", quarter, sub), v) for v in (dyh, dyl, yp[h])]
            + [(("all", quarter, sub), sin[h]), (("prev", quarter, sub), ends), (("prev", quarter, sub), prefix), (("all", quarter, q), oh), ("all", dskip)]
            + [("tok", value) for value in carry],
            [("tok", (tokens, quarter), F32)] + [("tok", narrow, F32)] * 5, [], "diagonal_back",
        )
        xparts.append(out[0])
        carry[:] = out[1:]

    def entry(where, h, sout, more):
        _, _, ends, decs, prefix = locals_[h]
        return where + [("all", sout), ("all", sin[h]), ("blk", norms[h][5]), ("blk", decs), ("blk", ends), ("blk", prefix), ("tok", cum),
                        ("tok", step), (("tok", span, h), x), ("tok", b), ("tok", xparts[2 * h]), ("tok", xparts[2 * h + 1]),
                        (("all", span, h), oh)] + more

    def backward_work(slot, message, arrived):
        where = tied(message)
        if slot == 0:
            norm(where, 1)
            back(where, 0)
            return norms[1][6], locals_[1][1]
        if slot == -1:
            back(where, 3)
            partly[:] = call(
                partial(input_kernel, final=False), True, entry(where, 0, arrived, []),
                [(("tok", span, 0), wide, BF16), ("tok", narrow, F32), ("tok", narrow, F32), ("blk", (blocks, 8, LANES), F32)],
                [(STATE, span), (1, span)], "input",
            )
            return
        back(where, slot)

    _, sout = relay(norms[0][6], locals_[0][1], "seq", False, backward_work)
    dbd, dc, rho1, rho2, rho3 = carry
    dc_other = exchange(dc)
    members = lax.axis_size(("seq", "batch"))
    ins = entry(plain, 1, sout, [
        ("any", partly[0]), ("tok", partly[1]), ("tok", partly[2]), ("blk", partly[3]), ("tok", c), ("tok", rho1), ("tok", rho2), ("tok", rho3),
        ("tok", sig), ("all", alog), ("tok", dbd), ("tok", dc), ("tok", dc_other), ("all", norms[0][4]), ("all", norms[1][4]),
    ])
    xgrad, db, dc, draw, sums = call(
        partial(input_kernel, final=True), True, ins,
        [(("tok", span, 1), wide, BF16), ("tok", narrow, F32), ("tok", narrow, F32), ("raw", (heads, tokens), F32),
         ("all", (members, 8 + width // LANES, LANES), F32)],
        [(STATE, span), (1, span), (8, LANES)], "input_last", {15: 0},
    )
    db = db + exchange(db)
    sums = jnp.sum(lax.all_to_all(sums, ("seq", "batch"), 0, 0), axis=0)
    return (
        norms[1][0][None],
        xgrad[None],
        norms[1][1][None],
        db[None],
        dc[None],
        draw.T[None],
        sums[0, :heads],
        sums[1, :heads],
        sums[2, :heads],
        sums[8:].reshape(width),
    )


def solution(mesh):
    wide = P(("groups", "batch"), "seq", "head")
    shared = P(("groups", "batch"), "seq", None)
    part = P(("groups", "head"))
    head = P("head")
    return jax.shard_map(
        shards,
        mesh=mesh,
        in_specs=(wide, wide, shared, shared, wide, P(("groups", "batch"), None), head, head, head, head, wide),
        out_specs=(wide, wide, wide, shared, shared, wide, part, part, part, part),
        check_vma=False,
    )
```

time: 150 us -> 159 us (1.060)
  waiting for transfers between devices: 41.3 us -> 17.6 us
  Pallas kernels: 69.7 us -> 91.4 us
  starting transfers between devices: 25.1 us -> 29.6 us
  other arithmetic: 4.96 us -> 8.63 us
    ppermute x16, waiting for transfers between devices: 32.6 us -> 8.94 us  [relay(): received.append(lax.ppermute(message, axis, pairs))]
    pallas_call x8 -> x14, Pallas kernels: 69.7 us -> 91.4 us  [call(): pl.pallas_call(kernel, grid=(blocks,), in_specs=[spec(kind, value.shape)...]
    all_to_all x1, starting transfers between devices: 3.37 us -> 8.73 us  [shards(): sums = jnp.sum(lax.all_to_all(sums, ('seq', 'batch'), 0, 0), axis=0)]
    add x12, other arithmetic: 0.33 us -> 3.65 us  [relay(): mine = chunk(halves[0], at) + chunk(halves[1], at) * arrived]
    unnamed x26 -> x32, local copies, waits for them, and re-layouts: 1.63 us -> 4.46 us
    select_n x4 -> x7, other arithmetic: 1.99 us -> 3.28 us  [the longest x4 3.13 us: half(): return jnp.where(rank > 0, jnp.concatenate(picked, axis=1), 0.0)]
  transfers between devices with their start and end apart: 20 -> 20, of which waited for: 8 -> 5; matrix products, arithmetic and copies ran while one was open for 2% -> 7% of each run, Pallas kernels for 17% -> 40%
where the time goes in v3:
time: 159 us; the launch traced here: 157 us
  Pallas kernels  91.4 us (57%)
  starting transfers between devices  29.6 us (19%)
  waiting for transfers between devices  17.6 us (11%)
  other arithmetic  8.63 us (5%)
  local copies, waits for them, and re-layouts  8.52 us (5%)
    pallas_call x14, Pallas kernels, call(): pl.pallas_call(kernel, grid=(blocks,), in_specs=[spec(kind, value.shape)...  91.4 us
    ppermute x16, starting transfers between devices, relay(): received.append(lax.ppermute(message, axis, pairs))  20.5 us
    ppermute x16, waiting for transfers between devices, relay(): received.append(lax.ppermute(message, axis, pairs))  8.94 us
    all_to_all x1, starting transfers between devices, shards(): sums = jnp.sum(lax.all_to_all(sums, ('seq', 'batch'), 0, 0), axis=0)  8.73 us
    all_to_all x1, waiting for transfers between devices, shards(): sums = jnp.sum(lax.all_to_all(sums, ('seq', 'batch'), 0, 0), axis=0)  6.94 us
    unnamed x32, local copies, waits for them, and re-layouts  4.46 us
    add x12, other arithmetic, relay(): mine = chunk(halves[0], at) + chunk(halves[1], at) * arrived  3.65 us
  transfers between devices with their start and end apart: 20, of which 5 were waited for; matrix products, arithmetic and copies ran while one was open for 7% of the time, Pallas kernels for 40%

profile of v3, /device:TPU:0, one launch (start us, length us, event | category | flops | bytes accessed | tf_op | source)
XLA Modules:
  0.0 157.1 jit_solution(7325041700037432122)
XLA Ops:
  0.7 7.0 %prepare.1 = (f32[2,128,384]{2,1,0:T(8,128)}, f32[2,1,384]{2,1,0:T(1,128)}, f32[4,128,768]{2,1,0:T(8,128)}, f32[4,1,768]{2,1,0:T(1,128)}, f32[4,1,768]{2,1,0:T(1...) custom-call(s32[2]{0:T(128)} %bitcast.172, ...), custom_call_target="tpu_custom_call" | custom-call | tf_op jit(solution)/shard_map/prepare/pallas_call | solution.py:467
  7.6 1.1 slice_bitcast_fusion.2
  8.7 4.9 %collective-permute-start = (f32[128,384]{1,0:T(8,128)S(1)}, f32[128,384]{1,0:T(8,128)S(1)}, u32[]{:S(2)}, u32[]{:S(2)}) collective-permute-start(f32[128,384]{1,0:T(8,128)S(1)} %get-tuple-element.205), channel_id=1, source_target_pairs={{0,4},{1,5},{2,6},{3,7},{16,20},{17,21},{18,22},{19,23}} | collective-permute-start | bytes 589832 | tf_op jit(solution)/shard_map/ppermute | solution.py:411
  13.6 1.3 collective-permute-start.1
  15.0 0.6 reshape.262.refs_14_.gain.refs_13_
  15.6 5.1 %states.1 = (f32[2,128,384]{2,1,0:T(8,128)}, f32[2,1,384]{2,1,0:T(1,128)}, f32[4,128,768]{2,1,0:T(8,128)}, f32[4,1,768]{2,1,0:T(1,128)}, f32[4,1,768]{2,1,0:T(1,128)}) custom-call(s32[2]{0:T(128)} %bitcast.173, s32[1]{0:T(128)} %bitcast.1.offset.refs_1_, f32[512,128]{1,0:T(8,128)} %get-tuple-element.99.cum.refs_5_.refs_4_, ...), custom_call_target="tpu_custom_call" | custom-call | tf_op jit(solution)/shard_map/states/pallas_call | solution.py:467
  20.8 0.0 copy-start.7
  20.8 0.0 copy-start.1
  20.8 0.0 copy-start.3
  20.8 4.7 %diagonal.3.refs_12_ = f32[512,768]{1,0:T(8,128)} custom-call(s32[2]{0:T(128)} %bitcast.174, s32[1]{0:T(128)} %bitcast.1.offset.refs_1_, f32[512,128]{1,0:T(8,128)} %get-tuple-element.99.cum.refs_5_.refs_4_, f32[2,32,512]{2,1,0:T(8,128)} %get-tuple-element.113.rows, bf16[512,1536]{1,0:T(8,128)(2,1)} %bitcast.124, bf16[512,128]{1,0:T(8,128)(2,1)} %bitcast.138, ...), custom_call_target="tpu_custom_call" | custom-call | tf_op jit(solution)/shard_map/diagonal/pallas_call | solution.py:467
  25.5 0.1 fusion.6
  25.7 1.3 collective-permute-start.2
  27.0 2.2 %collective-permute-start.3 = (f32[128,384]{1,0:T(8,128)S(1)}, f32[128,384]{1,0:T(8,128)S(1)}, u32[]{:S(2)}, u32[]{:S(2)}) collective-permute-start(f32[128,384]{1,0:T(8,128)S(1)} %bitcast_add_fusion.10), channel_id=1, source_target_pairs={{0,4},{4,8},{1,5},{5,9},{2,6},{6,10},{3,7},{7,11},{16,20},{20,24},... | collective-permute-start | bytes 589832 | tf_op jit(solution)/shard_map/ppermute | solution.py:411
  29.3 4.6 %diagonal.2.diag = f32[512,768]{1,0:T(8,128)} custom-call(s32[2]{0:T(128)} %bitcast.175, s32[1]{0:T(128)} %bitcast.1.offset.refs_1_, f32[512,128]{1,0:T(8,128)} %get-tuple-element.99.cum.refs_5_.refs_4_, f32[2,32,512]{2,1,0:T(8,128)} %get-tuple-element.113.rows, bf16[512,1536]{1,0:T(8,128)(2,1)} %bitcast.125, bf16[512,128]{1,0:T(8,128)(2,1)} %bitcast.139, ...), custom_call_target="tpu_custom_call" | custom-call | tf_op jit(solution)/shard_map/diagonal/pallas_call | solution.py:467
  34.0 0.7 collective-permute-start.4
  34.7 0.6 collective-permute-done.3
  35.4 0.7 collective-permute-start.5
  36.2 0.7 collective-permute-start.6
  36.9 0.7 collective-permute-start.7
  37.7 0.8 maximum_select_fusion.1.refs_2_.sin
  38.5 5.9 %output.2 = (f32[512,768]{1,0:T(8,128)}, f32[512,128]{1,0:T(8,128)}) custom-call(s32[2]{0:T(128)} %bitcast.176, s32[1]{0:T(128)} %bitcast.1.offset.refs_1_, f32[128,768]{1,0:T(8,128)} %maximum_select_fusion.1.refs_2_.sin, f32[4,128,768]{2,1,0:T(8,128)} %get-tuple-element.115.refs_3_.ends, f32[4,1,768]{2,1,0:T(1,128)} %get-tuple-element.116.refs_4_.prefix, ...), custom_call_target="tpu_custom_call" | custom-call | tf_op jit(solution)/shard_map/output/pallas_call | solution.py:467
  44.5 0.8 maximum_select_fusion.sin
  45.3 6.0 %output.3 = (f32[512,768]{1,0:T(8,128)}, f32[512,128]{1,0:T(8,128)}) custom-call(s32[2]{0:T(128)} %bitcast.177, s32[1]{0:T(128)} %bitcast.1.offset.refs_1_, f32[128,768]{1,0:T(8,128)} %maximum_select_fusion.sin, f32[4,128,768]{2,1,0:T(8,128)} %get-tuple-element.110.ends, f32[4,1,768]{2,1,0:T(1,128)} %get-tuple-element.111.prefix, ...), custom_call_target="tpu_custom_call" | custom-call | tf_op jit(solution)/shard_map/output/pallas_call | solution.py:467
  51.3 0.1 collective-permute-start.8
  51.4 1.7 %collective-permute-done.8.refs_3_.other = f32[512,128]{1,0:T(8,128)S(1)} collective-permute-done((f32[512,128]{1,0:T(8,128)}, f32[512,128]{1,0:T(8,128)S(1)}, u32[]{:S(2)}, u32[]{:S(2)}) %collective-permute-start.8) | collective-permute-done | bytes 262176 | tf_op jit(solution)/shard_map/ppermute | solution.py:539
  53.1 0.7 copy-done.4
  53.8 7.5 %norm.2 = (bf16[512,1536]{1,0:T(8,128)(2,1)}, bf16[512,1536]{1,0:T(8,128)(2,1)}, bf16[512,768]{1,0:T(8,128)(2,1)}, bf16[512,768]{1,0:T(8,128)(2,1)}, f32[1,768]{...) custom-call(s32[2]{0:T(128)} %bitcast.178, s32[1]{0:T(128)} %bitcast.1.offset.refs_1_, ...), custom_call_target="tpu_custom_call" | custom-call | tf_op jit(solution)/shard_map/norm/pallas_call | solution.py:467
  61.3 1.0 slice_bitcast_fusion
  62.4 0.7 collective-permute-start.9
  63.1 0.1 fusion.11
  63.2 0.7 collective-permute-start.10
  63.9 6.7 %diagonal_back.4 = (f32[512,384]{1,0:T(8,128)}, f32[512,128]{1,0:T(8,128)}, f32[512,128]{1,0:T(8,128)}, f32[512,128]{1,0:T(8,128)}, f32[512,128]{1,0:T(8,128)}, /*index=5*/f32[512,128]{1,0:T(8,128)}) custom-call(s32[2]{0:T(128)} %bitcast.179, s32[1]{0:T(128)} %bitcast.1.offset.refs_1_, f32[512,128]{1,0:T(8,128)} %get-tuple-element.99.cum.refs_5_.refs_4_, ...), custom_call_target="tpu_custom_call" | custom-call | tf_op jit(solution)/shard_map/diagonal_back/pallas_call | solution.py:467
  70.5 7.6 %norm.3 = (bf16[512,1536]{1,0:T(8,128)(2,1)}, bf16[512,1536]{1,0:T(8,128)(2,1)}, bf16[512,768]{1,0:T(8,128)(2,1)}, bf16[512,768]{1,0:T(8,128)(2,1)}, f32[1,768]{...) custom-call(s32[2]{0:T(128)} %bitcast.180, ...), custom_call_target="tpu_custom_call", output_to_operand_aliasing={{0}: (16, {}), {1}: (17, {})} | custom-call | tf_op jit(solution)/shard_map/norm/pallas_call | solution.py:467
  78.2 1.0 bitcast_add_fusion.5
  79.1 0.7 collective-permute-start.11
  79.8 1.0 bitcast_add_fusion.4
  80.8 0.7 collective-permute-start.12
  81.5 6.8 %diagonal_back.5 = (f32[512,384]{1,0:T(8,128)}, f32[512,128]{1,0:T(8,128)}, f32[512,128]{1,0:T(8,128)}, f32[512,128]{1,0:T(8,128)}, f32[512,128]{1,0:T(8,128)}, /*index=5*/f32[512,128]{1,0:T(8,128)}) custom-call(s32[2]{0:T(128)} %bitcast.181, s32[1]{0:T(128)} %bitcast.1.offset.refs_1_, f32[512,128]{1,0:T(8,128)} %get-tuple-element.99.cum.refs_5_.refs_4_, ...), custom_call_target="tpu_custom_call" | custom-call | tf_op jit(solution)/shard_map/diagonal_back/pallas_call | solution.py:467
  88.3 0.7 bitcast_dynamic-update-slice_fusion.12
  89.0 0.7 bitcast_dynamic-update-slice_fusion.10
  89.7 1.3 collective-permute-start.13
  91.1 1.3 collective-permute-start.14
  92.4 6.8 %diagonal_back.6 = (f32[512,384]{1,0:T(8,128)}, f32[512,128]{1,0:T(8,128)}, f32[512,128]{1,0:T(8,128)}, f32[512,128]{1,0:T(8,128)}, f32[512,128]{1,0:T(8,128)}, /*index=5*/f32[512,128]{1,0:T(8,128)}) custom-call(s32[2]{0:T(128)} %bitcast.182, s32[1]{0:T(128)} %bitcast.1.offset.refs_1_, f32[512,128]{1,0:T(8,128)} %get-tuple-element.99.cum.refs_5_.refs_4_, ...), custom_call_target="tpu_custom_call" | custom-call | tf_op jit(solution)/shard_map/diagonal_back/pallas_call | solution.py:467
  99.2 0.7 bitcast_dynamic-update-slice_fusion.8
  99.9 0.7 bitcast_dynamic-update-slice_fusion.6
  100.6 6.1 %collective-permute-done.13 = f32[128,384]{1,0:T(8,128)S(1)} collective-permute-done((f32[128,384]{1,0:T(8,128)S(1)}, f32[128,384]{1,0:T(8,128)S(1)}, u32[]{:S(2)}, u32[]{:S(2)}) %collective-permute-start.13) | collective-permute-done | bytes 196640 | tf_op jit(solution)/shard_map/ppermute | solution.py:411
  106.7 0.7 bitcast_add_fusion.1
  107.4 1.3 collective-permute-start.15
  108.7 2.2 %collective-permute-done.14 = f32[128,384]{1,0:T(8,128)S(1)} collective-permute-done((f32[128,384]{1,0:T(8,128)S(1)}, f32[128,384]{1,0:T(8,128)S(1)}, u32[]{:S(2)}, u32[]{:S(2)}) %collective-permute-start.14) | collective-permute-done | bytes 196640 | tf_op jit(solution)/shard_map/ppermute | solution.py:411
  110.9 0.7 bitcast_add_fusion
  111.6 1.5 collective-permute-start.16
  113.1 7.1 %diagonal_back.7 = (f32[512,384]{1,0:T(8,128)}, f32[512,128]{1,0:T(8,128)}, f32[512,128]{1,0:T(8,128)}, f32[512,128]{1,0:T(8,128)}, f32[512,128]{1,0:T(8,128)}, /*index=5*/f32[512,128]{1,0:T(8,128)}) custom-call(s32[2]{0:T(128)} %bitcast.183, s32[1]{0:T(128)} %bitcast.1.offset.refs_1_, f32[512,128]{1,0:T(8,128)} %get-tuple-element.99.cum.refs_5_.refs_4_, ...), custom_call_target="tpu_custom_call" | custom-call | tf_op jit(solution)/shard_map/diagonal_back/pallas_call | solution.py:467
  120.3 0.1 collective-permute-start.17
  120.5 0.8 maximum_select_fusion.3.sout
  121.3 7.2 %input.1 = (bf16[512,1536]{1,0:T(8,128)(2,1)}, f32[512,128]{1,0:T(8,128)}, f32[512,128]{1,0:T(8,128)}, f32[4,8,128]{2,1,0:T(8,128)}) custom-call(s32[2]{0:T(128)} %bitcast.184, s32[1]{0:T(128)} %bitcast.1.offset.refs_1_, f32[128,768]{1,0:T(8,128)} %maximum_select_fusion.3.sout, f32[128,768]{1,0:T(8,128)} %maximum_select_fusion.1.refs_2_.sin, ...), custom_call_target="tpu_custom_call" | custom-call | tf_op jit(solution)/shard_map/input/pallas_call | solution.py:467
  128.5 0.8 maximum_select_fusion.2.sout
  129.4 0.7 copy-done.5
  130.0 8.3 %input_last.1 = (bf16[512,1536]{1,0:T(8,128)(2,1)}, f32[512,128]{1,0:T(8,128)}, f32[512,128]{1,0:T(8,128)}, f32[24,512]{1,0:T(8,128)}, f32[8,20,128]{2,1,0:T(8,128)}) custom-call(s32[2]{0:T(128)} %bitcast.185, s32[1]{0:T(128)} %bitcast.1.offset.refs_1_, f32[128,768]{1,0:T(8,128)} %maximum_select_fusion.2.sout, ...), custom_call_target="tpu_custom_call", output_to_operand_aliasing={{0}: (15, {})} | custom-call | tf_op jit(solution)/shard_map/input_last/pallas_call | solution.py:467
  138.4 8.7 %all-to-all-start = ((f32[8,20,128]{2,1,0:T(8,128)}), f32[8,20,128]{2,1,0:T(8,128)S(1)}, u32[]{:S(2)}, u32[]{:S(2)}) async-start(f32[8,20,128]{2,1,0:T(8,128)} %get-tuple-element.181), calls=%async_computation | async-start | bytes 196608 | tf_op jit(solution)/shard_map/all_to_all | solution.py:617
  147.1 0.2 collective-permute-start.18
  147.3 6.9 %all-to-all-done = f32[8,20,128]{2,1,0:T(8,128)S(1)} async-done(((f32[8,20,128]{2,1,0:T(8,128)}), f32[8,20,128]{2,1,0:T(8,128)S(1)}, u32[]{:S(2)}, u32[]{:S(2)}) %all-to-all-start) | async-done | bytes 81952 | tf_op jit(solution)/shard_map/all_to_all | solution.py:617
  154.3 0.5 slice_bitcast_fusion.5
  154.8 0.6 slice_bitcast_fusion.4
  155.4 1.7 %add_bitcast_fusion = f32[1,512,128]{2,1,0:T(8,128)} fusion(f32[512,128]{1,0:T(8,128)} %get-tuple-element.178, f32[512,128]{1,0:T(8,128)S(1)} %collective-permute-done.18), kind=kLoop, calls=%fused_computation.4 | loop fusion | flops 65536 | bytes 786432 | tf_op jit(solution)/shard_map/broadcast_in_dim | solution.py:622
  (56 shorter events, 0.8 us)
Async XLA Ops:
  0.6 14.4 %copy-start.9 = (f32[1536]{0:T(1024)S(1)}, f32[1536]{0:T(1024)}, u32[]{:S(2)}) copy-start(f32[1536]{0:T(1024)} %param.21) | copy-start | bytes 18436
  8.7 16.9 %collective-permute-start = (f32[128,384]{1,0:T(8,128)S(1)}, f32[128,384]{1,0:T(8,128)S(1)}, u32[]{:S(2)}, u32[]{:S(2)}) collective-permute-start(f32[128,384]{1,0:T(8,128)S(1)} %get-tuple-element.205), channel_id=1, source_target_pairs={{0,4},{1,5},{2,6},{3,7},{16,20},{17,21},{18,22},{19,23}} | collective-permute-start | bytes 589832 | tf_op jit(solution)/shard_map/ppermute | solution.py:411
  13.6 13.4 %collective-permute-start.1 = (f32[128,384]{1,0:T(8,128)S(1)}, f32[128,384]{1,0:T(8,128)S(1)}, u32[]{:S(2)}, u32[]{:S(2)}) collective-permute-start(f32[128,384]{1,0:T(8,128)S(1)} %get-tuple-element.97), channel_id=1, source_target_pairs={{0,4},{1,5},{2,6},{3,7},{16,20},{17,21},{18,22},{19,23}} | collective-permute-start | bytes 589832 | tf_op jit(solution)/shard_map/ppermute | solution.py:411
  20.8 4.7 %copy-start.7 = (f32[2,1,384]{2,1,0:T(1,128)S(1)}, f32[2,1,384]{2,1,0:T(1,128)}, u32[]{:S(2)}) copy-start(f32[2,1,384]{2,1,0:T(1,128)} %get-tuple-element.102) | copy-start | bytes 9220
  20.8 4.7 %copy-start.8 = (f32[2,1,384]{2,1,0:T(1,128)S(1)}, f32[2,1,384]{2,1,0:T(1,128)}, u32[]{:S(2)}) copy-start(f32[2,1,384]{2,1,0:T(1,128)} %get-tuple-element.103) | copy-start | bytes 9220
  20.8 4.8 %copy-start.1 = (f32[2,128,384]{2,1,0:T(8,128)S(1)}, f32[2,128,384]{2,1,0:T(8,128)}, u32[]{:S(2)}) copy-start(f32[2,128,384]{2,1,0:T(8,128)} %get-tuple-element.96) | copy-start | bytes 1179652
  20.8 4.8 %copy-start.3 = (f32[2,128,384]{2,1,0:T(8,128)S(1)}, f32[2,128,384]{2,1,0:T(8,128)}, u32[]{:S(2)}) copy-start(f32[2,128,384]{2,1,0:T(8,128)} %get-tuple-element.101) | copy-start | bytes 1179652
  25.7 8.3 %collective-permute-start.2 = (f32[128,384]{1,0:T(8,128)S(1)}, f32[128,384]{1,0:T(8,128)S(1)}, u32[]{:S(2)}, u32[]{:S(2)}) collective-permute-start(f32[128,384]{1,0:T(8,128)S(1)} %bitcast_add_fusion.11), channel_id=1, source_target_pairs={{0,4},{4,8},{1,5},{5,9},{2,6},{6,10},{3,7},{7,11},{16,20},{20,24},... | collective-permute-start | bytes 589832 | tf_op jit(solution)/shard_map/ppermute | solution.py:411
  27.0 8.3 %collective-permute-start.3 = (f32[128,384]{1,0:T(8,128)S(1)}, f32[128,384]{1,0:T(8,128)S(1)}, u32[]{:S(2)}, u32[]{:S(2)}) collective-permute-start(f32[128,384]{1,0:T(8,128)S(1)} %bitcast_add_fusion.10), channel_id=1, source_target_pairs={{0,4},{4,8},{1,5},{5,9},{2,6},{6,10},{3,7},{7,11},{16,20},{20,24},... | collective-permute-start | bytes 589832 | tf_op jit(solution)/shard_map/ppermute | solution.py:411
  34.0 2.1 %collective-permute-start.4 = (f32[128,384]{1,0:T(8,128)S(1)}, f32[128,384]{1,0:T(8,128)S(1)}, u32[]{:S(2)}, u32[]{:S(2)}) collective-permute-start(f32[128,384]{1,0:T(8,128)S(1)} %bitcast_add_fusion.9), channel_id=1, source_target_pairs={{4,8},{8,12},{5,9},{9,13},{6,10},{10,14},{7,11},{11,15},{20,24},{2... | collective-permute-start | bytes 589832 | tf_op jit(solution)/shard_map/ppermute | solution.py:411
  35.4 1.5 collective-permute-start.5
  36.2 8.2 %collective-permute-start.6 = (f32[128,384]{1,0:T(8,128)S(1)}, f32[128,384]{1,0:T(8,128)S(1)}, u32[]{:S(2)}, u32[]{:S(2)}) collective-permute-start(f32[128,384]{1,0:T(8,128)S(1)} %bitcast_add_fusion.7), channel_id=1, source_target_pairs={{8,12},{9,13},{10,14},{11,15},{24,28},{25,29},{26,30},{27,31}} | collective-permute-start | bytes 589832 | tf_op jit(solution)/shard_map/ppermute | solution.py:411
  36.9 7.5 %collective-permute-start.7 = (f32[128,384]{1,0:T(8,128)S(1)}, f32[128,384]{1,0:T(8,128)S(1)}, u32[]{:S(2)}, u32[]{:S(2)}) collective-permute-start(f32[128,384]{1,0:T(8,128)S(1)} %bitcast_add_fusion.6), channel_id=1, source_target_pairs={{8,12},{9,13},{10,14},{11,15},{24,28},{25,29},{26,30},{27,31}} | collective-permute-start | bytes 589832 | tf_op jit(solution)/shard_map/ppermute | solution.py:411
  51.3 1.8 %collective-permute-start.8 = (f32[512,128]{1,0:T(8,128)}, f32[512,128]{1,0:T(8,128)S(1)}, u32[]{:S(2)}, u32[]{:S(2)}) collective-permute-start(f32[512,128]{1,0:T(8,128)} %get-tuple-element.118.refs_2_.mine), channel_id=1, source_target_pairs={{0,1},{1,0},{2,3},{3,2},{4,5},{5,4},{6,7},{7,6},{8,9},{9,8},{10,11... | collective-permute-start | bytes 786440 | tf_op jit(solution)/shard_map/ppermute | solution.py:539
  53.1 0.7 copy-start.4
  62.4 15.8 %collective-permute-start.9 = (f32[128,384]{1,0:T(8,128)S(1)}, f32[128,384]{1,0:T(8,128)S(1)}, u32[]{:S(2)}, u32[]{:S(2)}) collective-permute-start(f32[128,384]{1,0:T(8,128)S(1)} %get-tuple-element.202), channel_id=1, source_target_pairs={{12,8},{13,9},{14,10},{15,11},{28,24},{29,25},{30,26},{31,27}} | collective-permute-start | bytes 589832 | tf_op jit(solution)/shard_map/ppermute | solution.py:411
  63.2 16.6 %collective-permute-start.10 = (f32[128,384]{1,0:T(8,128)S(1)}, f32[128,384]{1,0:T(8,128)S(1)}, u32[]{:S(2)}, u32[]{:S(2)}) collective-permute-start(f32[128,384]{1,0:T(8,128)S(1)} %get-tuple-element.122), channel_id=1, source_target_pairs={{12,8},{13,9},{14,10},{15,11},{28,24},{29,25},{30,26},{31,27}} | collective-permute-start | bytes 589832 | tf_op jit(solution)/shard_map/ppermute | solution.py:411
  70.5 7.6 %copy-start = (f32[2,128,384]{2,1,0:T(8,128)S(1)}, f32[2,128,384]{2,1,0:T(8,128)}, u32[]{:S(2)}) copy-start(f32[2,128,384]{2,1,0:T(8,128)} %get-tuple-element.121) | copy-start | bytes 1179652
  79.1 10.6 %collective-permute-start.11 = (f32[128,384]{1,0:T(8,128)S(1)}, f32[128,384]{1,0:T(8,128)S(1)}, u32[]{:S(2)}, u32[]{:S(2)}) collective-permute-start(f32[128,384]{1,0:T(8,128)S(1)} %bitcast_add_fusion.5), channel_id=1, source_target_pairs={{12,8},{8,4},{13,9},{9,5},{14,10},{10,6},{15,11},{11,7},{28,24},{2... | collective-permute-start | bytes 589832 | tf_op jit(solution)/shard_map/ppermute | solution.py:411
  80.8 10.3 %collective-permute-start.12 = (f32[128,384]{1,0:T(8,128)S(1)}, f32[128,384]{1,0:T(8,128)S(1)}, u32[]{:S(2)}, u32[]{:S(2)}) collective-permute-start(f32[128,384]{1,0:T(8,128)S(1)} %bitcast_add_fusion.4), channel_id=1, source_target_pairs={{12,8},{8,4},{13,9},{9,5},{14,10},{10,6},{15,11},{11,7},{28,24},{2... | collective-permute-start | bytes 589832 | tf_op jit(solution)/shard_map/ppermute | solution.py:411
  81.5 8.2 %copy-start.2 = (f32[2,128,384]{2,1,0:T(8,128)S(1)}, f32[2,128,384]{2,1,0:T(8,128)}, u32[]{:S(2)}) copy-start(f32[2,128,384]{2,1,0:T(8,128)} %get-tuple-element.129) | copy-start | bytes 1179652
  89.7 17.0 %collective-permute-start.13 = (f32[128,384]{1,0:T(8,128)S(1)}, f32[128,384]{1,0:T(8,128)S(1)}, u32[]{:S(2)}, u32[]{:S(2)}) collective-permute-start(f32[128,384]{1,0:T(8,128)S(1)} %bitcast_add_fusion.3), channel_id=1, source_target_pairs={{8,4},{4,0},{9,5},{5,1},{10,6},{6,2},{11,7},{7,3},{24,20},{20,16},... | collective-permute-start | bytes 589832 | tf_op jit(solution)/shard_map/ppermute | solution.py:411
  91.1 19.8 %collective-permute-start.14 = (f32[128,384]{1,0:T(8,128)S(1)}, f32[128,384]{1,0:T(8,128)S(1)}, u32[]{:S(2)}, u32[]{:S(2)}) collective-permute-start(f32[128,384]{1,0:T(8,128)S(1)} %bitcast_add_fusion.2), channel_id=1, source_target_pairs={{8,4},{4,0},{9,5},{5,1},{10,6},{6,2},{11,7},{7,3},{24,20},{20,16},... | collective-permute-start | bytes 589832 | tf_op jit(solution)/shard_map/ppermute | solution.py:411
  107.4 21.0 %collective-permute-start.15 = (f32[128,384]{1,0:T(8,128)}, f32[128,384]{1,0:T(8,128)S(1)}, u32[]{:S(2)}, u32[]{:S(2)}) collective-permute-start(f32[128,384]{1,0:T(8,128)} %bitcast_add_fusion.1), channel_id=1, source_target_pairs={{4,0},{5,1},{6,2},{7,3},{20,16},{21,17},{22,18},{23,19}} | collective-permute-start | bytes 589832 | tf_op jit(solution)/shard_map/ppermute | solution.py:411
  111.6 16.8 %collective-permute-start.16 = (f32[128,384]{1,0:T(8,128)}, f32[128,384]{1,0:T(8,128)S(1)}, u32[]{:S(2)}, u32[]{:S(2)}) collective-permute-start(f32[128,384]{1,0:T(8,128)} %bitcast_add_fusion), channel_id=1, source_target_pairs={{4,0},{5,1},{6,2},{7,3},{20,16},{21,17},{22,18},{23,19}} | collective-permute-start | bytes 589832 | tf_op jit(solution)/shard_map/ppermute | solution.py:411
  113.1 7.2 %copy-start.6 = (f32[8,128,384]{2,1,0:T(8,128)S(1)}, f32[8,128,384]{2,1,0:T(8,128)}, u32[]{:S(2)}) copy-start(f32[8,128,384]{2,1,0:T(8,128)} %get-tuple-element.211) | copy-start | bytes 4718596
  120.3 9.1 %collective-permute-start.17 = (f32[512,128]{1,0:T(8,128)}, f32[512,128]{1,0:T(8,128)S(1)}, u32[]{:S(2)}, u32[]{:S(2)}) collective-permute-start(f32[512,128]{1,0:T(8,128)} %get-tuple-element.173.rest_11_), channel_id=1, source_target_pairs={{0,1},{1,0},{2,3},{3,2},{4,5},{5,4},{6,7},{7,6},{8,9},{9,8},{10,11... | collective-permute-start | bytes 786440 | tf_op jit(solution)/shard_map/ppermute | solution.py:604
  129.3 0.7 copy-start.5
  138.4 15.9 %all-to-all-start = ((f32[8,20,128]{2,1,0:T(8,128)}), f32[8,20,128]{2,1,0:T(8,128)S(1)}, u32[]{:S(2)}, u32[]{:S(2)}) async-start(f32[8,20,128]{2,1,0:T(8,128)} %get-tuple-element.181), calls=%async_computation | async-start | bytes 196608 | tf_op jit(solution)/shard_map/all_to_all | solution.py:617
  147.1 8.3 %collective-permute-start.18 = (f32[512,128]{1,0:T(8,128)}, f32[512,128]{1,0:T(8,128)S(1)}, u32[]{:S(2)}, u32[]{:S(2)}) collective-permute-start(f32[512,128]{1,0:T(8,128)} %get-tuple-element.178), channel_id=1, source_target_pairs={{0,1},{1,0},{2,3},{3,2},{4,5},{5,4},{6,7},{7,6},{8,9},{9,8},{10,11... | collective-permute-start | bytes 786440 | tf_op jit(solution)/shard_map/ppermute | solution.py:616

commit v4 on v3

--- a/solution.py
+++ b/solution.py
@@ -20,7 +20,7 @@
 HIGHEST = lax.Precision.HIGHEST
 F32 = jnp.float32
 BF16 = jnp.bfloat16
-VMEM_LIMIT = 60 * 1024 * 1024
+VMEM_LIMIT = 20 * 1024 * 1024
 
 
 def mm(a, b):
@@ -377,24 +377,38 @@
                 sums[k, 8 + rows + r : 9 + rows + r] = gpart1[:, r * LANES : (r + 1) * LANES]
 
 
-def relay(own, total, axis, forward, work):
+def take(array, at):
+    start = (at,) + (0,) * (array.ndim - 1)
+    return lax.dynamic_slice(array, start, (1,) + array.shape[1:], allow_negative_indices=False)[0]
+
+
+def relay_steps(count):
+    return 2 * HALF_CHUNKS + LAG * (count - 2)
+
+
+def relay_plan(rank, count):
+    chunks, steps = 2 * HALF_CHUNKS, relay_steps(count)
+    sends = []
+    for turn in range(LAG, steps):
+        at = jnp.clip(turn - LAG * rank, 0, chunks - 1)
+        sends.append((at < HALF_CHUNKS, [jnp.clip(at - k * HALF_CHUNKS, 0, HALF_CHUNKS - 1) for k in range(2)]))
+    arrivals = []
+    for which, turns in ((0, steps - LAG), (1, steps)):
+        at = [k + which * HALF_CHUNKS + LAG * (rank - 1) for k in range(HALF_CHUNKS)]
+        arrivals.append([jnp.clip(k, 0, turns - 1) for k in at])
+    return sends, arrivals, rank > 0
+
+
+def relay(own, total, axis, forward, plan, work):
     count = lax.axis_size(axis)
-    index = lax.axis_index(axis)
-    rank = index if forward else count - 1 - index
-    chunks = 2 * HALF_CHUNKS
-    steps = chunks + LAG * (count - 2)
+    chunks, steps = 2 * HALF_CHUNKS, relay_steps(count)
+    sends, arrivals, follows = plan
     received, halves, message = [], None, None
 
-    def chunk(pair, at):
-        picked = [lax.dynamic_index_in_dim(v, jnp.clip(at - k * HALF_CHUNKS, 0, HALF_CHUNKS - 1), 0, False) for k, v in enumerate(pair)]
-        return jnp.where(at < HALF_CHUNKS, picked[0], picked[1])
-
     def half(which):
-        turns = received[: steps - LAG] if which == 0 else received
-        stacked = jnp.stack(turns)
-        at = [k + which * HALF_CHUNKS + LAG * (rank - 1) for k in range(HALF_CHUNKS)]
-        picked = [lax.dynamic_index_in_dim(stacked, jnp.clip(k, 0, len(turns) - 1), 0, False) for k in at]
-        return jnp.where(rank > 0, jnp.concatenate(picked, axis=1), 0.0)
+        stacked = jnp.stack(received[: steps - LAG] if which == 0 else received)
+        picked = [take(stacked, at) for at in arrivals[which]]
+        return jnp.where(follows, jnp.concatenate(picked, axis=1), 0.0)
 
     for turn in range(steps):
         if turn < LAG:
@@ -402,9 +416,10 @@
             if message is not None:
                 mine, _ = lax.optimization_barrier((mine, message))
         else:
-            at = jnp.clip(turn - LAG * rank, 0, chunks - 1)
+            low, at = sends[turn - LAG]
             arrived, _ = lax.optimization_barrier((received[turn - LAG], message))
-            mine = chunk(halves[0], at) + chunk(halves[1], at) * arrived
+            mine, factor = (jnp.where(low, take(pair[0], at[0]), take(pair[1], at[1])) for pair in halves)
+            mine = mine + factor * arrived
         message = mine
         ranks = [r for r in range(count - 1) if 0 <= turn - LAG * r < chunks]
         pairs = [(r, r + 1) if forward else (count - 1 - r, count - 2 - r) for r in ranks]
@@ -420,6 +435,10 @@
     return first, half(1)
 
 
+def placed(kind, shape, dtype):
+    return pltpu.VMEM(shape, dtype) if kind in ("tok", "blk", "row") else jax.ShapeDtypeStruct(shape, dtype)
+
+
 def one_hot(width):
     lane = np.arange(LANES)[:, None]
     return np.logical_and(lane % GROUP == np.arange(width)[None, :] // HEADDIM, lane < 3 * GROUP)
@@ -437,8 +456,14 @@
     lengths = lengths.reshape(-1)
     bias, alog, dskip = (v.reshape(1, heads) for v in (bias, alog, dskip))
     gain = gain.reshape(1, width)
-    offset = jnp.reshape(lax.axis_index("seq") * tokens, (1,)).astype(jnp.int32)
     oh = jnp.asarray(one_hot(width), BF16)
+    x, z, grad, b, c, raw, bias, alog, dskip, gain, oh = (
+        pltpu.with_memory_space_constraint(v, pltpu.HBM) for v in (x, z, grad, b, c, raw, bias, alog, dskip, gain, oh)
+    )
+    count, index = lax.axis_size("seq"), lax.axis_index("seq")
+    offset = jnp.reshape(index * tokens, (1,)).astype(jnp.int32)
+    plans = relay_plan(index, count), relay_plan(count - 1 - index, count)
+    offset, plans = lax.optimization_barrier((offset, plans))
 
     def tied(message):
         return [("smem", lengths), ("smem", lax.optimization_barrier((offset, message))[0])]
@@ -469,7 +494,7 @@
             grid=(blocks,),
             in_specs=[spec(kind, value.shape) for kind, value in ins],
             out_specs=[spec(kind, shape) for kind, shape, _ in outs],
-            out_shape=[jax.ShapeDtypeStruct(shape, dtype) for _, shape, dtype in outs],
+            out_shape=[placed(kind, shape, dtype) for kind, shape, dtype in outs],
             scratch_shapes=[pltpu.VMEM(shape, F32) for shape in scratch],
             input_output_aliases=aliases or {},
             compiler_params=pltpu.CompilerParams(
@@ -532,7 +557,7 @@
             sin[0] = arrived
             stats = output(where, 0)
 
-    _, sin[1] = relay(locals_[0][0], locals_[0][1], "seq", True, forward_work)
+    _, sin[1] = relay(locals_[0][0], locals_[0][1], "seq", True, plans[0], forward_work)
     plain = [("smem", lengths), ("smem", offset)]
     stats = output(plain, 1)
     exchange = partial(lax.ppermute, axis_name="head", perm=[(0, 1), (1, 0)])
@@ -599,7 +624,7 @@
             return
         back(where, slot)
 
-    _, sout = relay(norms[0][6], locals_[0][1], "seq", False, backward_work)
+    _, sout = relay(norms[0][6], locals_[0][1], "seq", False, plans[1], backward_work)
     dbd, dc, rho1, rho2, rho3 = carry
     dc_other = exchange(dc)
     members = lax.axis_size(("seq", "batch"))
@@ -609,7 +634,7 @@
     ])
     xgrad, db, dc, draw, sums = call(
         partial(input_kernel, final=True), True, ins,
-        [(("tok", span, 1), wide, BF16), ("tok", narrow, F32), ("tok", narrow, F32), ("raw", (heads, tokens), F32),
+        [(("tok", span, 1), wide, BF16), (("tok", LANES, 0), narrow, F32), (("tok", LANES, 0), narrow, F32), ("raw", (heads, tokens), F32),
          ("all", (members, 8 + width // LANES, LANES), F32)],
         [(STATE, span), (1, span), (8, LANES)], "input_last", {15: 0},
     )

time: 159 us -> 133 us (0.84)
  Pallas kernels: 91.4 us -> 74.6 us
  waiting for transfers between devices: 17.6 us -> 25.3 us
  other arithmetic: 8.63 us -> 1.48 us
  local copies, waits for them, and re-layouts: 8.52 us -> 2.98 us
  starting transfers between devices: 29.6 us -> 25.8 us
    pallas_call x14, Pallas kernels: 91.4 us -> 74.6 us  [call(): pl.pallas_call(kernel, grid=(blocks,), in_specs=[spec(kind, value.shape)...]
    ppermute x16, waiting for transfers between devices: 8.94 us -> 16.8 us  [relay(): received.append(lax.ppermute(message, axis, pairs))]
    all_to_all x1, starting transfers between devices: 8.73 us -> 4.9 us  [shards(): sums = jnp.sum(lax.all_to_all(sums, ('seq', 'batch'), 0, 0), axis=0)]
    unnamed x32 -> x16, local copies, waits for them, and re-layouts: 4.46 us -> 0.97 us
    add x12, other arithmetic: 3.65 us -> 0.46 us  [relay(): mine = mine + factor * arrived]
    select_n x7, other arithmetic: 3.28 us -> 0.27 us  [the longest x3 0.15 us: relay(): jnp.where(low, take(pair[0], at[0]), take(pair[1], at[1]))]
    squeeze x2, local copies, waits for them, and re-layouts: 2.1 us -> 0.05 us  [relay(): mine = own[turn]]
  transfers between devices with their start and end apart: 20 -> 20, of which waited for: 5 -> 5; matrix products, arithmetic and copies ran while one was open for 7% -> 2% of each run, Pallas kernels for 40% -> 39%
where the time goes in v4:
time: 133 us; the launch traced here: 132 us
  Pallas kernels  74.6 us (56%)
  starting transfers between devices  25.8 us (19%)
  waiting for transfers between devices  25.3 us (19%)
  local copies, waits for them, and re-layouts  2.98 us (2%)
  other arithmetic  1.48 us (1%)
  between operations  1.41 us (1%)
    pallas_call x14, Pallas kernels, call(): pl.pallas_call(kernel, grid=(blocks,), in_specs=[spec(kind, value.shape)...  74.6 us
    ppermute x16, starting transfers between devices, relay(): received.append(lax.ppermute(message, axis, pairs))  20.5 us
    ppermute x16, waiting for transfers between devices, relay(): received.append(lax.ppermute(message, axis, pairs))  16.8 us
    all_to_all x1, waiting for transfers between devices, shards(): sums = jnp.sum(lax.all_to_all(sums, ('seq', 'batch'), 0, 0), axis=0)  6.94 us
    all_to_all x1, starting transfers between devices, shards(): sums = jnp.sum(lax.all_to_all(sums, ('seq', 'batch'), 0, 0), axis=0)  4.9 us
  transfers between devices with their start and end apart: 20, of which 5 were waited for; matrix products, arithmetic and copies ran while one was open for 2% of the time, Pallas kernels for 39%

profile of v4, /device:TPU:0, one launch (start us, length us, event | category | flops | bytes accessed | tf_op | source)
XLA Modules:
  0.0 131.5 jit_solution(8528754685336371742)
XLA Ops:
  0.7 0.0 copy-start.1
  0.8 0.0 copy-start
  0.8 0.6 copy-done
  1.5 5.9 %prepare.1 = (f32[2,128,384]{2,1,0:T(8,128)S(1)}, f32[2,1,384]{2,1,0:T(1,128)S(1)}, f32[4,128,768]{2,1,0:T(8,128)S(1)}, f32[4,1,768]{2,1,0:T(1,128)S(1)}, f32[4,...) custom-call(s32[2]{0:T(128)S(1)} %bitcast.122, ...), custom_call_target="tpu_custom_call" | custom-call | tf_op jit(solution)/shard_map/prepare/pallas_call | solution.py:492
  7.4 4.9 %collective-permute-start = (f32[128,384]{1,0:T(8,128)S(1)}, f32[128,384]{1,0:T(8,128)S(1)}, u32[]{:S(2)}, u32[]{:S(2)}) collective-permute-start(f32[128,384]{1,0:T(8,128)S(1)} %get-tuple-element.299), channel_id=1, source_target_pairs={{0,4},{1,5},{2,6},{3,7},{16,20},{17,21},{18,22},{19,23}} | collective-permute-start | bytes 589832 | tf_op jit(solution)/shard_map/ppermute | solution.py:426
  12.4 1.3 collective-permute-start.1
  13.7 0.0 copy-done.1
  13.7 0.6 reshape.262.refs_14_.gain.refs_13_
  14.3 3.9 %states.1 = (f32[2,128,384]{2,1,0:T(8,128)S(1)}, f32[2,1,384]{2,1,0:T(1,128)S(1)}, f32[4,128,768]{2,1,0:T(8,128)S(1)}, f32[4,1,768]{2,1,0:T(1,128)S(1)}, f32[4,1,768]{2,1,0:T(1,128)S(1)}) custom-call(s32[2]{0:T(128)S(1)} %bitcast.123, s32[1]{0:T(128)} %bitcast.1.offset.refs_1_, f32[512,128]{1,0:T(8,128)S(1)} %get-tuple-element.150.cum.refs_5_.refs_4_, ...), custom_call_target="tpu_custom_call" | custom-call | tf_op jit(solution)/shard_map/states/pallas_call | solution.py:492
  18.2 3.7 %diagonal.3.refs_12_ = f32[512,768]{1,0:T(8,128)S(1)} custom-call(s32[2]{0:T(128)S(1)} %bitcast.124, s32[1]{0:T(128)} %bitcast.1.offset.refs_1_, f32[512,128]{1,0:T(8,128)S(1)} %get-tuple-element.150.cum.refs_5_.refs_4_, f32[2,32,512]{2,1,0:T(8,128)S(1)} %get-tuple-element.182.rows, bf16[512,1536]{1,0:T(8,128)(2,1)} %bitcast.138, ...), custom_call_target="tpu_custom_call" | custom-call | tf_op jit(solution)/shard_map/diagonal/pallas_call | solution.py:492
  21.9 0.1 fusion.6
  22.0 0.0 collective-permute-done
  22.0 1.3 collective-permute-start.2
  23.3 0.0 collective-permute-done.1
  23.4 2.2 %collective-permute-start.3 = (f32[128,384]{1,0:T(8,128)S(1)}, f32[128,384]{1,0:T(8,128)S(1)}, u32[]{:S(2)}, u32[]{:S(2)}) collective-permute-start(f32[128,384]{1,0:T(8,128)S(1)} %bitcast_add_fusion.10), channel_id=1, source_target_pairs={{0,4},{4,8},{1,5},{5,9},{2,6},{6,10},{3,7},{7,11},{16,20},{20,24},... | collective-permute-start | bytes 589832 | tf_op jit(solution)/shard_map/ppermute | solution.py:426
  25.6 3.7 %diagonal.2.diag = f32[512,768]{1,0:T(8,128)S(1)} custom-call(s32[2]{0:T(128)S(1)} %bitcast.125, s32[1]{0:T(128)} %bitcast.1.offset.refs_1_, f32[512,128]{1,0:T(8,128)S(1)} %get-tuple-element.150.cum.refs_5_.refs_4_, f32[2,32,512]{2,1,0:T(8,128)S(1)} %get-tuple-element.182.rows, bf16[512,1536]{1,0:T(8,128)(2,1)} %bitcast.139, bf16[512,128]{1,0:T(8,128)(2,1)} %bitcast.153, ...), custom_call_target="tpu_custom_call" | custom-call | tf_op jit(solution)/shard_map/diagonal/pallas_call | solution.py:492
  29.4 0.0 collective-permute-done.2
  29.4 0.7 collective-permute-start.4
  30.1 1.6 %collective-permute-done.3 = f32[128,384]{1,0:T(8,128)S(1)} collective-permute-done((f32[128,384]{1,0:T(8,128)S(1)}, f32[128,384]{1,0:T(8,128)S(1)}, u32[]{:S(2)}, u32[]{:S(2)}) %collective-permute-start.3) | collective-permute-done | bytes 196640 | tf_op jit(solution)/shard_map/ppermute | solution.py:426
  31.7 0.7 collective-permute-start.5
  32.5 0.0 collective-permute-done.4
  32.5 0.7 collective-permute-start.6
  33.2 0.0 collective-permute-done.5
  33.3 0.7 collective-permute-start.7
  34.1 4.5 %output.2 = (f32[512,768]{1,0:T(8,128)S(1)}, f32[512,128]{1,0:T(8,128)S(1)}) custom-call(s32[2]{0:T(128)S(1)} %bitcast.126, s32[1]{0:T(128)} %bitcast.1.offset.refs_1_, f32[128,768]{1,0:T(8,128)S(1)} %maximum_select_fusion.1.refs_2_.sin, f32[4,128,768]{2,1,0:T(8,128)S(1)} %get-tuple-element.186.refs_3_.ends, ...), custom_call_target="tpu_custom_call" | custom-call | tf_op jit(solution)/shard_map/output/pallas_call | solution.py:492
  38.6 0.0 collective-permute-done.6
  38.6 0.0 collective-permute-done.7
  38.8 4.5 %output.3 = (f32[512,768]{1,0:T(8,128)S(1)}, f32[512,128]{1,0:T(8,128)S(1)}) custom-call(s32[2]{0:T(128)S(1)} %bitcast.127, s32[1]{0:T(128)} %bitcast.1.offset.refs_1_, f32[128,768]{1,0:T(8,128)S(1)} %maximum_select_fusion.sin, f32[4,128,768]{2,1,0:T(8,128)S(1)} %get-tuple-element.179.ends, f32[4,1,768]{2,1,0:T(1,128)S(1)} %get-tuple-element.180.prefix, ...), custom_call_target="tpu_custom_call" | custom-call | tf_op jit(solution)/shard_map/output/pallas_call | solution.py:492
  43.3 0.1 collective-permute-start.8
  43.4 1.5 %collective-permute-done.8.refs_3_.other = f32[512,128]{1,0:T(8,128)S(1)} collective-permute-done((f32[512,128]{1,0:T(8,128)S(1)}, f32[512,128]{1,0:T(8,128)S(1)}, u32[]{:S(2)}, u32[]{:S(2)}) %collective-permute-start.8) | collective-permute-done | bytes 262176 | tf_op jit(solution)/shard_map/ppermute | solution.py:564
  44.9 6.3 %norm.2 = (bf16[512,1536]{1,0:T(8,128)(2,1)}, bf16[512,1536]{1,0:T(8,128)(2,1)}, bf16[512,768]{1,0:T(8,128)(2,1)S(1)}, bf16[512,768]{1,0:T(8,128)(2,1)S(1)}, f32...) custom-call(s32[2]{0:T(128)S(1)} %bitcast.128, s32[1]{0:T(128)} %bitcast.1.offset.refs_1_, ...), custom_call_target="tpu_custom_call" | custom-call | tf_op jit(solution)/shard_map/norm/pallas_call | solution.py:492
  51.2 0.7 collective-permute-start.9
  51.9 0.1 fusion.11
  51.9 0.7 collective-permute-start.10
  52.6 5.6 %diagonal_back.4 = (f32[512,384]{1,0:T(8,128)S(1)}, f32[512,128]{1,0:T(8,128)S(1)}, f32[512,128]{1,0:T(8,128)S(1)}, f32[512,128]{1,0:T(8,128)S(1)}, f32[512,128]{1,0:T(8,128)S(1)}, /*index=5*/f32[512,128]{1,0:T(8,128)S(1)}) custom-call(s32[2]{0:T(128)S(1)} %bitcast.129, s32[1]{0:T(128)} %bitcast.1.offset.refs_1_, ...), custom_call_target="tpu_custom_call" | custom-call | tf_op jit(solution)/shard_map/diagonal_back/pallas_call | solution.py:492
  58.2 6.3 %norm.3 = (bf16[512,1536]{1,0:T(8,128)(2,1)}, bf16[512,1536]{1,0:T(8,128)(2,1)}, bf16[512,768]{1,0:T(8,128)(2,1)S(1)}, bf16[512,768]{1,0:T(8,128)(2,1)S(1)}, f32...) custom-call(s32[2]{0:T(128)S(1)} %bitcast.130, ...), custom_call_target="tpu_custom_call", output_to_operand_aliasing={{0}: (16, {}), {1}: (17, {})} | custom-call | tf_op jit(solution)/shard_map/norm/pallas_call | solution.py:492
  64.5 0.0 collective-permute-done.9
  64.6 0.7 collective-permute-start.11
  65.3 0.0 collective-permute-done.10
  65.3 0.7 collective-permute-start.12
  66.0 5.7 %diagonal_back.5 = (f32[512,384]{1,0:T(8,128)S(1)}, f32[512,128]{1,0:T(8,128)S(1)}, f32[512,128]{1,0:T(8,128)S(1)}, f32[512,128]{1,0:T(8,128)S(1)}, f32[512,128]{1,0:T(8,128)S(1)}, /*index=5*/f32[512,128]{1,0:T(8,128)S(1)}) custom-call(s32[2]{0:T(128)S(1)} %bitcast.131, s32[1]{0:T(128)} %bitcast.1.offset.refs_1_, ...), custom_call_target="tpu_custom_call" | custom-call | tf_op jit(solution)/shard_map/diagonal_back/pallas_call | solution.py:492
  71.8 0.0 collective-permute-done.11
  71.8 1.3 collective-permute-start.13
  73.1 0.0 collective-permute-done.12
  73.2 1.3 collective-permute-start.14
  74.5 5.7 %diagonal_back.6 = (f32[512,384]{1,0:T(8,128)S(1)}, f32[512,128]{1,0:T(8,128)S(1)}, f32[512,128]{1,0:T(8,128)S(1)}, f32[512,128]{1,0:T(8,128)S(1)}, f32[512,128]{1,0:T(8,128)S(1)}, /*index=5*/f32[512,128]{1,0:T(8,128)S(1)}) custom-call(s32[2]{0:T(128)S(1)} %bitcast.132, s32[1]{0:T(128)} %bitcast.1.offset.refs_1_, ...), custom_call_target="tpu_custom_call" | custom-call | tf_op jit(solution)/shard_map/diagonal_back/pallas_call | solution.py:492
  80.2 12.3 %collective-permute-done.13 = f32[128,384]{1,0:T(8,128)S(1)} collective-permute-done((f32[128,384]{1,0:T(8,128)S(1)}, f32[128,384]{1,0:T(8,128)S(1)}, u32[]{:S(2)}, u32[]{:S(2)}) %collective-permute-start.13) | collective-permute-done | bytes 196640 | tf_op jit(solution)/shard_map/ppermute | solution.py:426
  92.5 1.3 collective-permute-start.15
  93.8 2.9 %collective-permute-done.14 = f32[128,384]{1,0:T(8,128)S(1)} collective-permute-done((f32[128,384]{1,0:T(8,128)S(1)}, f32[128,384]{1,0:T(8,128)S(1)}, u32[]{:S(2)}, u32[]{:S(2)}) %collective-permute-start.14) | collective-permute-done | bytes 196640 | tf_op jit(solution)/shard_map/ppermute | solution.py:426
  96.8 1.5 %collective-permute-start.16 = (f32[128,384]{1,0:T(8,128)S(1)}, f32[128,384]{1,0:T(8,128)S(1)}, u32[]{:S(2)}, u32[]{:S(2)}) collective-permute-start(f32[128,384]{1,0:T(8,128)S(1)} %bitcast_add_fusion), channel_id=1, source_target_pairs={{4,0},{5,1},{6,2},{7,3},{20,16},{21,17},{22,18},{23,19}} | collective-permute-start | bytes 589832 | tf_op jit(solution)/shard_map/ppermute | solution.py:426
  98.2 5.9 %diagonal_back.7 = (f32[512,384]{1,0:T(8,128)S(1)}, f32[512,128]{1,0:T(8,128)S(1)}, f32[512,128]{1,0:T(8,128)S(1)}, f32[512,128]{1,0:T(8,128)S(1)}, f32[512,128]{1,0:T(8,128)S(1)}, /*index=5*/f32[512,128]{1,0:T(8,128)S(1)}) custom-call(s32[2]{0:T(128)S(1)} %bitcast.133, s32[1]{0:T(128)} %bitcast.1.offset.refs_1_, ...), custom_call_target="tpu_custom_call" | custom-call | tf_op jit(solution)/shard_map/diagonal_back/pallas_call | solution.py:492
  104.1 0.1 collective-permute-start.17
  104.4 5.9 %input.1 = (bf16[512,1536]{1,0:T(8,128)(2,1)}, f32[512,128]{1,0:T(8,128)S(1)}, f32[512,128]{1,0:T(8,128)S(1)}, f32[4,8,128]{2,1,0:T(8,128)S(1)}) custom-call(s32[2]{0:T(128)S(1)} %bitcast.134, s32[1]{0:T(128)} %bitcast.1.offset.refs_1_, f32[128,768]{1,0:T(8,128)S(1)} %maximum_select_fusion.3.sout, f32[128,768]{1,0:T(8,128)S(1)} %maximum_select_fusion.1.refs_2_.sin, ...), custom_call_target="tpu_custom_call" | custom-call | tf_op jit(solution)/shard_map/input/pallas_call | solution.py:492
  110.3 0.0 collective-permute-done.15
  110.3 0.0 collective-permute-done.16
  110.4 0.0 collective-permute-done.17.rest_12_
  110.4 7.2 %input_last.1 = (bf16[512,1536]{1,0:T(8,128)(2,1)}, f32[512,128]{1,0:T(8,128)S(1)}, f32[512,128]{1,0:T(8,128)}, f32[24,512]{1,0:T(8,128)}, f32[8,20,128]{2,1,0:T(8,128)}) custom-call(s32[2]{0:T(128)S(1)} %bitcast.135, s32[1]{0:T(128)} %bitcast.1.offset.refs_1_, f32[128,768]{1,0:T(8,128)S(1)} %maximum_select_fusion.2.sout, ...), custom_call_target="tpu_custom_call", output_to_operand_aliasing={{0}: (15, {})} | custom-call | tf_op jit(solution)/shard_map/input_last/pallas_call | solution.py:492
  117.6 4.9 %all-to-all-start = ((f32[8,20,128]{2,1,0:T(8,128)}), f32[8,20,128]{2,1,0:T(8,128)S(1)}, u32[]{:S(2)}, u32[]{:S(2)}) async-start(f32[8,20,128]{2,1,0:T(8,128)} %get-tuple-element.275), calls=%async_computation | async-start | bytes 196608 | tf_op jit(solution)/shard_map/all_to_all | solution.py:642
  122.5 0.2 collective-permute-start.18
  122.7 6.9 %all-to-all-done = f32[8,20,128]{2,1,0:T(8,128)S(1)} async-done(((f32[8,20,128]{2,1,0:T(8,128)}), f32[8,20,128]{2,1,0:T(8,128)S(1)}, u32[]{:S(2)}, u32[]{:S(2)}) %all-to-all-start) | async-done | bytes 81952 | tf_op jit(solution)/shard_map/all_to_all | solution.py:642
  129.7 0.5 slice_bitcast_fusion.5
  130.2 0.6 slice_bitcast_fusion.4
  130.8 0.0 collective-permute-done.18
  130.8 0.7 add_bitcast_fusion
  (40 shorter events, 1.2 us)
Async XLA Ops:
  0.7 13.0 %copy-start.1 = (f32[1536]{0:T(1024)S(1)}, f32[1536]{0:T(1024)}, u32[]{:S(2)}) copy-start(f32[1536]{0:T(1024)} %param.21) | copy-start | bytes 18436
  0.8 0.7 copy-start
  7.4 14.5 %collective-permute-start = (f32[128,384]{1,0:T(8,128)S(1)}, f32[128,384]{1,0:T(8,128)S(1)}, u32[]{:S(2)}, u32[]{:S(2)}) collective-permute-start(f32[128,384]{1,0:T(8,128)S(1)} %get-tuple-element.299), channel_id=1, source_target_pairs={{0,4},{1,5},{2,6},{3,7},{16,20},{17,21},{18,22},{19,23}} | collective-permute-start | bytes 589832 | tf_op jit(solution)/shard_map/ppermute | solution.py:426
  12.4 11.0 %collective-permute-start.1 = (f32[128,384]{1,0:T(8,128)S(1)}, f32[128,384]{1,0:T(8,128)S(1)}, u32[]{:S(2)}, u32[]{:S(2)}) collective-permute-start(f32[128,384]{1,0:T(8,128)S(1)} %get-tuple-element.146), channel_id=1, source_target_pairs={{0,4},{1,5},{2,6},{3,7},{16,20},{17,21},{18,22},{19,23}} | collective-permute-start | bytes 589832 | tf_op jit(solution)/shard_map/ppermute | solution.py:426
  22.0 7.4 %collective-permute-start.2 = (f32[128,384]{1,0:T(8,128)S(1)}, f32[128,384]{1,0:T(8,128)S(1)}, u32[]{:S(2)}, u32[]{:S(2)}) collective-permute-start(f32[128,384]{1,0:T(8,128)S(1)} %bitcast_add_fusion.11), channel_id=1, source_target_pairs={{0,4},{4,8},{1,5},{5,9},{2,6},{6,10},{3,7},{7,11},{16,20},{20,24},... | collective-permute-start | bytes 589832 | tf_op jit(solution)/shard_map/ppermute | solution.py:426
  23.4 8.3 %collective-permute-start.3 = (f32[128,384]{1,0:T(8,128)S(1)}, f32[128,384]{1,0:T(8,128)S(1)}, u32[]{:S(2)}, u32[]{:S(2)}) collective-permute-start(f32[128,384]{1,0:T(8,128)S(1)} %bitcast_add_fusion.10), channel_id=1, source_target_pairs={{0,4},{4,8},{1,5},{5,9},{2,6},{6,10},{3,7},{7,11},{16,20},{20,24},... | collective-permute-start | bytes 589832 | tf_op jit(solution)/shard_map/ppermute | solution.py:426
  29.4 3.1 %collective-permute-start.4 = (f32[128,384]{1,0:T(8,128)S(1)}, f32[128,384]{1,0:T(8,128)S(1)}, u32[]{:S(2)}, u32[]{:S(2)}) collective-permute-start(f32[128,384]{1,0:T(8,128)S(1)} %bitcast_add_fusion.9), channel_id=1, source_target_pairs={{4,8},{8,12},{5,9},{9,13},{6,10},{10,14},{7,11},{11,15},{20,24},{2... | collective-permute-start | bytes 589832 | tf_op jit(solution)/shard_map/ppermute | solution.py:426
  31.7 1.5 %collective-permute-start.5 = (f32[128,384]{1,0:T(8,128)S(1)}, f32[128,384]{1,0:T(8,128)S(1)}, u32[]{:S(2)}, u32[]{:S(2)}) collective-permute-start(f32[128,384]{1,0:T(8,128)S(1)} %bitcast_add_fusion.8), channel_id=1, source_target_pairs={{4,8},{8,12},{5,9},{9,13},{6,10},{10,14},{7,11},{11,15},{20,24},{2... | collective-permute-start | bytes 589832 | tf_op jit(solution)/shard_map/ppermute | solution.py:426
  32.5 6.1 %collective-permute-start.6 = (f32[128,384]{1,0:T(8,128)S(1)}, f32[128,384]{1,0:T(8,128)S(1)}, u32[]{:S(2)}, u32[]{:S(2)}) collective-permute-start(f32[128,384]{1,0:T(8,128)S(1)} %bitcast_add_fusion.7), channel_id=1, source_target_pairs={{8,12},{9,13},{10,14},{11,15},{24,28},{25,29},{26,30},{27,31}} | collective-permute-start | bytes 589832 | tf_op jit(solution)/shard_map/ppermute | solution.py:426
  33.3 5.4 %collective-permute-start.7 = (f32[128,384]{1,0:T(8,128)S(1)}, f32[128,384]{1,0:T(8,128)S(1)}, u32[]{:S(2)}, u32[]{:S(2)}) collective-permute-start(f32[128,384]{1,0:T(8,128)S(1)} %bitcast_add_fusion.6), channel_id=1, source_target_pairs={{8,12},{9,13},{10,14},{11,15},{24,28},{25,29},{26,30},{27,31}} | collective-permute-start | bytes 589832 | tf_op jit(solution)/shard_map/ppermute | solution.py:426
  43.3 1.6 %collective-permute-start.8 = (f32[512,128]{1,0:T(8,128)S(1)}, f32[512,128]{1,0:T(8,128)S(1)}, u32[]{:S(2)}, u32[]{:S(2)}) collective-permute-start(f32[512,128]{1,0:T(8,128)S(1)} %get-tuple-element.189.refs_2_.mine), channel_id=1, source_target_pairs={{0,1},{1,0},{2,3},{3,2},{4,5},{5,4},{6,7},{7,6},{8,9},{9,8},{10,11... | collective-permute-start | bytes 786440 | tf_op jit(solution)/shard_map/ppermute | solution.py:564
  51.2 13.4 %collective-permute-start.9 = (f32[128,384]{1,0:T(8,128)S(1)}, f32[128,384]{1,0:T(8,128)S(1)}, u32[]{:S(2)}, u32[]{:S(2)}) collective-permute-start(f32[128,384]{1,0:T(8,128)S(1)} %get-tuple-element.296), channel_id=1, source_target_pairs={{12,8},{13,9},{14,10},{15,11},{28,24},{29,25},{30,26},{31,27}} | collective-permute-start | bytes 589832 | tf_op jit(solution)/shard_map/ppermute | solution.py:426
  51.9 13.3 %collective-permute-start.10 = (f32[128,384]{1,0:T(8,128)S(1)}, f32[128,384]{1,0:T(8,128)S(1)}, u32[]{:S(2)}, u32[]{:S(2)}) collective-permute-start(f32[128,384]{1,0:T(8,128)S(1)} %get-tuple-element.193), channel_id=1, source_target_pairs={{12,8},{13,9},{14,10},{15,11},{28,24},{29,25},{30,26},{31,27}} | collective-permute-start | bytes 589832 | tf_op jit(solution)/shard_map/ppermute | solution.py:426
  64.6 7.2 %collective-permute-start.11 = (f32[128,384]{1,0:T(8,128)S(1)}, f32[128,384]{1,0:T(8,128)S(1)}, u32[]{:S(2)}, u32[]{:S(2)}) collective-permute-start(f32[128,384]{1,0:T(8,128)S(1)} %bitcast_add_fusion.5), channel_id=1, source_target_pairs={{12,8},{8,4},{13,9},{9,5},{14,10},{10,6},{15,11},{11,7},{28,24},{2... | collective-permute-start | bytes 589832 | tf_op jit(solution)/shard_map/ppermute | solution.py:426
  65.3 7.8 %collective-permute-start.12 = (f32[128,384]{1,0:T(8,128)S(1)}, f32[128,384]{1,0:T(8,128)S(1)}, u32[]{:S(2)}, u32[]{:S(2)}) collective-permute-start(f32[128,384]{1,0:T(8,128)S(1)} %bitcast_add_fusion.4), channel_id=1, source_target_pairs={{12,8},{8,4},{13,9},{9,5},{14,10},{10,6},{15,11},{11,7},{28,24},{2... | collective-permute-start | bytes 589832 | tf_op jit(solution)/shard_map/ppermute | solution.py:426
  71.8 20.7 %collective-permute-start.13 = (f32[128,384]{1,0:T(8,128)S(1)}, f32[128,384]{1,0:T(8,128)S(1)}, u32[]{:S(2)}, u32[]{:S(2)}) collective-permute-start(f32[128,384]{1,0:T(8,128)S(1)} %bitcast_add_fusion.3), channel_id=1, source_target_pairs={{8,4},{4,0},{9,5},{5,1},{10,6},{6,2},{11,7},{7,3},{24,20},{20,16},... | collective-permute-start | bytes 589832 | tf_op jit(solution)/shard_map/ppermute | solution.py:426
  73.2 23.6 %collective-permute-start.14 = (f32[128,384]{1,0:T(8,128)S(1)}, f32[128,384]{1,0:T(8,128)S(1)}, u32[]{:S(2)}, u32[]{:S(2)}) collective-permute-start(f32[128,384]{1,0:T(8,128)S(1)} %bitcast_add_fusion.2), channel_id=1, source_target_pairs={{8,4},{4,0},{9,5},{5,1},{10,6},{6,2},{11,7},{7,3},{24,20},{20,16},... | collective-permute-start | bytes 589832 | tf_op jit(solution)/shard_map/ppermute | solution.py:426
  92.5 17.7 %collective-permute-start.15 = (f32[128,384]{1,0:T(8,128)S(1)}, f32[128,384]{1,0:T(8,128)S(1)}, u32[]{:S(2)}, u32[]{:S(2)}) collective-permute-start(f32[128,384]{1,0:T(8,128)S(1)} %bitcast_add_fusion.1), channel_id=1, source_target_pairs={{4,0},{5,1},{6,2},{7,3},{20,16},{21,17},{22,18},{23,19}} | collective-permute-start | bytes 589832 | tf_op jit(solution)/shard_map/ppermute | solution.py:426
  96.8 13.5 %collective-permute-start.16 = (f32[128,384]{1,0:T(8,128)S(1)}, f32[128,384]{1,0:T(8,128)S(1)}, u32[]{:S(2)}, u32[]{:S(2)}) collective-permute-start(f32[128,384]{1,0:T(8,128)S(1)} %bitcast_add_fusion), channel_id=1, source_target_pairs={{4,0},{5,1},{6,2},{7,3},{20,16},{21,17},{22,18},{23,19}} | collective-permute-start | bytes 589832 | tf_op jit(solution)/shard_map/ppermute | solution.py:426
  104.1 6.3 %collective-permute-start.17 = (f32[512,128]{1,0:T(8,128)S(1)}, f32[512,128]{1,0:T(8,128)S(1)}, u32[]{:S(2)}, u32[]{:S(2)}) collective-permute-start(f32[512,128]{1,0:T(8,128)S(1)} %get-tuple-element.267.rest_11_), channel_id=1, source_target_pairs={{0,1},{1,0},{2,3},{3,2},{4,5},{5,4},{6,7},{7,6},{8,9},{9,8},{10,11... | collective-permute-start | bytes 786440 | tf_op jit(solution)/shard_map/ppermute | solution.py:629
  117.6 12.0 %all-to-all-start = ((f32[8,20,128]{2,1,0:T(8,128)}), f32[8,20,128]{2,1,0:T(8,128)S(1)}, u32[]{:S(2)}, u32[]{:S(2)}) async-start(f32[8,20,128]{2,1,0:T(8,128)} %get-tuple-element.275), calls=%async_computation | async-start | bytes 196608 | tf_op jit(solution)/shard_map/all_to_all | solution.py:642
  122.5 8.3 %collective-permute-start.18 = (f32[512,128]{1,0:T(8,128)S(1)}, f32[512,128]{1,0:T(8,128)S(1)}, u32[]{:S(2)}, u32[]{:S(2)}) collective-permute-start(f32[512,128]{1,0:T(8,128)S(1)} %get-tuple-element.272), channel_id=1, source_target_pairs={{0,1},{1,0},{2,3},{3,2},{4,5},{5,4},{6,7},{7,6},{8,9},{9,8},{10,11... | collective-permute-start | bytes 786440 | tf_op jit(solution)/shard_map/ppermute | solution.py:641
